TPU v7x, 32 devices: a whole 2x2x4 slice. The times are simulated.
32 devices in a mesh: clip: 2 (over y), frame: 4 (over x, core), tensor: 4 (over z).
Axes of the slice: x: 2, y: 2, z: 4, core: 2. Of those that a mesh axis runs over, the one named last changes fastest.
Arguments:
- x_in: bfloat16 [2, 16, 256, 1152], P('clip', 'frame', 'tensor'), may hold values from -6 to 6
- cond: bfloat16 [2, 1152], P('clip'), may hold values from -6 to 6
- mod_weight_one: float32 [1152, 6, 1152], P(('clip', 'frame'), None, 'tensor'), may hold values from -0.1875 to 0.1875
- qkv_weight_one: float32 [1152, 3, 1152], P(('clip', 'frame'), None, 'tensor'), may hold values from -0.1875 to 0.1875
- attn_out_one: float32 [1152, 1152], P('tensor', ('clip', 'frame')), may hold values from -0.75 to 0.75
- mlp_up_one: float32 [1152, 4608], P(('clip', 'frame'), 'tensor'), may hold values from -0.1875 to 0.1875
- mlp_down_one: float32 [4608, 1152], P('tensor', ('clip', 'frame')), may hold values from -0.09375 to 0.09375
- mod_weight_two: float32 [1152, 6, 1152], P(('clip', 'frame'), None, 'tensor'), may hold values from -0.1875 to 0.1875
- qkv_weight_two: float32 [1152, 3, 1152], P(('clip', 'frame'), None, 'tensor'), may hold values from -0.1875 to 0.1875
- attn_out_two: float32 [1152, 1152], P('tensor', ('clip', 'frame')), may hold values from -0.375 to 0.375
- mlp_up_two: float32 [1152, 4608], P(('clip', 'frame'), 'tensor'), may hold values from -0.1875 to 0.1875
- mlp_down_two: float32 [4608, 1152], P('tensor', ('clip', 'frame')), may hold values from -0.09375 to 0.09375
- out_cotangent: bfloat16 [2, 16, 256, 1152], P('clip', 'frame', 'tensor'), may hold values from -6 to 6
Outputs:
- layer_out: bfloat16 [2, 16, 256, 1152], P('clip', 'frame', 'tensor')
- input_grad: float32 [2, 16, 256, 1152], P('clip', 'frame', 'tensor')
- cond_grad: float32 [2, 1152], P('clip')
- grad_mod_one: float32 [1152, 6, 1152], P(('clip', 'frame'), None, 'tensor')
- grad_qkv_one: float32 [1152, 3, 1152], P(('clip', 'frame'), None, 'tensor')
- grad_attn_one: float32 [1152, 1152], P('tensor', ('clip', 'frame'))
- grad_up_one: float32 [1152, 4608], P(('clip', 'frame'), 'tensor')
- grad_down_one: float32 [4608, 1152], P('tensor', ('clip', 'frame'))
- grad_mod_two: float32 [1152, 6, 1152], P(('clip', 'frame'), None, 'tensor')
- grad_qkv_two: float32 [1152, 3, 1152], P(('clip', 'frame'), None, 'tensor')
- grad_attn_two: float32 [1152, 1152], P('tensor', ('clip', 'frame'))
- grad_up_two: float32 [1152, 4608], P(('clip', 'frame'), 'tensor')
- grad_down_two: float32 [4608, 1152], P('tensor', ('clip', 'frame'))
All inputs are finite; a program needn't handle non-finite values.
Results may differ from a plain program's by a relative error of at most 0.02.
Values may be sent and summed in bfloat16 or wider, within the bound.
No kernel may reach another device: no remote copies, remote signals or barrier semaphores. Data moves between devices by JAX's collectives and lax.ppermute only.
A program may use at most 192 MiB of HBM per device.

v0:
```python
import jax
import jax.numpy as jnp
from jax import lax
from jax.sharding import PartitionSpec as P

HD = 72


HIGHEST_PRECISION = lax.Precision.HIGHEST
SCORE_FORMS = {True: "cfphe,cfqhe->cfhpq", False: "cfphe,cgphe->cphfg"}
APPLY_FORMS = {True: "cfhpq,cfqhe->cfphe", False: "cphfg,cgphe->cfphe"}
BACK_FORMS = {True: "cfhpq,cfphe->cfqhe", False: "cphfg,cfphe->cgphe"}
GELU_COEFF = 0.7978845608028654
CUBIC_COEFF = 0.044715


def layer_norm(stream):
    centre = stream - jnp.mean(stream, axis=-1, keepdims=True)
    inv_scale = lax.rsqrt(jnp.mean(centre * centre, axis=-1, keepdims=True) + 1e-06)
    return (centre * inv_scale, inv_scale)


def norm_back(normed, inv_scale, upstream):
    return inv_scale * (
        upstream
        - jnp.mean(upstream, axis=-1, keepdims=True)
        - normed * jnp.mean(upstream * normed, axis=-1, keepdims=True)
    )


def gelu_tanh(inputs):
    return (
        0.5
        * inputs
        * (1.0 + jnp.tanh(GELU_COEFF * (inputs + CUBIC_COEFF * inputs * inputs * inputs)))
    )


def gelu_slope(inputs):
    tangent = jnp.tanh(GELU_COEFF * (inputs + CUBIC_COEFF * inputs * inputs * inputs))
    return 0.5 * (1.0 + tangent) + 0.5 * inputs * (1.0 - tangent * tangent) * GELU_COEFF * (
        1.0 + 3.0 * CUBIC_COEFF * inputs * inputs
    )


def choose(modulation, column):
    return modulation[:, column][:, None, None, :]


def split_heads(projected):
    leading = projected.shape[:3]
    row_width = projected.shape[-1]
    head_count = row_width // HD
    queries = projected[:, :, :, 0].reshape(leading + (head_count, HD))
    key_rows = projected[:, :, :, 1].reshape(leading + (head_count, HD))
    values = projected[:, :, :, 2].reshape(leading + (head_count, HD))
    return (queries, key_rows, values, leading, row_width)


def attend(projected, spatial):
    queries, key_rows, values, leading, row_width = split_heads(projected)
    scores = jnp.einsum(
        SCORE_FORMS[spatial], queries, key_rows, preferred_element_type=jnp.float32
    ) * HD ** (-0.5)
    highest = jnp.max(scores, axis=-1, keepdims=True)
    expo = jnp.exp(scores - highest)
    denominator = jnp.sum(expo, axis=-1, keepdims=True)
    probs = (expo / denominator).astype(jnp.bfloat16)
    log_total = highest + jnp.log(denominator)
    attended = jnp.einsum(APPLY_FORMS[spatial], probs, values, preferred_element_type=jnp.float32)
    return (attended.reshape(leading + (row_width,)).astype(jnp.bfloat16), log_total)


def attend_back(projected, log_total, d_attended, spatial):
    queries, key_rows, values, leading, row_width = split_heads(projected)
    scale_factor = HD ** (-0.5)
    scores = (
        jnp.einsum(SCORE_FORMS[spatial], queries, key_rows, preferred_element_type=jnp.float32)
        * scale_factor
    )
    probs = jnp.exp(scores - log_total)
    upstream = d_attended.reshape(leading + (row_width // HD, HD))
    d_probs = jnp.einsum(SCORE_FORMS[spatial], upstream, values, preferred_element_type=jnp.float32)
    d_values = jnp.einsum(
        BACK_FORMS[spatial],
        probs.astype(jnp.bfloat16),
        upstream,
        preferred_element_type=jnp.float32,
    )
    row_inner = jnp.sum(probs * d_probs, axis=-1, keepdims=True)
    d_scores = (probs * (d_probs - row_inner)).astype(jnp.bfloat16)
    d_queries = (
        jnp.einsum(APPLY_FORMS[spatial], d_scores, key_rows, preferred_element_type=jnp.float32)
        * scale_factor
    )
    d_keys = (
        jnp.einsum(BACK_FORMS[spatial], d_scores, queries, preferred_element_type=jnp.float32)
        * scale_factor
    )
    stacked = jnp.stack([d_queries, d_keys, d_values], axis=3)
    return stacked.reshape(leading + (3, row_width)).astype(jnp.bfloat16)


def fetch_weights(weights):
    cast = tuple((weight.astype(jnp.bfloat16) for weight in weights))
    return (
        lax.all_gather(cast[0], ("clip", "frame"), axis=0, tiled=True),
        lax.all_gather(cast[1], ("clip", "frame"), axis=0, tiled=True),
        lax.all_gather(cast[2], ("clip", "frame"), axis=1, tiled=True),
        lax.all_gather(cast[3], ("clip", "frame"), axis=0, tiled=True),
        lax.all_gather(cast[4], ("clip", "frame"), axis=1, tiled=True),
    )


def backward_weights(weights):
    cast = tuple((weight.astype(jnp.bfloat16) for weight in weights))
    return (
        lax.all_gather(cast[0], ("clip", "frame"), axis=0, tiled=True),
        lax.all_gather(cast[1], ("clip", "frame"), axis=0, tiled=True),
        lax.all_gather(cast[2], ("clip", "frame"), axis=1, tiled=True),
        lax.all_gather(cast[3], ("clip", "frame"), axis=0, tiled=True),
        lax.all_gather(cast[4], ("clip", "frame"), axis=1, tiled=True),
    )


def spread_rows(rows):
    return lax.all_gather(rows, "tensor", axis=2, tiled=True)


def collect_rows(term):
    return lax.psum_scatter(term, "tensor", scatter_dimension=2, tiled=True)


def attention_output(attended, attn_weight):
    return collect_rows(
        jnp.einsum("cfpz,zd->cfpd", attended, attn_weight, preferred_element_type=jnp.float32)
    )


def layer_forward(stream, silu_cond, gathered, spatial):
    mod_weight, qkv_weight, attn_weight, up_weight, down_weight = gathered
    partial_value = jnp.einsum(
        "cd,dkz->ckz", silu_cond, mod_weight, preferred_element_type=jnp.float32
    )
    modulation = lax.all_gather(partial_value, "tensor", axis=2, tiled=True)
    normed, inv_scale = layer_norm(stream)
    modulated = (normed * (1.0 + choose(modulation, 1)) + choose(modulation, 0)).astype(
        jnp.bfloat16
    )
    gathered_rows = spread_rows(modulated)
    projected = jnp.einsum(
        "cfpd,dkz->cfpkz", gathered_rows, qkv_weight, preferred_element_type=jnp.float32
    ).astype(jnp.bfloat16)
    if spatial:
        project_held = projected
        attended, log_total = attend(project_held, True)
    else:
        project_held = lax.all_to_all(projected, "frame", split_axis=2, concat_axis=1, tiled=True)
        placed, log_total = attend(project_held, False)
        attended = lax.all_to_all(placed, "frame", split_axis=1, concat_axis=2, tiled=True)
    branch_attn = attention_output(attended, attn_weight)
    middle = stream + choose(modulation, 2) * branch_attn
    normed_mlp, inv_mlp = layer_norm(middle)
    modulated_mlp = (normed_mlp * (1.0 + choose(modulation, 4)) + choose(modulation, 3)).astype(
        jnp.bfloat16
    )
    gathered_mlp = spread_rows(modulated_mlp)
    hidden_pre = jnp.einsum(
        "cfpd,dz->cfpz", gathered_mlp, up_weight, preferred_element_type=jnp.float32
    )
    hidden_act = gelu_tanh(hidden_pre).astype(jnp.bfloat16)
    branch_mlp = collect_rows(
        jnp.einsum("cfpz,zd->cfpd", hidden_act, down_weight, preferred_element_type=jnp.float32)
    )
    result = middle + choose(modulation, 5) * branch_mlp
    stored = (
        modulation,
        normed,
        inv_scale,
        gathered_rows,
        project_held,
        log_total,
        attended,
        branch_attn,
        normed_mlp,
        inv_mlp,
        gathered_mlp,
        hidden_pre,
        hidden_act,
        branch_mlp,
    )
    return (result, stored)


def layer_backward(upstream, silu_cond, gathered, stored, spatial):
    mod_weight, qkv_weight, attn_weight, up_weight, down_weight = gathered
    (
        modulation,
        normed,
        inv_scale,
        gathered_rows,
        project_held,
        log_total,
        attended,
        branch_attn,
        normed_mlp,
        inv_mlp,
        gathered_mlp,
        hidden_pre,
        hidden_act,
        branch_mlp,
    ) = stored
    d_branch_mlp = (upstream * choose(modulation, 5)).astype(jnp.bfloat16)
    d_gate_mlp = jnp.sum(upstream * branch_mlp, axis=(1, 2))
    d_branch_all = spread_rows(d_branch_mlp)
    grad_down = jnp.einsum(
        "cfpz,cfpd->zd", hidden_act, d_branch_all, preferred_element_type=jnp.float32
    )
    d_act = jnp.einsum(
        "cfpd,zd->cfpz", d_branch_all, down_weight, preferred_element_type=jnp.float32
    )
    d_pre = (d_act * gelu_slope(hidden_pre)).astype(jnp.bfloat16)
    grad_up = jnp.einsum("cfpd,cfpz->dz", gathered_mlp, d_pre, preferred_element_type=jnp.float32)
    d_mod_mlp = collect_rows(
        jnp.einsum("cfpz,dz->cfpd", d_pre, up_weight, preferred_element_type=jnp.float32)
    )
    d_shift_mlp = jnp.sum(d_mod_mlp, axis=(1, 2))
    d_scale_mlp = jnp.sum(d_mod_mlp * normed_mlp, axis=(1, 2))
    d_middle = upstream + norm_back(normed_mlp, inv_mlp, d_mod_mlp * (1.0 + choose(modulation, 4)))
    d_branch_attn = (d_middle * choose(modulation, 2)).astype(jnp.bfloat16)
    d_gate_attn = jnp.sum(d_middle * branch_attn, axis=(1, 2))
    d_attn_all = spread_rows(d_branch_attn)
    grad_attn = jnp.einsum(
        "cfpz,cfpd->zd", attended, d_attn_all, preferred_element_type=jnp.float32
    )
    d_attended = jnp.einsum(
        "cfpd,zd->cfpz", d_attn_all, attn_weight, preferred_element_type=jnp.float32
    ).astype(jnp.bfloat16)
    if spatial:
        d_projected = attend_back(project_held, log_total, d_attended, True)
    else:
        d_placed = lax.all_to_all(d_attended, "frame", split_axis=2, concat_axis=1, tiled=True)
        d_projected = lax.all_to_all(
            attend_back(project_held, log_total, d_placed, False),
            "frame",
            split_axis=1,
            concat_axis=2,
            tiled=True,
        )
    grad_qkv = jnp.einsum(
        "cfpd,cfpkz->dkz", gathered_rows, d_projected, preferred_element_type=jnp.float32
    )
    d_modulated = collect_rows(
        jnp.einsum("cfpkz,dkz->cfpd", d_projected, qkv_weight, preferred_element_type=jnp.float32)
    )
    d_shift_attn = jnp.sum(d_modulated, axis=(1, 2))
    d_scale_attn = jnp.sum(d_modulated * normed, axis=(1, 2))
    d_stream = d_middle + norm_back(normed, inv_scale, d_modulated * (1.0 + choose(modulation, 1)))
    d_modulation = jnp.stack(
        [d_shift_attn, d_scale_attn, d_gate_attn, d_shift_mlp, d_scale_mlp, d_gate_mlp], axis=1
    )
    d_mod_own = lax.psum_scatter(d_modulation, "tensor", scatter_dimension=2, tiled=True)
    grad_mod = jnp.einsum(
        "cd,ckz->dkz", silu_cond.astype(jnp.float32), d_mod_own, precision=HIGHEST_PRECISION
    )
    d_silu = jnp.einsum(
        "ckz,dkz->cd", d_mod_own, mod_weight.astype(jnp.float32), precision=HIGHEST_PRECISION
    )
    grads = (
        lax.psum_scatter(
            grad_mod.astype(jnp.bfloat16), ("clip", "frame"), scatter_dimension=0, tiled=True
        ).astype(jnp.float32),
        lax.psum_scatter(
            grad_qkv.astype(jnp.bfloat16), ("clip", "frame"), scatter_dimension=0, tiled=True
        ).astype(jnp.float32),
        lax.psum_scatter(
            grad_attn.astype(jnp.bfloat16), ("clip", "frame"), scatter_dimension=1, tiled=True
        ).astype(jnp.float32),
        lax.psum_scatter(
            grad_up.astype(jnp.bfloat16), ("clip", "frame"), scatter_dimension=0, tiled=True
        ).astype(jnp.float32),
        lax.psum_scatter(
            grad_down.astype(jnp.bfloat16), ("clip", "frame"), scatter_dimension=1, tiled=True
        ).astype(jnp.float32),
    )
    return (d_stream, d_silu, grads)


def local(
    x_in,
    cond,
    mod_weight_one,
    qkv_weight_one,
    attn_out_one,
    mlp_up_one,
    mlp_down_one,
    mod_weight_two,
    qkv_weight_two,
    attn_out_two,
    mlp_up_two,
    mlp_down_two,
    out_cotangent,
):
    weights_first = (mod_weight_one, qkv_weight_one, attn_out_one, mlp_up_one, mlp_down_one)
    weights_second = (mod_weight_two, qkv_weight_two, attn_out_two, mlp_up_two, mlp_down_two)
    cond_float = cond.astype(jnp.float32)
    silu_cond = jax.nn.silu(cond_float).astype(jnp.bfloat16)
    gathered_first = fetch_weights(weights_first)
    middle_stream, stored_first = layer_forward(
        x_in.astype(jnp.float32), silu_cond, gathered_first, True
    )
    gathered_second = fetch_weights(weights_second)
    result, stored_second = layer_forward(middle_stream, silu_cond, gathered_second, False)
    back_second = backward_weights(weights_second)
    d_middle_stream, d_silu_second, grads_second = layer_backward(
        out_cotangent.astype(jnp.float32), silu_cond, back_second, stored_second, False
    )
    back_first = backward_weights(weights_first)
    input_grad, d_silu_first, grads_first = layer_backward(
        d_middle_stream, silu_cond, back_first, stored_first, True
    )
    d_silu_total = lax.psum(d_silu_first + d_silu_second, ("frame", "tensor"))
    sigmoid_cond = jax.nn.sigmoid(cond_float)
    cond_grad = d_silu_total * (sigmoid_cond * (1.0 + cond_float * (1.0 - sigmoid_cond)))
    return (
        result.astype(jnp.bfloat16),
        input_grad,
        cond_grad,
        grads_first[0],
        grads_first[1],
        grads_first[2],
        grads_first[3],
        grads_first[4],
        grads_second[0],
        grads_second[1],
        grads_second[2],
        grads_second[3],
        grads_second[4],
    )


def solution(mesh):
    return jax.shard_map(
        local,
        mesh=mesh,
        in_specs=(
            P("clip", "frame", "tensor", None),
            P("clip", None),
            P(("clip", "frame"), None, "tensor"),
            P(("clip", "frame"), None, "tensor"),
            P("tensor", ("clip", "frame")),
            P(("clip", "frame"), "tensor"),
            P("tensor", ("clip", "frame")),
            P(("clip", "frame"), None, "tensor"),
            P(("clip", "frame"), None, "tensor"),
            P("tensor", ("clip", "frame")),
            P(("clip", "frame"), "tensor"),
            P("tensor", ("clip", "frame")),
            P("clip", "frame", "tensor", None),
        ),
        out_specs=(
            P("clip", "frame", "tensor", None),
            P("clip", "frame", "tensor", None),
            P("clip", None),
            P(("clip", "frame"), None, "tensor"),
            P(("clip", "frame"), None, "tensor"),
            P("tensor", ("clip", "frame")),
            P(("clip", "frame"), "tensor"),
            P("tensor", ("clip", "frame")),
            P(("clip", "frame"), None, "tensor"),
            P(("clip", "frame"), None, "tensor"),
            P("tensor", ("clip", "frame")),
            P(("clip", "frame"), "tensor"),
            P("tensor", ("clip", "frame")),
        ),
        check_vma=False,
    )
```

profile of v0, /device:TPU:0, one launch (start us, length us, event | category | flops | bytes accessed | tf_op | source)
XLA Modules:
  0.0 2178.8 jit_solution(7276182978386951180)
XLA Ops:
  11.7 43.0 %all-gather.21.cloned.1.call-done = bf16[1152,6,288]{2,0,1:T(8,128)(2,1)} async-done(((bf16[144,6,288]{2,0,1:T(8,128)(2,1)}), bf16[1152,6,288]{2,0,1:T(8,128)(2,1)}) %all-gather.21.cloned.1.call-update) | async-done | bytes 3981328 | tf_op jit(solution)/shard_map/all_gather | solution.py:107
  89.8 52.6 %all-gather.23.cloned.1.call-done = bf16[1,4,256,1152]{3,2,1,0:T(8,128)(2,1)} async-done(((bf16[1,4,64,1152]{3,2,1,0:T(8,128)(2,1)}), bf16[1,4,256,1152]{3,2,1,0:T(8,128)(2,1)}) %all-gather.23.cloned.1.call-update) | async-done | bytes 2359312 | tf_op jit(solution)/shard_map/all_gather | solution.py:127
  156.9 82.4 %reduce-scatter.25.cloned.1.call-done = f32[1,4,64,1152]{3,2,1,0:T(8,128)} async-done(((f32[1,4,256,1152]{3,2,1,0:T(8,128)}), f32[1,4,64,1152]{3,2,1,0:T(8,128)}) %reduce-scatter.25.cloned.1.call-update) | async-done | bytes 1179664 | tf_op jit(solution)/shard_map/reduce_scatter | solution.py:131
  272.4 52.5 %all-gather.27.cloned.1.call-done = bf16[1,4,256,1152]{3,2,1,0:T(8,128)(2,1)} async-done(((bf16[1,4,64,1152]{3,2,1,0:T(8,128)(2,1)}), bf16[1,4,256,1152]{3,2,1,0:T(8,128)(2,1)}) %all-gather.27.cloned.1.call-update) | async-done | bytes 2359312 | tf_op jit(solution)/shard_map/all_gather | solution.py:127
  418.2 70.3 %reduce-scatter.27.cloned.1.call-done = f32[1,4,64,1152]{3,2,1,0:T(8,128)} async-done(((f32[1,4,256,1152]{3,2,1,0:T(8,128)}), f32[1,4,64,1152]{3,2,1,0:T(8,128)}) %reduce-scatter.27.cloned.1.call-update) | async-done | bytes 1179664 | tf_op jit(solution)/shard_map/reduce_scatter | solution.py:131
  521.4 52.6 %all-gather.35.cloned.1.call-done = bf16[1,4,256,1152]{3,2,1,0:T(8,128)(2,1)} async-done(((bf16[1,4,64,1152]{3,2,1,0:T(8,128)(2,1)}), bf16[1,4,256,1152]{3,2,1,0:T(8,128)(2,1)}) %all-gather.35.cloned.1.call-update) | async-done | bytes 2359312 | tf_op jit(solution)/shard_map/all_gather | solution.py:127
  662.4 81.6 %reduce-scatter.29.cloned.1.call-done = f32[1,4,64,1152]{3,2,1,0:T(8,128)} async-done(((f32[1,4,256,1152]{3,2,1,0:T(8,128)}), f32[1,4,64,1152]{3,2,1,0:T(8,128)}) %reduce-scatter.29.cloned.1.call-update) | async-done | bytes 1179664 | tf_op jit(solution)/shard_map/reduce_scatter | solution.py:131
  776.6 52.5 %all-gather.39.cloned.1.call-done = bf16[1,4,256,1152]{3,2,1,0:T(8,128)(2,1)} async-done(((bf16[1,4,64,1152]{3,2,1,0:T(8,128)(2,1)}), bf16[1,4,256,1152]{3,2,1,0:T(8,128)(2,1)}) %all-gather.39.cloned.1.call-update) | async-done | bytes 2359312 | tf_op jit(solution)/shard_map/all_gather | solution.py:127
  860.5 52.5 %all-gather.45.cloned.1.call-done = bf16[1,4,256,1152]{3,2,1,0:T(8,128)(2,1)} async-done(((bf16[1,4,64,1152]{3,2,1,0:T(8,128)(2,1)}), bf16[1,4,256,1152]{3,2,1,0:T(8,128)(2,1)}) %all-gather.45.cloned.1.call-update) | async-done | bytes 2359312 | tf_op jit(solution)/shard_map/all_gather | solution.py:127
  936.9 74.7 %reduce-scatter.33.cloned.1.call-done = f32[1,4,64,1152]{3,2,1,0:T(8,128)} async-done(((f32[1,4,256,1152]{3,2,1,0:T(8,128)}), f32[1,4,64,1152]{3,2,1,0:T(8,128)}) %reduce-scatter.33.cloned.1.call-update) | async-done | bytes 1179664 | tf_op jit(solution)/shard_map/reduce_scatter | solution.py:131
  1014.3 85.2 %reduce-scatter.31.cloned.1.call-done = f32[1,4,64,1152]{3,2,1,0:T(8,128)} async-done(((f32[1,4,256,1152]{3,2,1,0:T(8,128)}), f32[1,4,64,1152]{3,2,1,0:T(8,128)}) %reduce-scatter.31.cloned.1.call-update) | async-done | bytes 1179664 | tf_op jit(solution)/shard_map/reduce_scatter | solution.py:131
  1106.1 51.1 %all-gather.47.cloned.1.call-done = bf16[1,4,256,1152]{3,2,1,0:T(8,128)(2,1)} async-done(((bf16[1,4,64,1152]{3,2,1,0:T(8,128)(2,1)}), bf16[1,4,256,1152]{3,2,1,0:T(8,128)(2,1)}) %all-gather.47.cloned.1.call-update) | async-done | bytes 2359312 | tf_op jit(solution)/shard_map/all_gather | solution.py:127
  1243.9 83.3 %reduce-scatter.35.cloned.1.call-done = f32[1,4,64,1152]{3,2,1,0:T(8,128)} async-done(((f32[1,4,256,1152]{3,2,1,0:T(8,128)}), f32[1,4,64,1152]{3,2,1,0:T(8,128)}) %reduce-scatter.35.cloned.1.call-update) | async-done | bytes 1179664 | tf_op jit(solution)/shard_map/reduce_scatter | solution.py:131
  1333.1 51.1 %all-gather.49.cloned.1.call-done = bf16[1,4,256,1152]{3,2,1,0:T(8,128)(2,1)} async-done(((bf16[1,4,64,1152]{3,2,1,0:T(8,128)(2,1)}), bf16[1,4,256,1152]{3,2,1,0:T(8,128)(2,1)}) %all-gather.49.cloned.1.call-update) | async-done | bytes 2359312 | tf_op jit(solution)/shard_map/all_gather | solution.py:127
  1398.5 84.2 %reduce-scatter.37.cloned.1.call-done = f32[1,4,64,1152]{3,2,1,0:T(8,128)} async-done(((f32[1,4,256,1152]{3,2,1,0:T(8,128)}), f32[1,4,64,1152]{3,2,1,0:T(8,128)}) %reduce-scatter.37.cloned.1.call-update) | async-done | bytes 1179664 | tf_op jit(solution)/shard_map/reduce_scatter | solution.py:131
  1489.0 50.6 %all-gather.51.cloned.1.call-done = bf16[1,4,256,1152]{3,2,1,0:T(8,128)(2,1)} async-done(((bf16[1,4,64,1152]{3,2,1,0:T(8,128)(2,1)}), bf16[1,4,256,1152]{3,2,1,0:T(8,128)(2,1)}) %all-gather.51.cloned.1.call-update) | async-done | bytes 2359312 | tf_op jit(solution)/shard_map/all_gather | solution.py:127
  1556.4 82.2 %reduce-scatter.39.cloned.1.call-done = f32[1,4,64,1152]{3,2,1,0:T(8,128)} async-done(((f32[1,4,256,1152]{3,2,1,0:T(8,128)}), f32[1,4,64,1152]{3,2,1,0:T(8,128)}) %reduce-scatter.39.cloned.1.call-update) | async-done | bytes 1179664 | tf_op jit(solution)/shard_map/reduce_scatter | solution.py:131
  1734.4 45.8 %reduce-scatter.59.cloned.1.call-done = bf16[1152,144]{0,1:T(8,128)(2,1)} async-done(((bf16[1152,1152]{0,1:T(8,128)(2,1)}), bf16[1152,144]{0,1:T(8,128)(2,1)}) %reduce-scatter.59.cloned.1.call-update) | async-done | bytes 331792 | tf_op jit(solution)/shard_map/reduce_scatter | solution.py:282
  1782.1 37.1 %reduce-scatter.55.cloned.1.call-done = bf16[288,144]{0,1:T(8,128)(2,1)} async-done(((bf16[288,1152]{0,1:T(8,128)(2,1)}), bf16[288,144]{0,1:T(8,128)(2,1)}) %reduce-scatter.55.cloned.1.call-update) | async-done | bytes 82960 | tf_op jit(solution)/shard_map/reduce_scatter | solution.py:276
  1820.8 45.9 %reduce-scatter.53.cloned.1.call-done = bf16[144,3,288]{2,0,1:T(8,128)(2,1)} async-done(((bf16[1152,3,288]{2,0,1:T(8,128)(2,1)}), bf16[144,3,288]{2,0,1:T(8,128)(2,1)}) %reduce-scatter.53.cloned.1.call-update) | async-done | bytes 248848 | tf_op jit(solution)/shard_map/reduce_scatter | solution.py:273
  1875.4 38.6 %reduce-scatter.47.cloned.1.call-done = bf16[144,1152]{1,0:T(8,128)(2,1)} async-done(((bf16[1152,1152]{1,0:T(8,128)(2,1)}), bf16[144,1152]{1,0:T(8,128)(2,1)}) %reduce-scatter.47.cloned.1.call-update) | async-done | bytes 331792 | tf_op jit(solution)/shard_map/reduce_scatter | solution.py:279
  1915.9 45.8 %reduce-scatter.49.cloned.1.call-done = bf16[1152,144]{0,1:T(8,128)(2,1)} async-done(((bf16[1152,1152]{0,1:T(8,128)(2,1)}), bf16[1152,144]{0,1:T(8,128)(2,1)}) %reduce-scatter.49.cloned.1.call-update) | async-done | bytes 331792 | tf_op jit(solution)/shard_map/reduce_scatter | solution.py:282
  2002.0 46.1 %reduce-scatter.43.cloned.1.call-done = bf16[144,3,288]{2,0,1:T(8,128)(2,1)} async-done(((bf16[1152,3,288]{2,0,1:T(8,128)(2,1)}), bf16[144,3,288]{2,0,1:T(8,128)(2,1)}) %reduce-scatter.43.cloned.1.call-update) | async-done | bytes 248848 | tf_op jit(solution)/shard_map/reduce_scatter | solution.py:273
  2111.3 58.4 %reduce-scatter.51.cloned.1.call-done = bf16[144,6,288]{2,0,1:T(8,128)(2,1)} async-done(((bf16[1152,6,288]{2,0,1:T(8,128)(2,1)}), bf16[144,6,288]{2,0,1:T(8,128)(2,1)}) %reduce-scatter.51.cloned.1.call-update) | async-done | bytes 497680 | tf_op jit(solution)/shard_map/reduce_scatter | solution.py:270
  (432 shorter events, 742.9 us)
Async XLA Ops:
  73.1 166.2 %reduce-scatter.25.cloned.1.call-start = ((), (), s32[]{:S(2)}) async-start(), calls=%async_computation.27 | async-start | bytes 5898240 | tf_op jit(solution)/shard_map/reduce_scatter | solution.py:131
  156.9 168.0 %all-gather.27.cloned.1.call-start = ((), (), s32[]{:S(2)}) async-start(), calls=%async_computation.28 | async-start | bytes 2949120 | tf_op jit(solution)/shard_map/all_gather | solution.py:127
  243.2 157.2 %all-gather.33.cloned.1.call-start = ((), (), s32[]{:S(2)}) async-start(), calls=%async_computation.32 | async-start | bytes 5971968 | tf_op jit(solution)/shard_map/all_gather | solution.py:107
  245.5 243.0 %reduce-scatter.27.cloned.1.call-start = ((), (), s32[]{:S(2)}) async-start(), calls=%async_computation.31 | async-start | bytes 5898240 | tf_op jit(solution)/shard_map/reduce_scatter | solution.py:131
  366.0 155.5 %all-gather.37.cloned.1.call-start = ((), (), s32[]{:S(2)}) async-start(), calls=%async_computation.34 | async-start | bytes 2985984 | tf_op jit(solution)/shard_map/all_gather | solution.py:108
  367.9 206.2 %all-gather.35.cloned.1.call-start = ((), (), s32[]{:S(2)}) async-start(), calls=%async_computation.33 | async-start | bytes 2949120 | tf_op jit(solution)/shard_map/all_gather | solution.py:127
  662.3 166.8 %all-gather.39.cloned.1.call-start = ((), (), s32[]{:S(2)}) async-start(), calls=%async_computation.36 | async-start | bytes 2949120 | tf_op jit(solution)/shard_map/all_gather | solution.py:127
  749.5 163.5 %all-gather.45.cloned.1.call-start = ((), (), s32[]{:S(2)}) async-start(), calls=%async_computation.40 | async-start | bytes 2949120 | tf_op jit(solution)/shard_map/all_gather | solution.py:127
  751.6 260.0 %reduce-scatter.33.cloned.1.call-start = ((), (), s32[]{:S(2)}) async-start(), calls=%async_computation.41 | async-start | bytes 5898240 | tf_op jit(solution)/shard_map/reduce_scatter | solution.py:131
  927.3 172.2 %reduce-scatter.31.cloned.1.call-start = ((), (), s32[]{:S(2)}) async-start(), calls=%async_computation.39 | async-start | bytes 5898240 | tf_op jit(solution)/shard_map/reduce_scatter | solution.py:131
  936.8 220.4 %all-gather.47.cloned.1.call-start = ((), (), s32[]{:S(2)}) async-start(), calls=%async_computation.42 | async-start | bytes 2949120 | tf_op jit(solution)/shard_map/all_gather | solution.py:127
  1167.3 160.0 %reduce-scatter.35.cloned.1.call-start = ((), (), s32[]{:S(2)}) async-start(), calls=%async_computation.43 | async-start | bytes 5898240 | tf_op jit(solution)/shard_map/reduce_scatter | solution.py:131
  1333.0 149.6 %reduce-scatter.37.cloned.1.call-start = ((), (), s32[]{:S(2)}) async-start(), calls=%async_computation.45 | async-start | bytes 5898240 | tf_op jit(solution)/shard_map/reduce_scatter | solution.py:131
  1488.5 150.2 %reduce-scatter.39.cloned.1.call-start = ((), (), s32[]{:S(2)}) async-start(), calls=%async_computation.47 | async-start | bytes 5898240 | tf_op jit(solution)/shard_map/reduce_scatter | solution.py:131
  1554.4 143.5 %reduce-scatter.63.cloned.1.call-start = ((), (), s32[]{:S(2)}) async-start(), calls=%async_computation.59 | async-start | bytes 737280
  1556.3 142.6 %reduce-scatter.61.cloned.1.call-start = ((), (), s32[]{:S(2)}) async-start(), calls=%async_computation.58 | async-start | bytes 737280
  1657.3 161.9 %reduce-scatter.55.cloned.1.call-start = ((), (), s32[]{:S(2)}) async-start(), calls=%async_computation.55 | async-start | bytes 995328 | tf_op jit(solution)/shard_map/reduce_scatter | solution.py:276
  1662.5 204.3 %reduce-scatter.53.cloned.1.call-start = ((), (), s32[]{:S(2)}) async-start(), calls=%async_computation.54 | async-start | bytes 2985984 | tf_op jit(solution)/shard_map/reduce_scatter | solution.py:273
  1669.7 244.3 %reduce-scatter.47.cloned.1.call-start = ((), (), s32[]{:S(2)}) async-start(), calls=%async_computation.51 | async-start | bytes 2985984 | tf_op jit(solution)/shard_map/reduce_scatter | solution.py:279
  1677.0 284.7 %reduce-scatter.49.cloned.1.call-start = ((), (), s32[]{:S(2)}) async-start(), calls=%async_computation.52 | async-start | bytes 2985984 | tf_op jit(solution)/shard_map/reduce_scatter | solution.py:282
  1685.3 315.2 %reduce-scatter.45.cloned.1.call-start = ((), (), s32[]{:S(2)}) async-start(), calls=%async_computation.50 | async-start | bytes 995328 | tf_op jit(solution)/shard_map/reduce_scatter | solution.py:276
  1690.4 357.8 %reduce-scatter.43.cloned.1.call-start = ((), (), s32[]{:S(2)}) async-start(), calls=%async_computation.49 | async-start | bytes 2985984 | tf_op jit(solution)/shard_map/reduce_scatter | solution.py:273
  1697.2 411.8 %reduce-scatter.41.cloned.1.call-start = ((), (), s32[]{:S(2)}) async-start(), calls=%async_computation.48 | async-start | bytes 5971968 | tf_op jit(solution)/shard_map/reduce_scatter | solution.py:270
  1706.7 463.0 %reduce-scatter.51.cloned.1.call-start = ((), (), s32[]{:S(2)}) async-start(), calls=%async_computation.53 | async-start | bytes 5971968 | tf_op jit(solution)/shard_map/reduce_scatter | solution.py:270
  (102 other events, 4732.4 us)
Sparse Core Ops, SparseCore 0:
  10.5 44.0 all-gather.20
  91.9 50.4 all-gather.22
  155.2 84.0 reduce-scatter.24
  274.4 50.4 all-gather.26
  402.7 85.7 reduce-scatter.26
  523.6 50.4 all-gather.34
  660.5 83.3 reduce-scatter.28
  778.6 50.4 all-gather.38
  862.5 50.4 all-gather.44
  927.4 84.1 reduce-scatter.32
  1013.7 85.7 reduce-scatter.30
  1106.3 50.9 all-gather.46
  1244.0 83.1 reduce-scatter.34
  1333.1 50.9 all-gather.48
  1398.5 84.0 reduce-scatter.36
  1488.6 50.9 all-gather.50
  1554.5 84.0 reduce-scatter.38
  1736.4 43.7 reduce-scatter.58
  1822.9 43.7 reduce-scatter.52
  1870.2 43.7 reduce-scatter.46
  1917.9 43.7 reduce-scatter.48
  2004.3 43.7 reduce-scatter.42
  2051.7 57.3 reduce-scatter.40
  2112.4 57.1 reduce-scatter.50
  (12 shorter events, 378.7 us)
where the time goes:
time: 2190 us; the launch traced here: 2180 us
  waiting for transfers between devices  1670 us (76%)
  matrix products  185 us (8%)
  blocking collectives  155 us (7%)
  other arithmetic  81.1 us (4%)
  local copies, waits for them, and re-layouts  56.7 us (3%)
    reduce_scatter x8, waiting for transfers between devices, collect_rows(): return lax.psum_scatter(term, 'tensor', scatter_dimension=2, tiled=True)  644 us
    all_gather x8, waiting for transfers between devices, spread_rows(): return lax.all_gather(rows, 'tensor', axis=2, tiled=True)  416 us
    reduce_scatter x2, waiting for transfers between devices, layer_backward(): lax.psum_scatter(grad_qkv.astype(jnp.bfloat16), ('clip', 'frame'), scatte...  92.1 us
    reduce_scatter x2, waiting for transfers between devices, layer_backward(): lax.psum_scatter(grad_down.astype(jnp.bfloat16), ('clip', 'frame'), scatt...  91.6 us
    all_gather x2, waiting for transfers between devices, fetch_weights(): lax.all_gather(cast[0], ('clip', 'frame'), axis=0, tiled=True)  75.4 us
    reduce_scatter x2, waiting for transfers between devices, layer_backward(): lax.psum_scatter(grad_mod.astype(jnp.bfloat16), ('clip', 'frame'), scatte...  74.1 us
    reduce_scatter x2, waiting for transfers between devices, layer_backward(): lax.psum_scatter(grad_attn.astype(jnp.bfloat16), ('clip', 'frame'), scatt...  74 us
    reduce_scatter x2, waiting for transfers between devices, layer_backward(): lax.psum_scatter(grad_up.astype(jnp.bfloat16), ('clip', 'frame'), scatter...  64 us
  transfers between devices with their start and end apart: 38, of which 35 were waited for; matrix products, arithmetic and copies ran while one was open for 8% of the time, Pallas kernels for 0%

commit v1 on v0

--- a/solution.py
+++ b/solution.py
@@ -1,9 +1,16 @@
+import functools
+
 import jax
 import jax.numpy as jnp
 from jax import lax
+from jax.experimental import pallas as pl
+from jax.experimental.pallas import tpu as pltpu
 from jax.sharding import PartitionSpec as P
 
 HD = 72
+FRAMES = 16
+CLIP, FRAME, TENSOR = "clip", "frame", "tensor"
+SHARDS = (CLIP, FRAME)
 
 
 HIGHEST_PRECISION = lax.Precision.HIGHEST
@@ -104,31 +111,31 @@
 def fetch_weights(weights):
     cast = tuple((weight.astype(jnp.bfloat16) for weight in weights))
     return (
-        lax.all_gather(cast[0], ("clip", "frame"), axis=0, tiled=True),
-        lax.all_gather(cast[1], ("clip", "frame"), axis=0, tiled=True),
-        lax.all_gather(cast[2], ("clip", "frame"), axis=1, tiled=True),
-        lax.all_gather(cast[3], ("clip", "frame"), axis=0, tiled=True),
-        lax.all_gather(cast[4], ("clip", "frame"), axis=1, tiled=True),
+        lax.all_gather(cast[0], SHARDS, axis=0, tiled=True),
+        lax.all_gather(cast[1], SHARDS, axis=0, tiled=True),
+        lax.all_gather(cast[2], SHARDS, axis=1, tiled=True),
+        lax.all_gather(cast[3], SHARDS, axis=0, tiled=True),
+        lax.all_gather(cast[4], SHARDS, axis=1, tiled=True),
     )
 
 
 def backward_weights(weights):
     cast = tuple((weight.astype(jnp.bfloat16) for weight in weights))
     return (
-        lax.all_gather(cast[0], ("clip", "frame"), axis=0, tiled=True),
-        lax.all_gather(cast[1], ("clip", "frame"), axis=0, tiled=True),
-        lax.all_gather(cast[2], ("clip", "frame"), axis=1, tiled=True),
-        lax.all_gather(cast[3], ("clip", "frame"), axis=0, tiled=True),
-        lax.all_gather(cast[4], ("clip", "frame"), axis=1, tiled=True),
+        lax.all_gather(cast[0], SHARDS, axis=0, tiled=True),
+        lax.all_gather(cast[1], SHARDS, axis=0, tiled=True),
+        lax.all_gather(cast[2], SHARDS, axis=1, tiled=True),
+        lax.all_gather(cast[3], SHARDS, axis=0, tiled=True),
+        lax.all_gather(cast[4], SHARDS, axis=1, tiled=True),
     )
 
 
 def spread_rows(rows):
-    return lax.all_gather(rows, "tensor", axis=2, tiled=True)
+    return lax.all_gather(rows, TENSOR, axis=2, tiled=True)
 
 
 def collect_rows(term):
-    return lax.psum_scatter(term, "tensor", scatter_dimension=2, tiled=True)
+    return lax.psum_scatter(term, TENSOR, scatter_dimension=2, tiled=True)
 
 
 def attention_output(attended, attn_weight):
@@ -142,7 +149,7 @@
     partial_value = jnp.einsum(
         "cd,dkz->ckz", silu_cond, mod_weight, preferred_element_type=jnp.float32
     )
-    modulation = lax.all_gather(partial_value, "tensor", axis=2, tiled=True)
+    modulation = lax.all_gather(partial_value, TENSOR, axis=2, tiled=True)
     normed, inv_scale = layer_norm(stream)
     modulated = (normed * (1.0 + choose(modulation, 1)) + choose(modulation, 0)).astype(
         jnp.bfloat16
@@ -155,9 +162,9 @@
         project_held = projected
         attended, log_total = attend(project_held, True)
     else:
-        project_held = lax.all_to_all(projected, "frame", split_axis=2, concat_axis=1, tiled=True)
+        project_held = lax.all_to_all(projected, FRAME, split_axis=2, concat_axis=1, tiled=True)
         placed, log_total = attend(project_held, False)
-        attended = lax.all_to_all(placed, "frame", split_axis=1, concat_axis=2, tiled=True)
+        attended = lax.all_to_all(placed, FRAME, split_axis=1, concat_axis=2, tiled=True)
     branch_attn = attention_output(attended, attn_weight)
     middle = stream + choose(modulation, 2) * branch_attn
     normed_mlp, inv_mlp = layer_norm(middle)
@@ -239,10 +246,10 @@
     if spatial:
         d_projected = attend_back(project_held, log_total, d_attended, True)
     else:
-        d_placed = lax.all_to_all(d_attended, "frame", split_axis=2, concat_axis=1, tiled=True)
+        d_placed = lax.all_to_all(d_attended, FRAME, split_axis=2, concat_axis=1, tiled=True)
         d_projected = lax.all_to_all(
             attend_back(project_held, log_total, d_placed, False),
-            "frame",
+            FRAME,
             split_axis=1,
             concat_axis=2,
             tiled=True,
@@ -259,7 +266,7 @@
     d_modulation = jnp.stack(
         [d_shift_attn, d_scale_attn, d_gate_attn, d_shift_mlp, d_scale_mlp, d_gate_mlp], axis=1
     )
-    d_mod_own = lax.psum_scatter(d_modulation, "tensor", scatter_dimension=2, tiled=True)
+    d_mod_own = lax.psum_scatter(d_modulation, TENSOR, scatter_dimension=2, tiled=True)
     grad_mod = jnp.einsum(
         "cd,ckz->dkz", silu_cond.astype(jnp.float32), d_mod_own, precision=HIGHEST_PRECISION
     )
@@ -268,19 +275,19 @@
     )
     grads = (
         lax.psum_scatter(
-            grad_mod.astype(jnp.bfloat16), ("clip", "frame"), scatter_dimension=0, tiled=True
+            grad_mod.astype(jnp.bfloat16), SHARDS, scatter_dimension=0, tiled=True
         ).astype(jnp.float32),
         lax.psum_scatter(
-            grad_qkv.astype(jnp.bfloat16), ("clip", "frame"), scatter_dimension=0, tiled=True
+            grad_qkv.astype(jnp.bfloat16), SHARDS, scatter_dimension=0, tiled=True
         ).astype(jnp.float32),
         lax.psum_scatter(
-            grad_attn.astype(jnp.bfloat16), ("clip", "frame"), scatter_dimension=1, tiled=True
+            grad_attn.astype(jnp.bfloat16), SHARDS, scatter_dimension=1, tiled=True
         ).astype(jnp.float32),
         lax.psum_scatter(
-            grad_up.astype(jnp.bfloat16), ("clip", "frame"), scatter_dimension=0, tiled=True
+            grad_up.astype(jnp.bfloat16), SHARDS, scatter_dimension=0, tiled=True
         ).astype(jnp.float32),
         lax.psum_scatter(
-            grad_down.astype(jnp.bfloat16), ("clip", "frame"), scatter_dimension=1, tiled=True
+            grad_down.astype(jnp.bfloat16), SHARDS, scatter_dimension=1, tiled=True
         ).astype(jnp.float32),
     )
     return (d_stream, d_silu, grads)
@@ -319,7 +326,7 @@
     input_grad, d_silu_first, grads_first = layer_backward(
         d_middle_stream, silu_cond, back_first, stored_first, True
     )
-    d_silu_total = lax.psum(d_silu_first + d_silu_second, ("frame", "tensor"))
+    d_silu_total = lax.psum(d_silu_first + d_silu_second, (FRAME, TENSOR))
     sigmoid_cond = jax.nn.sigmoid(cond_float)
     cond_grad = d_silu_total * (sigmoid_cond * (1.0 + cond_float * (1.0 - sigmoid_cond)))
     return (
@@ -338,40 +345,610 @@
         grads_second[4],
     )
 
+def flip(array, axis, bit):
+    count = lax.axis_size(axis)
+    return lax.ppermute(array, axis, [(i, i ^ bit) for i in range(count)])
+
+
+def exchange_sum(array, axis):
+    bit = 1
+    while bit < lax.axis_size(axis):
+        array = array + flip(array, axis, bit)
+        bit *= 2
+    return array
+
+
+def place_along(array, axis):
+    count = lax.axis_size(axis)
+    own = (jnp.arange(count) == lax.axis_index(axis)).reshape((count,) + (1,) * array.ndim)
+    return exchange_sum(jnp.where(own, array[None], 0.0), axis)
+
+
+def first_flip(shard):
+    return 2 if shard % 2 == 0 else 4
+
+
+def hop(array, which):
+    if which == 0:
+        pairs = [(i, i ^ 1) for i in range(8)]
+    elif which == 1:
+        pairs = [(i, i ^ first_flip(i)) for i in range(8)]
+    else:
+        pairs = [(i, i ^ (6 - first_flip(i))) for i in range(8)]
+    return lax.ppermute(array, SHARDS, pairs)
+
+
+def shard_index():
+    return lax.axis_index(CLIP) * lax.axis_size(FRAME) + lax.axis_index(FRAME)
+
+
+def piece_order():
+    shard = shard_index()
+    first = jnp.where(shard % 2 == 0, 2, 4)
+    second = 6 - first
+    masks = [0, first, second, 6, 1, 1 ^ second, 1 ^ first, 7]
+    return jnp.stack([shard ^ mask for mask in masks]).astype(jnp.int32)
+
+
+def gather_piece(piece):
+    own = lax.all_gather(piece, TENSOR, axis=0, tiled=False)
+    near = hop(own, 1)
+    mine = (own, near, hop(own, 2), hop(near, 2))
+    return mine + tuple(hop(array, 0) for array in mine)
+
+
+def scatter_piece(grad):
+    keep, send = grad
+    got = hop(send, 0)
+    wide = lambda array: array.astype(jnp.float32)
+    low = lambda array: array.astype(jnp.bfloat16)
+    far = hop(low(wide(keep[2:]) + wide(got[2:])), 2)
+    near = hop(low(wide(keep[1]) + wide(got[1]) + wide(far[1])), 1)
+    own = low(wide(keep[0]) + wide(got[0]) + wide(far[0]) + wide(near))
+    return lax.psum_scatter(own, TENSOR, scatter_dimension=0, tiled=False)
+
+
+def pack_layer(weights):
+    qkv, attn, up, down = (weight.astype(jnp.bfloat16) for weight in weights)
+    rows = qkv.shape[0]
+    attn_part = jnp.concatenate([qkv.reshape(rows, -1), attn.T], axis=1)
+    return attn_part, up, down.T
+
+
+PIECES = 8
+VMEM_BYTES = 48 << 20
+
+
+def contract(left, right, left_dim, right_dim):
+    return lax.dot_general(
+        left, right, (((left_dim,), (right_dim,)), ((), ())), preferred_element_type=jnp.float32
+    )
+
+
+def assemble(order_ref, piece_refs, whole_ref):
+    rows = piece_refs[0].shape[1]
+    for j in range(PIECES):
+        start = pl.multiple_of(order_ref[j] * rows, 16)
+        whole_ref[pl.ds(start, rows), :] = piece_refs[j][0]
+
+
+def up_kernel(order_ref, x_ref, *refs):
+    pre_ref, act_ref, whole_ref = refs[PIECES:]
+    assemble(order_ref, refs[:PIECES], whole_ref)
+    pre = contract(x_ref[...], whole_ref[...], 1, 0)
+    pre_ref[...] = pre
+    act_ref[...] = gelu_tanh(pre).astype(jnp.bfloat16)
+
+
+def slope_kernel(order_ref, x_ref, pre_ref, *refs):
+    out_ref, whole_ref = refs[PIECES:]
+    assemble(order_ref, refs[:PIECES], whole_ref)
+    d_act = contract(x_ref[...], whole_ref[...], 1, 0)
+    out_ref[...] = (d_act * gelu_slope(pre_ref[...])).astype(jnp.bfloat16)
+
+
+def turned_kernel(low, high, order_ref, x_ref, *refs):
+    out_ref, whole_ref = refs[PIECES:]
+    assemble(order_ref, refs[:PIECES], whole_ref)
+    whole = contract(x_ref[...], whole_ref[...], 1, 0)
+    out_ref[0] = whole[:, low:high].astype(jnp.bfloat16).T
+
+
+def collect_kernel(low, high, turned, order_ref, y_ref, *refs):
+    out_ref, whole_ref = refs[PIECES:]
+    assemble(order_ref, refs[:PIECES], whole_ref)
+    rows = y_ref[0].T if turned else y_ref[...]
+    term = contract(rows, whole_ref[:, low:high], 1, 1)
+
+    @pl.when(pl.program_id(0) == 0)
+    def _():
+        out_ref[...] = term
+
+    @pl.when(pl.program_id(0) > 0)
+    def _():
+        out_ref[...] += term
+
+
+def deal_out(order_ref, whole_ref, keep_ref, send_ref):
+    rows = keep_ref.shape[2]
+    for j in range(PIECES):
+        start = pl.multiple_of(order_ref[j] * rows, 16)
+        to_ref = keep_ref if j < PIECES // 2 else send_ref
+        to_ref[j % (PIECES // 2), 0] = whole_ref[pl.ds(start, rows), :]
+
+
+def grad_kernel(order_ref, x_ref, y_ref, keep_ref, send_ref, whole_ref):
+    whole_ref[...] = contract(x_ref[...], y_ref[...], 0, 0).astype(jnp.bfloat16)
+    deal_out(order_ref, whole_ref, keep_ref, send_ref)
+
+
+def attn_grad_kernel(order_ref, x_ref, y_ref, b_ref, a_ref, keep_ref, send_ref, whole_ref):
+    split = y_ref.shape[1]
+    whole_ref[:, :split] = contract(x_ref[...], y_ref[0].T, 0, 0).astype(jnp.bfloat16)
+    whole_ref[:, split:] = contract(b_ref[...], a_ref[0].T, 0, 0).astype(jnp.bfloat16)
+    deal_out(order_ref, whole_ref, keep_ref, send_ref)
+
+
+def masked_scores(queries, keys, group):
+    scores = contract(queries, keys, 0, 0) * HD ** (-0.5)
+    if group:
+        place = lax.broadcasted_iota(jnp.int32, scores.shape, 0) % group
+        other = lax.broadcasted_iota(jnp.int32, scores.shape, 1) % group
+        scores = jnp.where(place == other, scores, -3e38)
+    expo = jnp.exp(scores - jnp.max(scores, axis=-1, keepdims=True))
+    return expo / jnp.sum(expo, axis=-1, keepdims=True)
+
+
+def attend_kernel(group, projected_ref, out_ref):
+    part = out_ref.shape[1]
+    for start in range(0, part, HD):
+        queries, keys, values = (
+            projected_ref[0, pl.ds(j * part + start, HD), :] for j in range(3)
+        )
+        probs = masked_scores(queries, keys, group).astype(jnp.bfloat16)
+        out_ref[0, pl.ds(start, HD), :] = contract(values, probs, 1, 1).astype(jnp.bfloat16)
+
+
+def attend_back_kernel(group, projected_ref, upstream_ref, out_ref):
+    part = upstream_ref.shape[1]
+    scale_factor = HD ** (-0.5)
+    for start in range(0, part, HD):
+        queries, keys, values = (
+            projected_ref[0, pl.ds(j * part + start, HD), :] for j in range(3)
+        )
+        upstream = upstream_ref[0, pl.ds(start, HD), :]
+        probs = masked_scores(queries, keys, group)
+        d_probs = contract(upstream, values, 0, 0)
+        row_inner = jnp.sum(probs * d_probs, axis=-1, keepdims=True)
+        d_scores = (probs * (d_probs - row_inner)).astype(jnp.bfloat16)
+        grads = (
+            contract(keys, d_scores, 1, 1) * scale_factor,
+            contract(queries, d_scores, 1, 0) * scale_factor,
+            contract(upstream, probs.astype(jnp.bfloat16), 1, 0),
+        )
+        for j in range(3):
+            out_ref[0, pl.ds(j * part + start, HD), :] = grads[j].astype(jnp.bfloat16)
+
+
+def call(kernel, grid, in_specs, out_specs, out_shape, scratch, flops, args):
+    moved = sum(a.size * a.dtype.itemsize for a in args)
+    moved += sum(o.size * o.dtype.itemsize for o in jax.tree.leaves(out_shape))
+    return pl.pallas_call(
+        kernel,
+        out_shape=out_shape,
+        grid_spec=pltpu.PrefetchScalarGridSpec(
+            num_scalar_prefetch=1 if scratch else 0,
+            grid=grid,
+            in_specs=in_specs,
+            out_specs=out_specs,
+            scratch_shapes=scratch,
+        ),
+        compiler_params=pltpu.CompilerParams(vmem_limit_bytes=VMEM_BYTES),
+        cost_estimate=pl.CostEstimate(flops=flops, bytes_accessed=moved, transcendentals=0),
+    )(*args)
+
+
+def still(shape):
+    return pl.BlockSpec(shape, lambda z, *_: (0,) * len(shape))
+
+
+def lead(shape):
+    return pl.BlockSpec((1,) + shape, lambda z, *_: (z,) + (0,) * len(shape))
+
+
+def column(tokens, width):
+    return pl.BlockSpec((tokens, width), lambda z, *_: (0, z))
+
+
+def sizes(pieces):
+    return pieces[0].shape + (pieces[0].shape[1] * PIECES,)
+
+
+def times_up(order, x, pieces):
+    groups, rows, width, depth = sizes(pieces)
+    tokens = x.shape[0]
+    shape = (tokens, groups * width)
+    return call(
+        up_kernel,
+        (groups,),
+        [still(x.shape)] + [lead((rows, width))] * PIECES,
+        [column(tokens, width)] * 2,
+        [jax.ShapeDtypeStruct(shape, jnp.float32), jax.ShapeDtypeStruct(shape, jnp.bfloat16)],
+        [pltpu.VMEM((depth, width), jnp.bfloat16)],
+        2 * tokens * depth * width * groups,
+        (order, x) + pieces,
+    )
+
+
+def times_slope(order, x, pre, pieces):
+    groups, rows, width, depth = sizes(pieces)
+    tokens = x.shape[0]
+    return call(
+        slope_kernel,
+        (groups,),
+        [still(x.shape), column(tokens, width)] + [lead((rows, width))] * PIECES,
+        column(tokens, width),
+        jax.ShapeDtypeStruct(pre.shape, jnp.bfloat16),
+        [pltpu.VMEM((depth, width), jnp.bfloat16)],
+        2 * tokens * depth * width * groups,
+        (order, x, pre) + pieces,
+    )
+
+
+def times_turned(order, x, pieces, low, high):
+    groups, rows, width, depth = sizes(pieces)
+    tokens = x.shape[0]
+    return call(
+        functools.partial(turned_kernel, low, high),
+        (groups,),
+        [still(x.shape)] + [lead((rows, width))] * PIECES,
+        lead((high - low, tokens)),
+        jax.ShapeDtypeStruct((groups, high - low, tokens), jnp.bfloat16),
+        [pltpu.VMEM((depth, width), jnp.bfloat16)],
+        2 * tokens * depth * width * groups,
+        (order, x) + pieces,
+    )
+
+
+def collect(order, y, pieces, low, high, turned):
+    groups, rows, width, depth = sizes(pieces)
+    tokens = y.shape[2] if turned else y.shape[0]
+    return call(
+        functools.partial(collect_kernel, low, high, turned),
+        (groups,),
+        [lead(y.shape[1:]) if turned else column(tokens, width)]
+        + [lead((rows, width))] * PIECES,
+        still((tokens, depth)),
+        jax.ShapeDtypeStruct((tokens, depth), jnp.float32),
+        [pltpu.VMEM((depth, width), jnp.bfloat16)],
+        2 * tokens * depth * (high - low) * groups,
+        (order, y) + pieces,
+    )
+
+
+def grad_call(kernel, args, specs, groups, depth, width):
+    rows = depth // PIECES
+    half = PIECES // 2
+    tokens = args[1].shape[0]
+    return call(
+        kernel,
+        (groups,),
+        specs,
+        [pl.BlockSpec((half, 1, rows, width), lambda z, *_: (0, z, 0, 0))] * 2,
+        [jax.ShapeDtypeStruct((half, groups, rows, width), jnp.bfloat16)] * 2,
+        [pltpu.VMEM((depth, width), jnp.bfloat16)],
+        2 * tokens * depth * width * groups,
+        args,
+    )
+
+
+def grad_of(order, x, y, groups):
+    tokens, width = x.shape[0], y.shape[1] // groups
+    specs = [still(x.shape), column(tokens, width)]
+    return grad_call(grad_kernel, (order, x, y), specs, groups, x.shape[1], width)
+
+
+def attn_grad_of(order, x, y, b, a):
+    groups, wide, tokens = y.shape
+    part = a.shape[1]
+    specs = [still(x.shape), lead((wide, tokens)), still(b.shape), lead((part, tokens))]
+    args = (order, x, y, b, a)
+    return grad_call(attn_grad_kernel, args, specs, groups, x.shape[1], wide + part)
+
+
+def attend_call(projected, group):
+    groups, wide, tokens = projected.shape
+    part = wide // 3
+    return call(
+        functools.partial(attend_kernel, group),
+        (groups,),
+        [lead((wide, tokens))],
+        lead((part, tokens)),
+        jax.ShapeDtypeStruct((groups, part, tokens), jnp.bfloat16),
+        [],
+        4 * tokens * tokens * part * groups,
+        (projected,),
+    )
+
+
+def attend_back_call(projected, upstream, group):
+    groups, wide, tokens = projected.shape
+    part = wide // 3
+    return call(
+        functools.partial(attend_back_kernel, group),
+        (groups,),
+        [lead((wide, tokens)), lead((part, tokens))],
+        lead((wide, tokens)),
+        jax.ShapeDtypeStruct((groups, wide, tokens), jnp.bfloat16),
+        [],
+        10 * tokens * tokens * part * groups,
+        (projected, upstream),
+    )
+
+
+def own_forward(stream, modulation, order, weights, group):
+    attn, up, down = weights
+    width = attn[0].shape[2]
+    part = width // 4
+    normed, inv_scale = layer_norm(stream)
+    modulated = (normed * (1.0 + modulation[1]) + modulation[0]).astype(jnp.bfloat16)
+    projected = times_turned(order, modulated, attn, 0, 3 * part)
+    attended = attend_call(projected, group)
+    branch_attn = collect(order, attended, attn, 3 * part, width, True)
+    middle = stream + modulation[2] * branch_attn
+    normed_mlp, inv_mlp = layer_norm(middle)
+    modulated_mlp = (normed_mlp * (1.0 + modulation[4]) + modulation[3]).astype(jnp.bfloat16)
+    hidden_pre, hidden_act = times_up(order, modulated_mlp, up)
+    branch_mlp = collect(order, hidden_act, down, 0, width, False)
+    result = middle + modulation[5] * branch_mlp
+    stored = (
+        normed,
+        inv_scale,
+        modulated,
+        projected,
+        attended,
+        branch_attn,
+        normed_mlp,
+        inv_mlp,
+        modulated_mlp,
+        hidden_pre,
+        hidden_act,
+        branch_mlp,
+    )
+    return result, stored
+
+
+def own_backward(upstream, modulation, order, weights, stored, group):
+    attn, up, down = weights
+    width = attn[0].shape[2]
+    part = width // 4
+    groups = attn[0].shape[0]
+    (
+        normed,
+        inv_scale,
+        modulated,
+        projected,
+        attended,
+        branch_attn,
+        normed_mlp,
+        inv_mlp,
+        modulated_mlp,
+        hidden_pre,
+        hidden_act,
+        branch_mlp,
+    ) = stored
+    d_branch_mlp = (upstream * modulation[5]).astype(jnp.bfloat16)
+    d_gate_mlp = jnp.sum(upstream * branch_mlp, axis=0)
+    grad_down = grad_of(order, d_branch_mlp, hidden_act, groups)
+    d_pre = times_slope(order, d_branch_mlp, hidden_pre, down)
+    grad_up = grad_of(order, modulated_mlp, d_pre, groups)
+    d_mod_mlp = collect(order, d_pre, up, 0, width, False)
+    d_shift_mlp = jnp.sum(d_mod_mlp, axis=0)
+    d_scale_mlp = jnp.sum(d_mod_mlp * normed_mlp, axis=0)
+    d_middle = upstream + norm_back(normed_mlp, inv_mlp, d_mod_mlp * (1.0 + modulation[4]))
+    d_branch_attn = (d_middle * modulation[2]).astype(jnp.bfloat16)
+    d_gate_attn = jnp.sum(d_middle * branch_attn, axis=0)
+    d_attended = times_turned(order, d_branch_attn, attn, 3 * part, width)
+    d_projected = attend_back_call(projected, d_attended, group)
+    grad_attn = attn_grad_of(order, modulated, d_projected, d_branch_attn, attended)
+    d_modulated = collect(order, d_projected, attn, 0, 3 * part, True)
+    d_shift_attn = jnp.sum(d_modulated, axis=0)
+    d_scale_attn = jnp.sum(d_modulated * normed, axis=0)
+    d_stream = d_middle + norm_back(normed, inv_scale, d_modulated * (1.0 + modulation[1]))
+    d_modulation = jnp.stack(
+        [d_shift_attn, d_scale_attn, d_gate_attn, d_shift_mlp, d_scale_mlp, d_gate_mlp]
+    )
+    return d_stream, d_modulation, (grad_attn, grad_up, grad_down)
+
+
+def finish_grads(attn_piece, up_piece, down_piece):
+    rows, width = attn_piece.shape
+    part = width // 4
+    qkv = attn_piece[:, : 3 * part].reshape(rows, 3, part).astype(jnp.float32)
+    attn = attn_piece[:, 3 * part :].T.astype(jnp.float32)
+    return qkv, attn, up_piece.astype(jnp.float32), down_piece.T.astype(jnp.float32)
+
+
+def places_out(stream):
+    clips, frames, places, width = stream.shape
+    devices, tensors = lax.axis_size(FRAME), lax.axis_size(TENSOR)
+    part = places // (devices * tensors)
+    blocks = stream.reshape(clips, frames, tensors, devices, part, width).transpose(
+        0, 1, 3, 2, 4, 5
+    )
+    return lax.all_to_all(
+        blocks.reshape(clips, frames, places, width),
+        (FRAME, TENSOR),
+        split_axis=2,
+        concat_axis=1,
+        tiled=True,
+    )
+
+
+def places_back(stream):
+    devices, tensors = lax.axis_size(FRAME), lax.axis_size(TENSOR)
+    moved = lax.all_to_all(stream, (FRAME, TENSOR), split_axis=1, concat_axis=2, tiled=True)
+    clips, frames, places, width = moved.shape
+    part = places // (devices * tensors)
+    blocks = moved.reshape(clips, frames, devices, tensors, part, width).transpose(
+        0, 1, 3, 2, 4, 5
+    )
+    return blocks.reshape(clips, frames, places, width)
+
+
+def local_whole(
+    x_in,
+    cond,
+    mod_weight_one,
+    qkv_weight_one,
+    attn_out_one,
+    mlp_up_one,
+    mlp_down_one,
+    mod_weight_two,
+    qkv_weight_two,
+    attn_out_two,
+    mlp_up_two,
+    mlp_down_two,
+    out_cotangent,
+):
+    rows, _, part = qkv_weight_one.shape
+    width = x_in.shape[-1]
+    packed = [
+        pack_layer((qkv_weight_one, attn_out_one, mlp_up_one, mlp_down_one)),
+        pack_layer((qkv_weight_two, attn_out_two, mlp_up_two, mlp_down_two)),
+    ]
+    cond_every = lax.all_gather(cond, CLIP, axis=0, tiled=True).astype(jnp.float32)
+    clip_count = cond_every.shape[0]
+    silu_every = jax.nn.silu(cond_every).astype(jnp.bfloat16)
+    silu_rows = lax.dynamic_slice_in_dim(silu_every, shard_index() * rows, rows, axis=1)
+    mod_weights = (mod_weight_one.astype(jnp.bfloat16), mod_weight_two.astype(jnp.bfloat16))
+    partial_value = jnp.stack(
+        [
+            jnp.einsum("cd,dkz->ckz", silu_rows, weight, preferred_element_type=jnp.float32)
+            for weight in mod_weights
+        ],
+        axis=1,
+    )
+    summed = exchange_sum(exchange_sum(partial_value, FRAME), CLIP)
+    summed = lax.dynamic_index_in_dim(summed, lax.axis_index(CLIP), 0, keepdims=False)
+    placed = place_along(summed, TENSOR)
+    modulations = placed.transpose(1, 2, 0, 3).reshape(summed.shape[:2] + (-1,))
+
+    order = piece_order()
+    whole_weights = [[gather_piece(piece) for piece in pieces] for pieces in packed]
+
+    frames_in = lax.all_to_all(x_in, TENSOR, split_axis=1, concat_axis=2, tiled=True)
+    cotangent = lax.all_to_all(out_cotangent, FRAME, split_axis=2, concat_axis=1, tiled=True)
+    frame_shape, place_shape = frames_in.shape, cotangent.shape
+    group = place_shape[2]
+    wide = lambda array: array.reshape(-1, width).astype(jnp.float32)
+    low = lambda array, shape: array.astype(jnp.bfloat16).reshape(shape)
+    middle_stream, stored_first = own_forward(
+        wide(frames_in), modulations[0], order, whole_weights[0], 0
+    )
+    second_in = wide(places_out(low(middle_stream, frame_shape)))
+    result, stored_second = own_forward(
+        second_in, modulations[1], order, whole_weights[1], group
+    )
+    layer_out = lax.all_to_all(
+        low(result, place_shape), FRAME, split_axis=1, concat_axis=2, tiled=True
+    )
+    d_second, d_mod_second, grads_second = own_backward(
+        wide(cotangent), modulations[1], order, whole_weights[1], stored_second, group
+    )
+    d_first_out = wide(places_back(low(d_second, place_shape)))
+    d_first, d_mod_first, grads_first = own_backward(
+        d_first_out, modulations[0], order, whole_weights[0], stored_first, 0
+    )
+    input_grad = lax.all_to_all(
+        low(d_first, frame_shape), TENSOR, split_axis=2, concat_axis=1, tiled=True
+    ).astype(jnp.float32)
+
+    second_out = finish_grads(*(scatter_piece(grad) for grad in grads_second))
+    first_out = finish_grads(*(scatter_piece(grad) for grad in grads_first))
+
+    d_mods = jnp.stack([d_mod_first, d_mod_second])
+    d_mods = exchange_sum(exchange_sum(d_mods, FRAME), TENSOR)
+    d_mods = lax.dynamic_slice_in_dim(d_mods, lax.axis_index(TENSOR) * part, part, axis=2)
+    d_every = place_along(d_mods, CLIP)
+    silu_float = silu_rows.astype(jnp.float32)
+    grad_mods = [
+        sum(
+            silu_float[c][:, None, None] * d_every[c, layer][None] for c in range(clip_count)
+        )
+        for layer in range(2)
+    ]
+    d_silu = jnp.stack(
+        [
+            sum(
+                jnp.sum(
+                    d_every[c, layer][None] * mod_weights[layer].astype(jnp.float32), axis=(1, 2)
+                )
+                for layer in range(2)
+            )
+            for c in range(clip_count)
+        ]
+    )
+    d_silu = place_along(place_along(exchange_sum(d_silu, TENSOR), FRAME), CLIP)
+    d_silu = d_silu.transpose(2, 0, 1, 3).reshape(clip_count, -1)
+    d_silu = lax.dynamic_slice_in_dim(d_silu, lax.axis_index(CLIP), 1, axis=0)
+    cond_float = cond.astype(jnp.float32)
+    sigmoid_cond = jax.nn.sigmoid(cond_float)
+    cond_grad = d_silu * (sigmoid_cond * (1.0 + cond_float * (1.0 - sigmoid_cond)))
+    return (
+        layer_out,
+        input_grad,
+        cond_grad,
+        grad_mods[0],
+        *first_out,
+        grad_mods[1],
+        *second_out,
+    )
+
+
+def holds_whole(mesh):
+    tensors = mesh.shape[TENSOR]
+    return (
+        mesh.shape[CLIP] == 2
+        and mesh.shape[FRAME] == 4
+        and FRAMES % (4 * tensors) == 0
+        and tensors & (tensors - 1) == 0
+    )
+
 
 def solution(mesh):
     return jax.shard_map(
-        local,
+        local_whole if holds_whole(mesh) else local,
         mesh=mesh,
         in_specs=(
-            P("clip", "frame", "tensor", None),
-            P("clip", None),
-            P(("clip", "frame"), None, "tensor"),
-            P(("clip", "frame"), None, "tensor"),
-            P("tensor", ("clip", "frame")),
-            P(("clip", "frame"), "tensor"),
-            P("tensor", ("clip", "frame")),
-            P(("clip", "frame"), None, "tensor"),
-            P(("clip", "frame"), None, "tensor"),
-            P("tensor", ("clip", "frame")),
-            P(("clip", "frame"), "tensor"),
-            P("tensor", ("clip", "frame")),
-            P("clip", "frame", "tensor", None),
+            P(CLIP, FRAME, TENSOR, None),
+            P(CLIP, None),
+            P(SHARDS, None, TENSOR),
+            P(SHARDS, None, TENSOR),
+            P(TENSOR, SHARDS),
+            P(SHARDS, TENSOR),
+            P(TENSOR, SHARDS),
+            P(SHARDS, None, TENSOR),
+            P(SHARDS, None, TENSOR),
+            P(TENSOR, SHARDS),
+            P(SHARDS, TENSOR),
+            P(TENSOR, SHARDS),
+            P(CLIP, FRAME, TENSOR, None),
         ),
         out_specs=(
-            P("clip", "frame", "tensor", None),
-            P("clip", "frame", "tensor", None),
-            P("clip", None),
-            P(("clip", "frame"), None, "tensor"),
-            P(("clip", "frame"), None, "tensor"),
-            P("tensor", ("clip", "frame")),
-            P(("clip", "frame"), "tensor"),
-            P("tensor", ("clip", "frame")),
-            P(("clip", "frame"), None, "tensor"),
-            P(("clip", "frame"), None, "tensor"),
-            P("tensor", ("clip", "frame")),
-            P(("clip", "frame"), "tensor"),
-            P("tensor", ("clip", "frame")),
+            P(CLIP, FRAME, TENSOR, None),
+            P(CLIP, FRAME, TENSOR, None),
+            P(CLIP, None),
+            P(SHARDS, None, TENSOR),
+            P(SHARDS, None, TENSOR),
+            P(TENSOR, SHARDS),
+            P(SHARDS, TENSOR),
+            P(TENSOR, SHARDS),
+            P(SHARDS, None, TENSOR),
+            P(SHARDS, None, TENSOR),
+            P(TENSOR, SHARDS),
+            P(SHARDS, TENSOR),
+            P(TENSOR, SHARDS),
         ),
         check_vma=False,
     )

time: 2190 us -> 852 us (0.39)
  waiting for transfers between devices: 1670 us -> 370 us
  Pallas kernels: 0 us -> 211 us
  matrix products: 185 us -> 0.41 us
  blocking collectives: 155 us -> 5.26 us
  starting transfers between devices: 11.7 us -> 93.2 us
  other arithmetic: 81.1 us -> 115 us
    reduce_scatter x18 -> x6, waiting for transfers between devices: 1040 us -> 15.9 us  [scatter_piece(): return lax.psum_scatter(own, TENSOR, scatter_dimension=0, tiled=False)]
    all_gather x16 -> x6, waiting for transfers between devices: 622 us -> 45.5 us  [gather_piece(): own = lax.all_gather(piece, TENSOR, axis=0, tiled=False)]
    ppermute x0 -> x75, waiting for transfers between devices: none -> 270 us  [the longest x60 224 us: hop(): return lax.ppermute(array, SHARDS, pairs)]
    pallas_call x0 -> x26, Pallas kernels: none -> 211 us  [call(): pl.pallas_call(kernel, out_shape=out_shape, grid_spec=pltpu.PrefetchScala...]
    dot_general x40 -> x2, matrix products: 185 us -> 0.41 us  [local_whole(): jnp.einsum('cd,dkz->ckz', silu_rows, weight, preferred_element_type=jnp.f...]
    ppermute x0 -> x75, starting transfers between devices: none -> 68.1 us  [the longest x60 48.7 us: hop(): return lax.ppermute(array, SHARDS, pairs)]
    all_to_all x2 -> x0, blocking collectives: 62.5 us -> none  [the longest x1 31.3 us: layer_forward(): lax.all_to_all(projected, 'frame', split_axis=2, concat_axis=1, tiled=True)]
    all_gather x4 -> x1, blocking collectives: 58.5 us -> 5.26 us  [local_whole(): lax.all_gather(cond, CLIP, axis=0, tiled=True).astype(jnp.float32)]
  transfers between devices with their start and end apart: 38 -> 93, of which waited for: 35 -> 32; matrix products, arithmetic and copies ran while one was open for 8% -> 15% of each run, Pallas kernels for 0% -> 18%
where the time goes in v1:
time: 852 us
  waiting for transfers between devices  370 us (43%)
  Pallas kernels  211 us (25%)
  other arithmetic  115 us (13%)
  starting transfers between devices  93.2 us (11%)
  local copies, waits for them, and re-layouts  40.3 us (5%)
  between operations  15.9 us (2%)
    ppermute x60, waiting for transfers between devices, hop(): return lax.ppermute(array, SHARDS, pairs)  224 us
    pallas_call x26, Pallas kernels, call(): pl.pallas_call(kernel, out_shape=out_shape, grid_spec=pltpu.PrefetchScala...  211 us
    convert_element_type x18, other arithmetic, scatter_piece(): low = lambda array: array.astype(jnp.bfloat16)  67.6 us
    ppermute x60, starting transfers between devices, hop(): return lax.ppermute(array, SHARDS, pairs)  48.7 us
    ppermute x15, waiting for transfers between devices, flip(): return lax.ppermute(array, axis, [(i, i ^ bit) for i in range(count)])  46.1 us
    all_gather x6, waiting for transfers between devices, gather_piece(): own = lax.all_gather(piece, TENSOR, axis=0, tiled=False)  45.5 us
    unnamed x155, local copies, waits for them, and re-layouts  31 us
    all_to_all x1, waiting for transfers between devices, local_whole(): lax.all_to_all(x_in, TENSOR, split_axis=1, concat_axis=2, tiled=True)  21.9 us
  transfers between devices with their start and end apart: 93, of which 32 were waited for; matrix products, arithmetic and copies ran while one was open for 15% of the time, Pallas kernels for 18%

profile of v1, /device:TPU:0, one launch (start us, length us, event | category | flops | bytes accessed | tf_op | source)
XLA Modules:
  0.0 851.8 jit_solution(15998201904424214651)
XLA Ops:
  20.0 26.5 %all-gather.14.cloned.1.call-done = bf16[576,1152]{1,0:T(8,128)(2,1)} async-done(((bf16[144,1152]{1,0:T(8,128)(2,1)}), bf16[576,1152]{1,0:T(8,128)(2,1)}) %all-gather.14.cloned.1.call-update) | async-done | bytes 1327120 | tf_op jit(solution)/shard_map/all_gather | solution.py:394
  51.4 27.5 %collective-permute-done.1 = f32[2,2,6,288]{3,0,2,1:T(2,128)S(1)} collective-permute-done((f32[2,2,6,288]{3,0,2,1:T(2,128)S(1)}, f32[2,2,6,288]{3,0,2,1:T(2,128)S(1)}, u32[]{:S(2)}, u32[]{:S(2)}) %collective-permute-start.1) | collective-permute-done | bytes 27680 | tf_op jit(solution)/shard_map/ppermute | solution.py:350
  97.1 19.0 %all-gather.18.cloned.1.call-done = bf16[576,1152]{1,0:T(8,128)(2,1)} async-done(((bf16[144,1152]{1,0:T(8,128)(2,1)}), bf16[576,1152]{1,0:T(8,128)(2,1)}) %all-gather.18.cloned.1.call-update) | async-done | bytes 1327120 | tf_op jit(solution)/shard_map/all_gather | solution.py:394
  123.2 27.4 %collective-permute-done.19.refs_1_ = bf16[4,144,1152]{2,1,0:T(8,128)(2,1)} collective-permute-done((bf16[4,144,1152]{2,1,0:T(8,128)(2,1)}, bf16[4,144,1152]{2,1,0:T(8,128)(2,1)}, u32[]{:S(2)}, u32[]{:S(2)}) %collective-permute-start.19) | collective-permute-done | bytes 1327136 | tf_op jit(solution)/shard_map/ppermute | solution.py:378
  160.7 21.9 %all-to-all-done = bf16[1,4,64,1152]{3,2,0,1:T(8,128)(2,1)S(1)} async-done(((bf16[1,4,64,1152]{3,2,0,1:T(8,128)(2,1)}), bf16[1,4,64,1152]{3,2,0,1:T(8,128)(2,1)S(1)}, u32[]{:S(2)}, u32[]{:S(2)}) %all-to-all-start) | async-done | bytes 589856 | tf_op jit(solution)/shard_map/all_to_all | solution.py:840
  211.8 13.6 %collective-permute-done.26.refs_1_ = bf16[4,144,1152]{2,1,0:T(8,128)(2,1)} collective-permute-done((bf16[4,144,1152]{2,1,0:T(8,128)(2,1)}, bf16[4,144,1152]{2,1,0:T(8,128)(2,1)}, u32[]{:S(2)}, u32[]{:S(2)}) %collective-permute-start.26) | collective-permute-done | bytes 1327136 | tf_op jit(solution)/shard_map/ppermute | solution.py:378
  247.5 9.2 %shard_map.231 = (f32[256,4608]{1,0:T(8,128)}, bf16[256,4608]{1,0:T(8,128)(2,1)}) custom-call(s32[8]{0:T(128)S(1)} %stack.103.order_ref, bf16[256,1152]{1,0:T(8,128)(2,1)S(1)} %add_convert_fusion.15.x_ref, bf16[4,144,1152]{2,1,0:T(8,128)(2,1)S(1)} %bitcast.239, bf16[4,144,1152]{2,1,0:T(8,128)(2,1)S(1)} %copy-done.19, ...), custom_call_target="tpu_custom_call" | custom-call | flops 2717908992 | bytes 18284576 | tf_op jit(solution)/shard_map/pallas_call | solution.py:536
  256.7 8.6 %shard_map.232 = f32[256,1152]{1,0:T(8,128)S(1)} custom-call(s32[8]{0:T(128)S(1)} %stack.103.order_ref, bf16[256,4608]{1,0:T(8,128)(2,1)} %get-tuple-element.29.y_ref, bf16[4,144,1152]{2,1,0:T(8,128)(2,1)} %bitcast.22.refs_0_, bf16[4,144,1152]{2,1,0:T(8,128)(2,1)} %collective-permute-done.19.refs_1_, bf16[4,144,1152]{2,1,0:T(8,128)(2,1)} %collective-permute-done.20.refs_2_, ...), custom_call_target="tpu_custom_call" | custom-call | flops 2717908992 | bytes 14155808 | tf_op jit(solution)/shard_map/pallas_call | solution.py:536
  281.1 8.7 %collective-permute-done.34.refs_2_ = bf16[4,144,1152]{2,1,0:T(8,128)(2,1)} collective-permute-done((bf16[4,144,1152]{2,1,0:T(8,128)(2,1)}, bf16[4,144,1152]{2,1,0:T(8,128)(2,1)}, u32[]{:S(2)}, u32[]{:S(2)}) %collective-permute-start.34) | collective-permute-done | bytes 1327136 | tf_op jit(solution)/shard_map/ppermute | solution.py:378
  292.2 22.4 %collective-permute-done.28.refs_3_ = bf16[4,144,1152]{2,1,0:T(8,128)(2,1)} collective-permute-done((bf16[4,144,1152]{2,1,0:T(8,128)(2,1)}, bf16[4,144,1152]{2,1,0:T(8,128)(2,1)}, u32[]{:S(2)}, u32[]{:S(2)}) %collective-permute-start.28) | collective-permute-done | bytes 1327136 | tf_op jit(solution)/shard_map/ppermute | solution.py:378
  358.8 13.6 %collective-permute-done.42.refs_3_ = bf16[4,144,1152]{2,1,0:T(8,128)(2,1)S(1)} collective-permute-done((bf16[4,144,1152]{2,1,0:T(8,128)(2,1)}, bf16[4,144,1152]{2,1,0:T(8,128)(2,1)S(1)}, u32[]{:S(2)}, u32[]{:S(2)}) %collective-permute-start.42) | collective-permute-done | bytes 1327136 | tf_op jit(solution)/shard_map/ppermute | solution.py:378
  374.2 9.2 %shard_map.236 = (f32[256,4608]{1,0:T(8,128)}, bf16[256,4608]{1,0:T(8,128)(2,1)}) custom-call(s32[8]{0:T(128)S(1)} %stack.103.order_ref, bf16[256,1152]{1,0:T(8,128)(2,1)S(1)} %add_convert_fusion.13.x_ref, bf16[4,144,1152]{2,1,0:T(8,128)(2,1)S(1)} %bitcast.244, bf16[4,144,1152]{2,1,0:T(8,128)(2,1)} %collective-permute-done.33.refs_1_, ...), custom_call_target="tpu_custom_call" | custom-call | flops 2717908992 | bytes 18284576 | tf_op jit(solution)/shard_map/pallas_call | solution.py:536
  383.5 9.5 %shard_map.238.y_ref = bf16[256,4608]{1,0:T(8,128)(2,1)} custom-call(s32[8]{0:T(128)S(1)} %stack.103.order_ref, bf16[256,1152]{1,0:T(8,128)(2,1)S(1)} %copy-done.38, f32[256,4608]{1,0:T(8,128)} %get-tuple-element.31.pre_ref, bf16[4,144,1152]{2,1,0:T(8,128)(2,1)S(1)} %bitcast.249, bf16[4,144,1152]{2,1,0:T(8,128)(2,1)} %collective-permute-done.40.refs_1_, ...), custom_call_target="tpu_custom_call" | custom-call | flops 2717908992 | bytes 18284576 | tf_op jit(solution)/shard_map/pallas_call | solution.py:536
  411.4 19.2 %shard_map.240.upstream_ref = bf16[4,288,256]{2,1,0:T(8,128)(2,1)S(1)} custom-call(s32[8]{0:T(128)S(1)} %stack.103.order_ref, bf16[256,1152]{1,0:T(8,128)(2,1)S(1)} %multiply_convert_fusion.1.x_ref.b_ref, bf16[4,144,1152]{2,1,0:T(8,128)(2,1)} %bitcast.28.refs_0_, bf16[4,144,1152]{2,1,0:T(8,128)(2,1)} %collective-permute-done.26.refs_1_, ...), custom_call_target="tpu_custom_call" | custom-call | flops 2717908992 | bytes 11796512 | tf_op jit(solution)/shard_map/pallas_call | solution.py:536
  430.6 8.4 shard_map.241.y_ref
  479.3 10.4 %shard_map.243.y_ref = bf16[256,4608]{1,0:T(8,128)(2,1)} custom-call(s32[8]{0:T(128)S(1)} %stack.103.order_ref, bf16[256,1152]{1,0:T(8,128)(2,1)S(1)} %fusion.33.x_ref, f32[256,4608]{1,0:T(8,128)} %get-tuple-element.32.pre_ref, bf16[4,144,1152]{2,1,0:T(8,128)(2,1)} %bitcast.22.refs_0_, bf16[4,144,1152]{2,1,0:T(8,128)(2,1)} %collective-permute-done.19.refs_1_, ...), custom_call_target="tpu_custom_call" | custom-call | flops 2717908992 | bytes 18284576 | tf_op jit(solution)/shard_map/pallas_call | solution.py:536
  513.0 8.4 shard_map.246.y_ref
  571.4 15.9 %collective-permute-done.68 = bf16[4,144,1152]{2,1,0:T(8,128)(2,1)S(1)} collective-permute-done((bf16[4,144,1152]{2,1,0:T(8,128)(2,1)S(1)}, bf16[4,144,1152]{2,1,0:T(8,128)(2,1)S(1)}, u32[]{:S(2)}, u32[]{:S(2)}) %collective-permute-start.68) | collective-permute-done | bytes 1327136 | tf_op jit(solution)/shard_map/ppermute | solution.py:378
  613.9 18.5 %collective-permute-done.71 = bf16[4,144,1152]{2,1,0:T(8,128)(2,1)S(1)} collective-permute-done((bf16[4,144,1152]{2,1,0:T(8,128)(2,1)S(1)}, bf16[4,144,1152]{2,1,0:T(8,128)(2,1)S(1)}, u32[]{:S(2)}, u32[]{:S(2)}) %collective-permute-start.71) | collective-permute-done | bytes 1327136 | tf_op jit(solution)/shard_map/ppermute | solution.py:378
  653.7 21.7 %collective-permute-done.74 = bf16[4,144,1152]{2,1,0:T(8,128)(2,1)S(1)} collective-permute-done((bf16[4,144,1152]{2,1,0:T(8,128)(2,1)S(1)}, bf16[4,144,1152]{2,1,0:T(8,128)(2,1)S(1)}, u32[]{:S(2)}, u32[]{:S(2)}) %collective-permute-start.74) | collective-permute-done | bytes 1327136 | tf_op jit(solution)/shard_map/ppermute | solution.py:378
  696.0 22.7 %collective-permute-done.59 = bf16[4,144,1152]{2,1,0:T(8,128)(2,1)S(1)} collective-permute-done((bf16[4,144,1152]{2,1,0:T(8,128)(2,1)S(1)}, bf16[4,144,1152]{2,1,0:T(8,128)(2,1)S(1)}, u32[]{:S(2)}, u32[]{:S(2)}) %collective-permute-start.59) | collective-permute-done | bytes 1327136 | tf_op jit(solution)/shard_map/ppermute | solution.py:378
  744.2 17.0 %collective-permute-done.62 = bf16[4,144,1152]{2,1,0:T(8,128)(2,1)S(1)} collective-permute-done((bf16[4,144,1152]{2,1,0:T(8,128)(2,1)S(1)}, bf16[4,144,1152]{2,1,0:T(8,128)(2,1)S(1)}, u32[]{:S(2)}, u32[]{:S(2)}) %collective-permute-start.62) | collective-permute-done | bytes 1327136 | tf_op jit(solution)/shard_map/ppermute | solution.py:378
  795.4 16.3 %all-to-all-done.5 = bf16[4,2,36864]{2,1,0:T(2,128)(2,1)S(1)} async-done(((bf16[4,2,36864]{2,1,0:T(2,128)(2,1)}), bf16[4,2,36864]{2,1,0:T(2,128)(2,1)S(1)}, u32[]{:S(2)}, u32[]{:S(2)}) %all-to-all-start.5) | async-done | bytes 589856 | tf_op jit(solution)/shard_map/all_to_all | solution.py:863
  826.9 15.9 %reduce-scatter.11.cloned.1.call-done = bf16[1,144,1152]{2,1,0:T(8,128)(2,1)} async-done(((bf16[4,144,1152]{2,1,0:T(8,128)(2,1)}), bf16[1,144,1152]{2,1,0:T(8,128)(2,1)}) %reduce-scatter.11.cloned.1.call-update) | async-done | bytes 331792 | tf_op jit(solution)/shard_map/reduce_scatter | solution.py:408
  (517 shorter events, 444.1 us)
Async XLA Ops:
  10.6 79.1 %all-gather.16.cloned.1.call-start = ((), (), s32[]{:S(2)}) async-start(), calls=%async_computation.19 | async-start | bytes 1658880 | tf_op jit(solution)/shard_map/all_gather | solution.py:394
  11.5 104.6 %all-gather.18.cloned.1.call-start = ((), (), s32[]{:S(2)}) async-start(), calls=%async_computation.20 | async-start | bytes 1658880 | tf_op jit(solution)/shard_map/all_gather | solution.py:394
  12.3 174.7 %all-gather.20.cloned.1.call-start = ((), (), s32[]{:S(2)}) async-start(), calls=%async_computation.21 | async-start | bytes 1658880 | tf_op jit(solution)/shard_map/all_gather | solution.py:394
  14.1 227.6 %all-gather.22.cloned.1.call-start = ((), (), s32[]{:S(2)}) async-start(), calls=%async_computation.22 | async-start | bytes 1658880 | tf_op jit(solution)/shard_map/all_gather | solution.py:394
  47.9 68.2 %collective-permute-start.6 = (bf16[4,144,1152]{2,1,0:T(8,128)(2,1)}, bf16[4,144,1152]{2,1,0:T(8,128)(2,1)}, u32[]{:S(2)}, u32[]{:S(2)}) collective-permute-start(bf16[4,144,1152]{2,1,0:T(8,128)(2,1)} %bitcast.230), channel_id=1, source_target_pairs={{0,16},{4,12},{8,24},{12,4},{16,0},{20,28},{24,8},{28,20},{1,17},{... | collective-permute-start | bytes 3981320 | tf_op jit(solution)/shard_map/ppermute | solution.py:378
  51.4 67.0 %collective-permute-start.8 = (bf16[4,144,1152]{2,1,0:T(8,128)(2,1)}, bf16[4,144,1152]{2,1,0:T(8,128)(2,1)}, u32[]{:S(2)}, u32[]{:S(2)}) collective-permute-start(bf16[4,144,1152]{2,1,0:T(8,128)(2,1)} %bitcast.231), channel_id=1, source_target_pairs={{0,4},{4,0},{8,12},{12,8},{16,20},{20,16},{24,28},{28,24},{1,5},{5... | collective-permute-start | bytes 3981320 | tf_op jit(solution)/shard_map/ppermute | solution.py:378
  122.0 65.1 %collective-permute-start.20 = (bf16[4,144,1152]{2,1,0:T(8,128)(2,1)}, bf16[4,144,1152]{2,1,0:T(8,128)(2,1)}, u32[]{:S(2)}, u32[]{:S(2)}) collective-permute-start(bf16[4,144,1152]{2,1,0:T(8,128)(2,1)} %bitcast.22.refs_0_), channel_id=1, source_target_pairs={{0,16},{4,12},{8,24},{12,4},{16,0},{20,28},{24,8},{28,20},{1,17},{... | collective-permute-start | bytes 3981320 | tf_op jit(solution)/shard_map/ppermute | solution.py:378
  122.7 66.5 %collective-permute-start.22 = (bf16[4,144,1152]{2,1,0:T(8,128)(2,1)}, bf16[4,144,1152]{2,1,0:T(8,128)(2,1)}, u32[]{:S(2)}, u32[]{:S(2)}) collective-permute-start(bf16[4,144,1152]{2,1,0:T(8,128)(2,1)} %bitcast.22.refs_0_), channel_id=1, source_target_pairs={{0,4},{4,0},{8,12},{12,8},{16,20},{20,16},{24,28},{28,24},{1,5},{5... | collective-permute-start | bytes 3981320 | tf_op jit(solution)/shard_map/ppermute | solution.py:378
  122.7 66.5 %collective-permute-start.9 = (bf16[4,144,1152]{2,1,0:T(8,128)(2,1)S(1)}, bf16[4,144,1152]{2,1,0:T(8,128)(2,1)}, u32[]{:S(2)}, u32[]{:S(2)}) collective-permute-start(bf16[4,144,1152]{2,1,0:T(8,128)(2,1)S(1)} %collective-permute-done.5.refs_1_), channel_id=1, source_target_pairs={{0,4},{4,0},{8,12},{12,8},{16,20},{20,16},{24,28},{28,24},{1,5},{5... | collective-permute-start | bytes 3981320 | tf_op jit(solution)/shard_map/ppermute | solution.py:378
  154.0 125.4 %all-gather.24.cloned.1.call-start = ((), (), s32[]{:S(2)}) async-start(), calls=%async_computation.23 | async-start | bytes 1658880 | tf_op jit(solution)/shard_map/all_gather | solution.py:394
  182.6 92.4 %all-to-all-start.3 = ((bf16[1,4,64,1152]{3,1,0,2:T(4,128)(2,1)}), bf16[1,4,64,1152]{3,1,0,2:T(4,128)(2,1)}, u32[]{:S(2)}, u32[]{:S(2)}) async-start(bf16[1,4,64,1152]{3,1,0,2:T(4,128)(2,1)} %copy.71), calls=%async_computation.3 | async-start | bytes 1179648 | tf_op jit(solution)/shard_map/all_to_all | solution.py:841
  243.5 71.1 %collective-permute-start.28 = (bf16[4,144,1152]{2,1,0:T(8,128)(2,1)}, bf16[4,144,1152]{2,1,0:T(8,128)(2,1)}, u32[]{:S(2)}, u32[]{:S(2)}) collective-permute-start(bf16[4,144,1152]{2,1,0:T(8,128)(2,1)} %collective-permute-done.26.refs_1_), channel_id=1, source_target_pairs={{0,16},{4,12},{8,24},{12,4},{16,0},{20,28},{24,8},{28,20},{1,17},{... | collective-permute-start | bytes 3981320 | tf_op jit(solution)/shard_map/ppermute | solution.py:378
  461.0 352.4 %reduce-scatter.13.cloned.1.call-start = ((), (), s32[]{:S(2)}) async-start(), calls=%async_computation.15 | async-start | bytes 1658880 | tf_op jit(solution)/shard_map/reduce_scatter | solution.py:408
  470.1 76.1 %collective-permute-start.69 = (bf16[4,4,144,1152]{3,2,1,0:T(8,128)(2,1)}, bf16[4,4,144,1152]{3,2,1,0:T(8,128)(2,1)}, u32[]{:S(2)}, u32[]{:S(2)}) collective-permute-start(bf16[4,4,144,1152]{3,2,1,0:T(8,128)(2,1)} %get-tuple-element.42), channel_id=1, source_target_pairs={{0,4},{4,0},{8,12},{12,8},{16,20},{20,16},{24,28},{28,24},{1,5},{5... | collective-permute-start | bytes 15925256 | tf_op jit(solution)/shard_map/ppermute | solution.py:378
  477.9 87.0 %collective-permute-start.72 = (bf16[4,4,144,1152]{3,2,1,0:T(8,128)(2,1)}, bf16[4,4,144,1152]{3,2,1,0:T(8,128)(2,1)}, u32[]{:S(2)}, u32[]{:S(2)}) collective-permute-start(bf16[4,4,144,1152]{3,2,1,0:T(8,128)(2,1)} %get-tuple-element.44), channel_id=1, source_target_pairs={{0,4},{4,0},{8,12},{12,8},{16,20},{20,16},{24,28},{28,24},{1,5},{5... | collective-permute-start | bytes 15925256 | tf_op jit(solution)/shard_map/ppermute | solution.py:378
  564.9 83.6 %collective-permute-start.60 = (bf16[4,4,144,1152]{3,2,1,0:T(8,128)(2,1)}, bf16[4,4,144,1152]{3,2,1,0:T(8,128)(2,1)}, u32[]{:S(2)}, u32[]{:S(2)}) collective-permute-start(bf16[4,4,144,1152]{3,2,1,0:T(8,128)(2,1)} %get-tuple-element.36), channel_id=1, source_target_pairs={{0,4},{4,0},{8,12},{12,8},{16,20},{20,16},{24,28},{28,24},{1,5},{5... | collective-permute-start | bytes 15925256 | tf_op jit(solution)/shard_map/ppermute | solution.py:378
  591.8 225.6 %reduce-scatter.15.cloned.1.call-start = ((), (), s32[]{:S(2)}) async-start(), calls=%async_computation.16 | async-start | bytes 1658880 | tf_op jit(solution)/shard_map/reduce_scatter | solution.py:408
  609.4 81.6 %collective-permute-start.63 = (bf16[4,4,144,1152]{3,2,1,0:T(8,128)(2,1)}, bf16[4,4,144,1152]{3,2,1,0:T(8,128)(2,1)}, u32[]{:S(2)}, u32[]{:S(2)}) collective-permute-start(bf16[4,4,144,1152]{3,2,1,0:T(8,128)(2,1)} %get-tuple-element.38), channel_id=1, source_target_pairs={{0,4},{4,0},{8,12},{12,8},{16,20},{20,16},{24,28},{28,24},{1,5},{5... | collective-permute-start | bytes 15925256 | tf_op jit(solution)/shard_map/ppermute | solution.py:378
  644.9 92.0 %all-to-all-start.2 = ((bf16[1,16,16,1152]{3,2,0,1:T(8,128)(2,1)}), bf16[1,16,16,1152]{3,2,0,1:T(8,128)(2,1)S(1)}, u32[]{:S(2)}, u32[]{:S(2)}) async-start(bf16[1,16,16,1152]{3,2,0,1:T(8,128)(2,1)} %bitcast.33), calls=%async_computation.2 | async-start | bytes 1179648 | tf_op jit(solution)/shard_map/all_to_all | solution.py:853
  648.3 170.9 %reduce-scatter.17.cloned.1.call-start = ((), (), s32[]{:S(2)}) async-start(), calls=%async_computation.17 | async-start | bytes 1658880 | tf_op jit(solution)/shard_map/reduce_scatter | solution.py:408
  653.3 73.2 %collective-permute-start.61 = (bf16[2,4,144,1152]{3,2,1,0:T(8,128)(2,1)}, bf16[2,4,144,1152]{3,2,1,0:T(8,128)(2,1)}, u32[]{:S(2)}, u32[]{:S(2)}) collective-permute-start(bf16[2,4,144,1152]{3,2,1,0:T(8,128)(2,1)} %add_convert_fusion.4), channel_id=1, source_target_pairs={{0,16},{4,12},{8,24},{12,4},{16,0},{20,28},{24,8},{28,20},{1,17},{... | collective-permute-start | bytes 7962632 | tf_op jit(solution)/shard_map/ppermute | solution.py:378
  679.2 141.9 %reduce-scatter.7.cloned.1.call-start = ((), (), s32[]{:S(2)}) async-start(), calls=%async_computation.12 | async-start | bytes 1658880 | tf_op jit(solution)/shard_map/reduce_scatter | solution.py:408
  695.7 73.4 %collective-permute-start.64 = (bf16[2,4,144,1152]{3,2,1,0:T(8,128)(2,1)}, bf16[2,4,144,1152]{3,2,1,0:T(8,128)(2,1)}, u32[]{:S(2)}, u32[]{:S(2)}) collective-permute-start(bf16[2,4,144,1152]{3,2,1,0:T(8,128)(2,1)} %add_convert_fusion.3), channel_id=1, source_target_pairs={{0,16},{4,12},{8,24},{12,4},{16,0},{20,28},{24,8},{28,20},{1,17},{... | collective-permute-start | bytes 7962632 | tf_op jit(solution)/shard_map/ppermute | solution.py:378
  722.7 102.4 %reduce-scatter.9.cloned.1.call-start = ((), (), s32[]{:S(2)}) async-start(), calls=%async_computation.13 | async-start | bytes 1658880 | tf_op jit(solution)/shard_map/reduce_scatter | solution.py:408
  (142 other events, 2780.8 us)
Sparse Core Ops, SparseCore 0:
  10.8 35.6 all-gather.13
  48.6 31.9 all-gather.15
  82.7 33.3 all-gather.17
  118.1 31.8 all-gather.19
  152.0 40.5 all-gather.21
  194.6 31.1 all-gather.23
  591.9 31.8 reduce-scatter.12
  638.1 31.4 reduce-scatter.14
  679.3 31.8 reduce-scatter.16
  722.8 32.2 reduce-scatter.6
  765.2 42.0 reduce-scatter.8
  809.4 33.3 reduce-scatter.10

commit v2 on v1

--- a/solution.py
+++ b/solution.py
@@ -350,20 +350,6 @@
     return lax.ppermute(array, axis, [(i, i ^ bit) for i in range(count)])
 
 
-def exchange_sum(array, axis):
-    bit = 1
-    while bit < lax.axis_size(axis):
-        array = array + flip(array, axis, bit)
-        bit *= 2
-    return array
-
-
-def place_along(array, axis):
-    count = lax.axis_size(axis)
-    own = (jnp.arange(count) == lax.axis_index(axis)).reshape((count,) + (1,) * array.ndim)
-    return exchange_sum(jnp.where(own, array[None], 0.0), axis)
-
-
 def first_flip(shard):
     return 2 if shard % 2 == 0 else 4
 
@@ -378,6 +364,48 @@
     return lax.ppermute(array, SHARDS, pairs)
 
 
+class Line:
+    def __init__(self):
+        self.last = ()
+        self.awaited = []
+        self.under_way = []
+
+    def held(self, value):
+        return lax.optimization_barrier((value, self.last, self.awaited))[0]
+
+    def __call__(self, work, *inputs):
+        self.last = work(*self.held(inputs))
+        self.awaited = []
+        return self.last
+
+    def wait(self, value):
+        self.awaited.append(value)
+        return value
+
+    def send(self, array, move):
+        self.under_way.append(move(self.held(array)))
+        return self.under_way[-1]
+
+    def hop(self, array, which):
+        return self.send(array, lambda held: hop(held, which))
+
+    def exchange_sum(self, array, axis):
+        bit = 1
+        while bit < lax.axis_size(axis):
+            array = self(jnp.add, array, flip(array, axis, bit))
+            bit *= 2
+        return array
+
+    def place_along(self, array, axis):
+        count = lax.axis_size(axis)
+        own = (jnp.arange(count) == lax.axis_index(axis)).reshape((count,) + (1,) * array.ndim)
+        return self.exchange_sum(jnp.where(own, array[None], 0.0), axis)
+
+    def tick(self):
+        self.awaited += self.under_way
+        self.under_way = []
+
+
 def shard_index():
     return lax.axis_index(CLIP) * lax.axis_size(FRAME) + lax.axis_index(FRAME)
 
@@ -390,22 +418,56 @@
     return jnp.stack([shard ^ mask for mask in masks]).astype(jnp.int32)
 
 
-def gather_piece(piece):
-    own = lax.all_gather(piece, TENSOR, axis=0, tiled=False)
-    near = hop(own, 1)
-    mine = (own, near, hop(own, 2), hop(near, 2))
-    return mine + tuple(hop(array, 0) for array in mine)
-
-
-def scatter_piece(grad):
-    keep, send = grad
-    got = hop(send, 0)
-    wide = lambda array: array.astype(jnp.float32)
-    low = lambda array: array.astype(jnp.bfloat16)
-    far = hop(low(wide(keep[2:]) + wide(got[2:])), 2)
-    near = hop(low(wide(keep[1]) + wide(got[1]) + wide(far[1])), 1)
-    own = low(wide(keep[0]) + wide(got[0]) + wide(far[0]) + wide(near))
-    return lax.psum_scatter(own, TENSOR, scatter_dimension=0, tiled=False)
+class Gather:
+    def __init__(self, line, piece):
+        self.line = line
+        self.whole = lax.all_gather(piece, TENSOR, axis=0, tiled=False)
+
+    def soon(self):
+        self.line.under_way.append(self.whole)
+
+    def send(self):
+        self.line.wait(self.whole)
+        self.near = self.line.hop(self.whole, 1)
+
+    def relay(self):
+        self.pair = self.line(lambda *pair: jnp.stack(pair), self.whole, self.near)
+        self.far = self.line.hop(self.pair, 2)
+        self.other_pair = self.line.hop(self.pair, 0)
+
+    def end(self):
+        other_far = self.line.hop(self.far, 0)
+        self.pieces = (self.pair, self.far, self.other_pair, other_far)
+
+
+def wide(array):
+    return array.astype(jnp.float32)
+
+
+def low(array):
+    return array.astype(jnp.bfloat16)
+
+
+def total(*arrays):
+    return low(sum(wide(array) for array in arrays))
+
+
+class Scatter:
+    def __init__(self, line, grad):
+        self.line = line
+        self.keep, self.away = grad
+
+    def send(self):
+        self.far = self.line.hop(self.away, 2)
+
+    def relay(self):
+        work = lambda keep, far: total(keep[1], far[1])
+        self.near = self.line.hop(self.line(work, self.keep, self.far), 1)
+
+    def finish(self):
+        work = lambda keep, far, near: total(keep[0], far[0], near)
+        own = self.line(work, self.keep, self.far, self.near)
+        self.piece = lax.psum_scatter(own, TENSOR, scatter_dimension=0, tiled=False)
 
 
 def pack_layer(weights):
@@ -416,7 +478,9 @@
 
 
 PIECES = 8
+PAIRS = 4
 VMEM_BYTES = 48 << 20
+COST_SHARE = 8
 
 
 def contract(left, right, left_dim, right_dim):
@@ -426,37 +490,37 @@
 
 
 def assemble(order_ref, piece_refs, whole_ref):
-    rows = piece_refs[0].shape[1]
+    rows = piece_refs[0].shape[2]
     for j in range(PIECES):
         start = pl.multiple_of(order_ref[j] * rows, 16)
-        whole_ref[pl.ds(start, rows), :] = piece_refs[j][0]
+        whole_ref[pl.ds(start, rows), :] = piece_refs[j // 2][j % 2, 0]
 
 
 def up_kernel(order_ref, x_ref, *refs):
-    pre_ref, act_ref, whole_ref = refs[PIECES:]
-    assemble(order_ref, refs[:PIECES], whole_ref)
+    pre_ref, act_ref, whole_ref = refs[PAIRS:]
+    assemble(order_ref, refs[:PAIRS], whole_ref)
     pre = contract(x_ref[...], whole_ref[...], 1, 0)
     pre_ref[...] = pre
     act_ref[...] = gelu_tanh(pre).astype(jnp.bfloat16)
 
 
 def slope_kernel(order_ref, x_ref, pre_ref, *refs):
-    out_ref, whole_ref = refs[PIECES:]
-    assemble(order_ref, refs[:PIECES], whole_ref)
+    out_ref, whole_ref = refs[PAIRS:]
+    assemble(order_ref, refs[:PAIRS], whole_ref)
     d_act = contract(x_ref[...], whole_ref[...], 1, 0)
     out_ref[...] = (d_act * gelu_slope(pre_ref[...])).astype(jnp.bfloat16)
 
 
 def turned_kernel(low, high, order_ref, x_ref, *refs):
-    out_ref, whole_ref = refs[PIECES:]
-    assemble(order_ref, refs[:PIECES], whole_ref)
+    out_ref, whole_ref = refs[PAIRS:]
+    assemble(order_ref, refs[:PAIRS], whole_ref)
     whole = contract(x_ref[...], whole_ref[...], 1, 0)
     out_ref[0] = whole[:, low:high].astype(jnp.bfloat16).T
 
 
 def collect_kernel(low, high, turned, order_ref, y_ref, *refs):
-    out_ref, whole_ref = refs[PIECES:]
-    assemble(order_ref, refs[:PIECES], whole_ref)
+    out_ref, whole_ref = refs[PAIRS:]
+    assemble(order_ref, refs[:PAIRS], whole_ref)
     rows = y_ref[0].T if turned else y_ref[...]
     term = contract(rows, whole_ref[:, low:high], 1, 1)
 
@@ -469,24 +533,54 @@
         out_ref[...] += term
 
 
-def deal_out(order_ref, whole_ref, keep_ref, send_ref):
-    rows = keep_ref.shape[2]
-    for j in range(PIECES):
-        start = pl.multiple_of(order_ref[j] * rows, 16)
-        to_ref = keep_ref if j < PIECES // 2 else send_ref
-        to_ref[j % (PIECES // 2), 0] = whole_ref[pl.ds(start, rows), :]
-
-
-def grad_kernel(order_ref, x_ref, y_ref, keep_ref, send_ref, whole_ref):
-    whole_ref[...] = contract(x_ref[...], y_ref[...], 0, 0).astype(jnp.bfloat16)
-    deal_out(order_ref, whole_ref, keep_ref, send_ref)
-
-
-def attn_grad_kernel(order_ref, x_ref, y_ref, b_ref, a_ref, keep_ref, send_ref, whole_ref):
-    split = y_ref.shape[1]
-    whole_ref[:, :split] = contract(x_ref[...], y_ref[0].T, 0, 0).astype(jnp.bfloat16)
-    whole_ref[:, split:] = contract(b_ref[...], a_ref[0].T, 0, 0).astype(jnp.bfloat16)
-    deal_out(order_ref, whole_ref, keep_ref, send_ref)
+def turn(order_ref, x_refs, whole_ref, turned_ref):
+    rows, tokens = turned_ref.shape[0] * 2 // PIECES, turned_ref.shape[1] // 2
+    for side in range(2):
+        whole_ref[...] = x_refs[side][...].T
+        for j in range(PIECES // 2):
+            start = pl.multiple_of(order_ref[j] * rows, 16)
+            turned_ref[pl.ds(j * rows, rows), pl.ds(side * tokens, tokens)] = whole_ref[
+                pl.ds(start, rows), :
+            ]
+
+
+def deal_out(grad, *out_refs):
+    rows = out_refs[0].shape[2]
+    for j in range(PIECES // 2):
+        out_refs[j // 2][j % 2, 0] = grad[j * rows : (j + 1) * rows]
+
+
+def grad_kernel(order_ref, x_ref, x_other, y_ref, y_other, *refs):
+    whole_ref, turned_ref = refs[2:]
+
+    @pl.when(pl.program_id(0) == 0)
+    def _():
+        turn(order_ref, (x_ref, x_other), whole_ref, turned_ref)
+
+    tokens = x_ref.shape[0]
+    grad = contract(turned_ref[:, :tokens], y_ref[...], 1, 0)
+    grad += contract(turned_ref[:, tokens:], y_other[...], 1, 0)
+    deal_out(grad.astype(jnp.bfloat16), *refs[:2])
+
+
+def attn_grad_kernel(order_ref, *refs):
+    x_refs, b_refs, y_refs, a_refs = (refs[2 * j : 2 * j + 2] for j in range(4))
+    out_refs, (whole_ref, x_turned, b_turned, grad_ref) = refs[8:10], refs[10:]
+
+    @pl.when(pl.program_id(0) == 0)
+    def _():
+        turn(order_ref, x_refs, whole_ref, x_turned)
+        turn(order_ref, b_refs, whole_ref, b_turned)
+
+    tokens, split = y_refs[0].shape[2], y_refs[0].shape[1]
+    for turned, pair, lanes in (
+        (x_turned, y_refs, slice(0, split)),
+        (b_turned, a_refs, slice(split, grad_ref.shape[1])),
+    ):
+        grad = contract(turned[:, :tokens], pair[0][0], 1, 1)
+        grad += contract(turned[:, tokens:], pair[1][0], 1, 1)
+        grad_ref[:, lanes] = grad.astype(jnp.bfloat16)
+    deal_out(grad_ref[...], *out_refs)
 
 
 def masked_scores(queries, keys, group):
@@ -544,7 +638,9 @@
             scratch_shapes=scratch,
         ),
         compiler_params=pltpu.CompilerParams(vmem_limit_bytes=VMEM_BYTES),
-        cost_estimate=pl.CostEstimate(flops=flops, bytes_accessed=moved, transcendentals=0),
+        cost_estimate=pl.CostEstimate(
+            flops=flops // COST_SHARE, bytes_accessed=moved // COST_SHARE, transcendentals=0
+        ),
     )(*args)
 
 
@@ -561,7 +657,12 @@
 
 
 def sizes(pieces):
-    return pieces[0].shape + (pieces[0].shape[1] * PIECES,)
+    _, groups, rows, width = pieces[0].shape
+    return groups, rows, width, rows * PIECES
+
+
+def pair_specs(rows, width, count):
+    return [pl.BlockSpec((2, 1, rows, width), lambda z, *_: (0, z, 0, 0))] * count
 
 
 def times_up(order, x, pieces):
@@ -571,7 +672,7 @@
     return call(
         up_kernel,
         (groups,),
-        [still(x.shape)] + [lead((rows, width))] * PIECES,
+        [still(x.shape)] + pair_specs(rows, width, PAIRS),
         [column(tokens, width)] * 2,
         [jax.ShapeDtypeStruct(shape, jnp.float32), jax.ShapeDtypeStruct(shape, jnp.bfloat16)],
         [pltpu.VMEM((depth, width), jnp.bfloat16)],
@@ -586,7 +687,7 @@
     return call(
         slope_kernel,
         (groups,),
-        [still(x.shape), column(tokens, width)] + [lead((rows, width))] * PIECES,
+        [still(x.shape), column(tokens, width)] + pair_specs(rows, width, PAIRS),
         column(tokens, width),
         jax.ShapeDtypeStruct(pre.shape, jnp.bfloat16),
         [pltpu.VMEM((depth, width), jnp.bfloat16)],
@@ -601,7 +702,7 @@
     return call(
         functools.partial(turned_kernel, low, high),
         (groups,),
-        [still(x.shape)] + [lead((rows, width))] * PIECES,
+        [still(x.shape)] + pair_specs(rows, width, PAIRS),
         lead((high - low, tokens)),
         jax.ShapeDtypeStruct((groups, high - low, tokens), jnp.bfloat16),
         [pltpu.VMEM((depth, width), jnp.bfloat16)],
@@ -617,7 +718,7 @@
         functools.partial(collect_kernel, low, high, turned),
         (groups,),
         [lead(y.shape[1:]) if turned else column(tokens, width)]
-        + [lead((rows, width))] * PIECES,
+        + pair_specs(rows, width, PAIRS),
         still((tokens, depth)),
         jax.ShapeDtypeStruct((tokens, depth), jnp.float32),
         [pltpu.VMEM((depth, width), jnp.bfloat16)],
@@ -626,34 +727,40 @@
     )
 
 
-def grad_call(kernel, args, specs, groups, depth, width):
+def grad_call(kernel, args, specs, groups, depth, width, scratch):
     rows = depth // PIECES
-    half = PIECES // 2
     tokens = args[1].shape[0]
     return call(
         kernel,
         (groups,),
         specs,
-        [pl.BlockSpec((half, 1, rows, width), lambda z, *_: (0, z, 0, 0))] * 2,
-        [jax.ShapeDtypeStruct((half, groups, rows, width), jnp.bfloat16)] * 2,
-        [pltpu.VMEM((depth, width), jnp.bfloat16)],
+        pair_specs(rows, width, 2),
+        [jax.ShapeDtypeStruct((2, groups, rows, width), jnp.bfloat16)] * 2,
+        [pltpu.VMEM((depth, tokens), jnp.bfloat16)]
+        + [pltpu.VMEM(shape, jnp.bfloat16) for shape in scratch],
         2 * tokens * depth * width * groups,
         args,
     )
 
 
-def grad_of(order, x, y, groups):
+def grad_of(order, x, x_other, y, y_other, groups):
     tokens, width = x.shape[0], y.shape[1] // groups
-    specs = [still(x.shape), column(tokens, width)]
-    return grad_call(grad_kernel, (order, x, y), specs, groups, x.shape[1], width)
-
-
-def attn_grad_of(order, x, y, b, a):
-    groups, wide, tokens = y.shape
-    part = a.shape[1]
-    specs = [still(x.shape), lead((wide, tokens)), still(b.shape), lead((part, tokens))]
-    args = (order, x, y, b, a)
-    return grad_call(attn_grad_kernel, args, specs, groups, x.shape[1], wide + part)
+    depth = x.shape[1]
+    specs = [still(x.shape)] * 2 + [column(tokens, width)] * 2
+    args = (order, x, x_other, y, y_other)
+    scratch = [(depth // 2, 2 * tokens)]
+    return grad_call(grad_kernel, args, specs, groups, depth, width, scratch)
+
+
+def attn_grad_of(order, *args):
+    x, y, a = args[0], args[4], args[6]
+    groups, wide_part, tokens = y.shape
+    part, depth = a.shape[1], x.shape[1]
+    specs = [still(x.shape)] * 4 + [lead((wide_part, tokens))] * 2 + [lead((part, tokens))] * 2
+    scratch = [(depth // 2, 2 * tokens)] * 2 + [(depth // 2, wide_part + part)]
+    return grad_call(
+        attn_grad_kernel, (order, *args), specs, groups, depth, wide_part + part, scratch
+    )
 
 
 def attend_call(projected, group):
@@ -686,79 +793,142 @@
     )
 
 
-def own_forward(stream, modulation, order, weights, group):
-    attn, up, down = weights
-    width = attn[0].shape[2]
-    part = width // 4
-    normed, inv_scale = layer_norm(stream)
-    modulated = (normed * (1.0 + modulation[1]) + modulation[0]).astype(jnp.bfloat16)
-    projected = times_turned(order, modulated, attn, 0, 3 * part)
-    attended = attend_call(projected, group)
-    branch_attn = collect(order, attended, attn, 3 * part, width, True)
-    middle = stream + modulation[2] * branch_attn
-    normed_mlp, inv_mlp = layer_norm(middle)
-    modulated_mlp = (normed_mlp * (1.0 + modulation[4]) + modulation[3]).astype(jnp.bfloat16)
-    hidden_pre, hidden_act = times_up(order, modulated_mlp, up)
-    branch_mlp = collect(order, hidden_act, down, 0, width, False)
-    result = middle + modulation[5] * branch_mlp
-    stored = (
-        normed,
-        inv_scale,
-        modulated,
-        projected,
-        attended,
-        branch_attn,
-        normed_mlp,
-        inv_mlp,
-        modulated_mlp,
-        hidden_pre,
-        hidden_act,
-        branch_mlp,
-    )
-    return result, stored
-
-
-def own_backward(upstream, modulation, order, weights, stored, group):
-    attn, up, down = weights
-    width = attn[0].shape[2]
-    part = width // 4
-    groups = attn[0].shape[0]
-    (
-        normed,
-        inv_scale,
-        modulated,
-        projected,
-        attended,
-        branch_attn,
-        normed_mlp,
-        inv_mlp,
-        modulated_mlp,
-        hidden_pre,
-        hidden_act,
-        branch_mlp,
-    ) = stored
-    d_branch_mlp = (upstream * modulation[5]).astype(jnp.bfloat16)
-    d_gate_mlp = jnp.sum(upstream * branch_mlp, axis=0)
-    grad_down = grad_of(order, d_branch_mlp, hidden_act, groups)
-    d_pre = times_slope(order, d_branch_mlp, hidden_pre, down)
-    grad_up = grad_of(order, modulated_mlp, d_pre, groups)
-    d_mod_mlp = collect(order, d_pre, up, 0, width, False)
-    d_shift_mlp = jnp.sum(d_mod_mlp, axis=0)
-    d_scale_mlp = jnp.sum(d_mod_mlp * normed_mlp, axis=0)
-    d_middle = upstream + norm_back(normed_mlp, inv_mlp, d_mod_mlp * (1.0 + modulation[4]))
-    d_branch_attn = (d_middle * modulation[2]).astype(jnp.bfloat16)
-    d_gate_attn = jnp.sum(d_middle * branch_attn, axis=0)
-    d_attended = times_turned(order, d_branch_attn, attn, 3 * part, width)
-    d_projected = attend_back_call(projected, d_attended, group)
-    grad_attn = attn_grad_of(order, modulated, d_projected, d_branch_attn, attended)
-    d_modulated = collect(order, d_projected, attn, 0, 3 * part, True)
-    d_shift_attn = jnp.sum(d_modulated, axis=0)
-    d_scale_attn = jnp.sum(d_modulated * normed, axis=0)
-    d_stream = d_middle + norm_back(normed, inv_scale, d_modulated * (1.0 + modulation[1]))
-    d_modulation = jnp.stack(
-        [d_shift_attn, d_scale_attn, d_gate_attn, d_shift_mlp, d_scale_mlp, d_gate_mlp]
-    )
-    return d_stream, d_modulation, (grad_attn, grad_up, grad_down)
+class Layer:
+    def __init__(self, line, order, modulation, group):
+        self.line = line
+        self.order = order
+        self.modulation = modulation
+        self.group = group
+        self.others = {}
+
+    def share(self, *arrays):
+        for array in arrays:
+            self.others[id(array)] = self.line.hop(array, 0)
+
+    def both(self, array):
+        return array, self.others[id(array)]
+
+    def project(self, stream, attn):
+        self.stream = stream
+        self.attn = attn
+        self.width = attn[0].shape[-1]
+        self.part = self.width // 4
+        rows = self.modulation
+
+        def work(stream, attn):
+            normed, inv_scale = layer_norm(stream)
+            modulated = low(normed * (1.0 + rows[1]) + rows[0])
+            projected = times_turned(self.order, modulated, attn, 0, 3 * self.part)
+            return normed, inv_scale, modulated, projected
+
+        made = self.line(work, stream, attn)
+        self.normed, self.inv_scale, self.modulated, self.projected = made
+
+    def attend(self):
+        self.attended = self.line(
+            lambda projected: attend_call(projected, self.group), self.projected
+        )
+
+    def attention_out(self):
+        rows = self.modulation
+
+        def work(attended, stream, attn):
+            branch_attn = collect(self.order, attended, attn, 3 * self.part, self.width, True)
+            middle = stream + rows[2] * branch_attn
+            normed_mlp, inv_mlp = layer_norm(middle)
+            modulated_mlp = low(normed_mlp * (1.0 + rows[4]) + rows[3])
+            return branch_attn, middle, normed_mlp, inv_mlp, modulated_mlp
+
+        made = self.line(work, self.attended, self.stream, self.attn)
+        self.branch_attn, self.middle, self.normed_mlp, self.inv_mlp, self.modulated_mlp = made
+
+    def mlp_up(self, up):
+        self.up = up
+        work = lambda rows, up: times_up(self.order, rows, up)
+        self.hidden_pre, self.hidden_act = self.line(work, self.modulated_mlp, up)
+
+    def mlp_down(self, down, last):
+        rows = self.modulation
+
+        def work(act, middle, down):
+            branch_mlp = collect(self.order, act, down, 0, self.width, False)
+            return branch_mlp, last(middle + rows[5] * branch_mlp)
+
+        self.branch_mlp, result = self.line(work, self.hidden_act, self.middle, down)
+        return result
+
+    def turn_back(self, upstream):
+        rows = self.modulation
+        self.upstream = upstream
+        self.d_branch_mlp = self.line(lambda rows_in: low(rows_in * rows[5]), upstream)
+
+    def gradient(self, *args):
+        groups = self.attn[0].shape[1]
+        work = lambda *rows: grad_of(self.order, *rows, groups)
+        return Scatter(self.line, self.line(work, *args))
+
+    def grad_down(self):
+        return self.gradient(*self.both(self.d_branch_mlp), *self.both(self.hidden_act))
+
+    def slope(self, down):
+        work = lambda rows, pre, down: times_slope(self.order, rows, pre, down)
+        self.d_pre = self.line(work, self.d_branch_mlp, self.hidden_pre, down)
+
+    def grad_up(self):
+        return self.gradient(*self.both(self.modulated_mlp), *self.both(self.d_pre))
+
+    def back_up(self):
+        rows = self.modulation
+
+        def work(d_pre, upstream, normed, inv_mlp, up):
+            d_mod_mlp = collect(self.order, d_pre, up, 0, self.width, False)
+            d_middle = upstream + norm_back(normed, inv_mlp, d_mod_mlp * (1.0 + rows[4]))
+            return d_mod_mlp, d_middle, low(d_middle * rows[2])
+
+        made = self.line(
+            work, self.d_pre, self.upstream, self.normed_mlp, self.inv_mlp, self.up
+        )
+        self.d_mod_mlp, self.d_middle, self.d_branch_attn = made
+
+    def back_out(self):
+        work = lambda rows, attn: times_turned(
+            self.order, rows, attn, 3 * self.part, self.width
+        )
+        self.d_attended = self.line(work, self.d_branch_attn, self.attn)
+
+    def back_attend(self):
+        work = lambda projected, upstream: attend_back_call(projected, upstream, self.group)
+        self.d_projected = self.line(work, self.projected, self.d_attended)
+
+    def grad_attn(self):
+        work = lambda *rows: attn_grad_of(self.order, *rows)
+        rows = (self.modulated, self.d_branch_attn, self.d_projected, self.attended)
+        grad = self.line(work, *(one for array in rows for one in self.both(array)))
+        return Scatter(self.line, grad)
+
+    def back_project(self, last):
+        rows = self.modulation
+
+        def work(d_projected, d_middle, normed, inv_scale, attn):
+            d_modulated = collect(self.order, d_projected, attn, 0, 3 * self.part, True)
+            back = norm_back(normed, inv_scale, d_modulated * (1.0 + rows[1]))
+            return d_modulated, last(d_middle + back)
+
+        self.d_modulated, result = self.line(
+            work, self.d_projected, self.d_middle, self.normed, self.inv_scale, self.attn
+        )
+        return result
+
+    def d_modulation(self):
+        terms = (
+            self.d_modulated,
+            self.d_modulated * self.normed,
+            self.d_middle * self.branch_attn,
+            self.d_mod_mlp,
+            self.d_mod_mlp * self.normed_mlp,
+            self.upstream * self.branch_mlp,
+        )
+        return jnp.stack([jnp.sum(term, axis=0) for term in terms])
 
 
 def finish_grads(attn_piece, up_piece, down_piece):
@@ -769,31 +939,12 @@
     return qkv, attn, up_piece.astype(jnp.float32), down_piece.T.astype(jnp.float32)
 
 
-def places_out(stream):
-    clips, frames, places, width = stream.shape
-    devices, tensors = lax.axis_size(FRAME), lax.axis_size(TENSOR)
-    part = places // (devices * tensors)
-    blocks = stream.reshape(clips, frames, tensors, devices, part, width).transpose(
-        0, 1, 3, 2, 4, 5
-    )
-    return lax.all_to_all(
-        blocks.reshape(clips, frames, places, width),
-        (FRAME, TENSOR),
-        split_axis=2,
-        concat_axis=1,
-        tiled=True,
-    )
-
-
-def places_back(stream):
-    devices, tensors = lax.axis_size(FRAME), lax.axis_size(TENSOR)
-    moved = lax.all_to_all(stream, (FRAME, TENSOR), split_axis=1, concat_axis=2, tiled=True)
-    clips, frames, places, width = moved.shape
-    part = places // (devices * tensors)
-    blocks = moved.reshape(clips, frames, devices, tensors, part, width).transpose(
-        0, 1, 3, 2, 4, 5
-    )
-    return blocks.reshape(clips, frames, places, width)
+def deal_rows(rows, axes):
+    return lax.all_to_all(rows, axes, split_axis=0, concat_axis=0, tiled=True)
+
+
+def swap_blocks(rows, outer, inner):
+    return rows.reshape(outer, inner, -1, rows.shape[1]).swapaxes(0, 1).reshape(rows.shape)
 
 
 def local_whole(
@@ -829,48 +980,135 @@
         ],
         axis=1,
     )
-    summed = exchange_sum(exchange_sum(partial_value, FRAME), CLIP)
+    devices, tensors = lax.axis_size(FRAME), lax.axis_size(TENSOR)
+    own_frames = x_in.shape[1]
+    own_places = x_in.shape[2] // devices
+    cotangent = deal_rows(swap_blocks(out_cotangent.reshape(-1, width), own_frames, devices), FRAME)
+    cotangent = swap_blocks(cotangent, devices, own_frames)
+    line = Line()
+    summed = line.exchange_sum(line.exchange_sum(partial_value, FRAME), CLIP)
+    line.wait(cotangent)
     summed = lax.dynamic_index_in_dim(summed, lax.axis_index(CLIP), 0, keepdims=False)
-    placed = place_along(summed, TENSOR)
+    placed = line.place_along(summed, TENSOR)
     modulations = placed.transpose(1, 2, 0, 3).reshape(summed.shape[:2] + (-1,))
 
     order = piece_order()
-    whole_weights = [[gather_piece(piece) for piece in pieces] for pieces in packed]
-
-    frames_in = lax.all_to_all(x_in, TENSOR, split_axis=1, concat_axis=2, tiled=True)
-    cotangent = lax.all_to_all(out_cotangent, FRAME, split_axis=2, concat_axis=1, tiled=True)
-    frame_shape, place_shape = frames_in.shape, cotangent.shape
-    group = place_shape[2]
-    wide = lambda array: array.reshape(-1, width).astype(jnp.float32)
-    low = lambda array, shape: array.astype(jnp.bfloat16).reshape(shape)
-    middle_stream, stored_first = own_forward(
-        wide(frames_in), modulations[0], order, whole_weights[0], 0
-    )
-    second_in = wide(places_out(low(middle_stream, frame_shape)))
-    result, stored_second = own_forward(
-        second_in, modulations[1], order, whole_weights[1], group
-    )
-    layer_out = lax.all_to_all(
-        low(result, place_shape), FRAME, split_axis=1, concat_axis=2, tiled=True
-    )
-    d_second, d_mod_second, grads_second = own_backward(
-        wide(cotangent), modulations[1], order, whole_weights[1], stored_second, group
-    )
-    d_first_out = wide(places_back(low(d_second, place_shape)))
-    d_first, d_mod_first, grads_first = own_backward(
-        d_first_out, modulations[0], order, whole_weights[0], stored_first, 0
-    )
-    input_grad = lax.all_to_all(
-        low(d_first, frame_shape), TENSOR, split_axis=2, concat_axis=1, tiled=True
-    ).astype(jnp.float32)
-
-    second_out = finish_grads(*(scatter_piece(grad) for grad in grads_second))
-    first_out = finish_grads(*(scatter_piece(grad) for grad in grads_first))
-
-    d_mods = jnp.stack([d_mod_first, d_mod_second])
-    d_mods = exchange_sum(exchange_sum(d_mods, FRAME), TENSOR)
+    attn_one, up_one, down_one = (Gather(line, piece) for piece in packed[0])
+    attn_two, up_two, down_two = (Gather(line, piece) for piece in packed[1])
+    one = Layer(line, order, modulations[0], 0)
+    two = Layer(line, order, modulations[1], own_places)
+
+    attn_one.send()
+    line.tick()
+    attn_one.relay()
+    frames_in = line.send(x_in.reshape(-1, width), lambda held: deal_rows(held, TENSOR))
+    up_one.send()
+    down_one.soon()
+    line.tick()
+    attn_one.end()
+    up_one.relay()
+    down_one.send()
+    one.project(line(wide, frames_in), attn_one.pieces)
+    one.attend()
+    one.attention_out()
+    attn_two.soon()
+    line.tick()
+    up_one.end()
+    down_one.relay()
+    attn_two.send()
+    one.mlp_up(up_one.pieces)
+    cotangent = line(wide, cotangent)
+    up_two.soon()
+    line.tick()
+    down_one.end()
+    attn_two.relay()
+    up_two.send()
+    down_two.soon()
+    between = one.mlp_down(down_one.pieces, low)
+    two.turn_back(cotangent)
+    line.tick()
+    attn_two.end()
+    up_two.relay()
+    down_two.send()
+    two.share(two.d_branch_mlp)
+    between = line(wide, line.send(between, lambda held: deal_rows(held, (TENSOR, FRAME))))
+    two.project(between, attn_two.pieces)
+    two.attend()
+    two.attention_out()
+    line.tick()
+    up_two.end()
+    down_two.relay()
+    two.mlp_up(up_two.pieces)
+    two.share(two.hidden_act)
+    down_grad = two.grad_down()
+    line.tick()
+    down_two.end()
+    down_grad.send()
+    two.share(two.modulated_mlp, two.modulated)
+    two.slope(down_two.pieces)
+    two.share(two.d_pre)
+    two.back_up()
+    up_grad = two.grad_up()
+    line.tick()
+    down_grad.relay()
+    up_grad.send()
+    two.share(two.d_branch_attn, two.attended)
+    two.back_out()
+    two.back_attend()
+    two.share(two.d_projected)
+    d_second = two.back_project(low)
+    attn_grad = two.grad_attn()
+    line.tick()
+    up_grad.relay()
+    attn_grad.send()
+    one.share(one.hidden_act, one.attended)
+    d_second = line(wide, deal_rows(d_second, (TENSOR, FRAME)))
+    down_grad.finish()
+    one.turn_back(d_second)
+    one.share(one.d_branch_mlp)
+    one.slope(down_one.pieces)
+    down_last = one.grad_down()
+    line.tick()
+    attn_grad.relay()
+    down_last.send()
+    one.share(one.d_pre, one.modulated_mlp, one.modulated)
+    up_grad.finish()
+    one.back_up()
+    up_last = one.grad_up()
+    one.back_out()
+    one.back_attend()
+    line.tick()
+    down_last.relay()
+    up_last.send()
+    one.share(one.d_branch_attn, one.d_projected)
+    attn_grad.finish()
+    d_first = one.back_project(low)
+    result = two.mlp_down(
+        down_two.pieces, lambda rows: swap_blocks(low(rows), own_frames, devices)
+    )
+    d_mods = line(lambda: jnp.stack([one.d_modulation(), two.d_modulation()]))
+    d_mods = line(jnp.add, d_mods, flip(d_mods, FRAME, 1))
+    attn_last = one.grad_attn()
+    d_mods = line(jnp.add, d_mods, flip(d_mods, TENSOR, 1))
+    near_mods = flip(d_mods, TENSOR, 2)
+    line.tick()
+    up_last.relay()
+    attn_last.send()
+    down_last.finish()
+    input_grad = deal_rows(d_first, TENSOR)
+    line.under_way.append(input_grad)
+    d_mods = line(jnp.add, d_mods, near_mods)
+    near_mods = line.send(d_mods, lambda held: flip(held, FRAME, 2))
+    line.tick()
+    attn_last.relay()
+    up_last.finish()
+    input_grad = line(wide, input_grad).reshape(x_in.shape)
+    layer_out = swap_blocks(deal_rows(result, FRAME), devices, own_frames).reshape(x_in.shape)
+    d_mods = line(jnp.add, d_mods, near_mods)
     d_mods = lax.dynamic_slice_in_dim(d_mods, lax.axis_index(TENSOR) * part, part, axis=2)
-    d_every = place_along(d_mods, CLIP)
+    d_every = line.place_along(d_mods, CLIP)
+    line.tick()
+    attn_last.finish()
     silu_float = silu_rows.astype(jnp.float32)
     grad_mods = [
         sum(
@@ -889,12 +1127,15 @@
             for c in range(clip_count)
         ]
     )
-    d_silu = place_along(place_along(exchange_sum(d_silu, TENSOR), FRAME), CLIP)
+    d_silu = line.exchange_sum(d_silu, TENSOR)
+    d_silu = line.place_along(line.place_along(d_silu, FRAME), CLIP)
     d_silu = d_silu.transpose(2, 0, 1, 3).reshape(clip_count, -1)
     d_silu = lax.dynamic_slice_in_dim(d_silu, lax.axis_index(CLIP), 1, axis=0)
     cond_float = cond.astype(jnp.float32)
     sigmoid_cond = jax.nn.sigmoid(cond_float)
     cond_grad = d_silu * (sigmoid_cond * (1.0 + cond_float * (1.0 - sigmoid_cond)))
+    first_out = finish_grads(attn_last.piece, up_last.piece, down_last.piece)
+    second_out = finish_grads(attn_grad.piece, up_grad.piece, down_grad.piece)
     return (
         layer_out,
         input_grad,

time: 852 us -> 756 us (0.89); the launches traced: 852 us -> 746 us
  waiting for transfers between devices: 370 us -> 302 us
  starting transfers between devices: 93.2 us -> 73.8 us
  local copies, waits for them, and re-layouts: 40.3 us -> 30.1 us
    ppermute x60 -> x52, waiting for transfers between devices: 224 us -> 125 us  [hop(): return lax.ppermute(array, SHARDS, pairs)]
    all_gather x6, waiting for transfers between devices: 45.5 us -> 83.6 us  [__init__(): self.whole = lax.all_gather(piece, TENSOR, axis=0, tiled=False)]
    all_to_all x6, waiting for transfers between devices: 38.3 us -> 16.4 us  [deal_rows(): return lax.all_to_all(rows, axes, split_axis=0, concat_axis=0, tiled=True)]
    convert_element_type x29 -> x26, other arithmetic: 71.7 us -> 53.5 us  [the longest x21 45.8 us: low(): return array.astype(jnp.bfloat16)]
    another operation x1 -> x7, other arithmetic: 0.01 us -> 17.9 us  [the longest x6 17.9 us: relay(): self.pair = self.line(lambda *pair: jnp.stack(pair), self.whole, self.near)]
    ppermute x60 -> x52, starting transfers between devices: 48.7 us -> 32.9 us  [hop(): return lax.ppermute(array, SHARDS, pairs)]
    ppermute x15, waiting for transfers between devices: 46.1 us -> 57 us  [flip(): return lax.ppermute(array, axis, [(i, i ^ bit) for i in range(count)])]
    unnamed x155 -> x162, local copies, waits for them, and re-layouts: 31 us -> 21.6 us
  transfers between devices with their start and end apart: 93 -> 85, of which waited for: 32 -> 35; matrix products, arithmetic and copies ran while one was open for 15% -> 16% of each run, Pallas kernels for 18% -> 27%
where the time goes in v2:
time: 756 us; the launch traced here: 746 us
  waiting for transfers between devices  302 us (40%)
  Pallas kernels  203 us (27%)
  other arithmetic  116 us (15%)
  starting transfers between devices  73.8 us (10%)
  local copies, waits for them, and re-layouts  30.1 us (4%)
  between operations  15.8 us (2%)
    pallas_call x26, Pallas kernels, call(): pl.pallas_call(kernel, out_shape=out_shape, grid_spec=pltpu.PrefetchScala...  203 us
    ppermute x52, waiting for transfers between devices, hop(): return lax.ppermute(array, SHARDS, pairs)  125 us
    all_gather x6, waiting for transfers between devices, __init__(): self.whole = lax.all_gather(piece, TENSOR, axis=0, tiled=False)  83.6 us
    ppermute x15, waiting for transfers between devices, flip(): return lax.ppermute(array, axis, [(i, i ^ bit) for i in range(count)])  57 us
    convert_element_type x21, other arithmetic, low(): return array.astype(jnp.bfloat16)  45.8 us
    ppermute x52, starting transfers between devices, hop(): return lax.ppermute(array, SHARDS, pairs)  32.9 us
    all_to_all x6, starting transfers between devices, deal_rows(): return lax.all_to_all(rows, axes, split_axis=0, concat_axis=0, tiled=True)  24.2 us
    unnamed x162, local copies, waits for them, and re-layouts  21.6 us
  transfers between devices with their start and end apart: 85, of which 35 were waited for; matrix products, arithmetic and copies ran while one was open for 16% of the time, Pallas kernels for 27%

profile of v2, /device:TPU:0, one launch (start us, length us, event | category | flops | bytes accessed | tf_op | source)
XLA Modules:
  0.0 746.3 jit_solution(5446215203147442381)
XLA Ops:
  41.3 10.0 %collective-permute-done.4 = f32[4,2,6,288]{3,2,1,0:T(8,128)S(1)} collective-permute-done((f32[4,2,6,288]{3,2,1,0:T(8,128)S(1)}, f32[4,2,6,288]{3,2,1,0:T(8,128)S(1)}, u32[]{:S(2)}, u32[]{:S(2)}) %collective-permute-start.4) | collective-permute-done | bytes 55328 | tf_op jit(solution)/shard_map/ppermute | solution.py:350
  54.3 15.7 %collective-permute-done.5 = bf16[4,144,1152]{2,1,0:T(8,128)(2,1)S(1)} collective-permute-done((bf16[4,144,1152]{2,1,0:T(8,128)(2,1)}, bf16[4,144,1152]{2,1,0:T(8,128)(2,1)S(1)}, u32[]{:S(2)}, u32[]{:S(2)}) %collective-permute-start.5) | collective-permute-done | bytes 1327136 | tf_op jit(solution)/shard_map/ppermute | solution.py:364
  75.5 9.6 %all-gather.16.cloned.1.call-done = bf16[576,1152]{1,0:T(8,128)(2,1)} async-done(((bf16[144,1152]{1,0:T(8,128)(2,1)}), bf16[576,1152]{1,0:T(8,128)(2,1)}) %all-gather.16.cloned.1.call-update) | async-done | bytes 1327120 | tf_op jit(solution)/shard_map/all_gather | solution.py:424
  90.1 36.9 %all-gather.18.cloned.1.call-done = bf16[576,1152]{1,0:T(8,128)(2,1)} async-done(((bf16[144,1152]{1,0:T(8,128)(2,1)}), bf16[576,1152]{1,0:T(8,128)(2,1)}) %all-gather.18.cloned.1.call-update) | async-done | bytes 1327120 | tf_op jit(solution)/shard_map/all_gather | solution.py:424
  172.2 12.5 %collective-permute-done.10.refs_1_ = bf16[2,4,144,1152]{3,2,1,0:T(8,128)(2,1)} collective-permute-done((bf16[2,4,144,1152]{3,2,1,0:T(8,128)(2,1)}, bf16[2,4,144,1152]{3,2,1,0:T(8,128)(2,1)}, u32[]{:S(2)}, u32[]{:S(2)}) %collective-permute-start.10) | collective-permute-done | bytes 2654240 | tf_op jit(solution)/shard_map/ppermute | solution.py:364
  193.0 10.1 %shard_map.231 = (f32[256,4608]{1,0:T(8,128)}, bf16[256,4608]{1,0:T(8,128)(2,1)}) custom-call(s32[8]{0:T(128)S(1)} %stack.154.order_ref, bf16[256,1152]{1,0:T(8,128)(2,1)S(1)} %copy-done.16, bf16[2,4,144,1152]{3,2,1,0:T(8,128)(2,1)} %pad_maximum_fusion.1.refs_0_, bf16[2,4,144,1152]{3,2,1,0:T(8,128)(2,1)} %collective-permute-done.10.refs_1_, ...), custom_call_target="tpu_custom_call" | custom-call | flops 339738624 | bytes 2285572 | tf_op jit(solution)/shard_map/pallas_call | solution.py:630
  204.3 18.1 %all-gather.22.cloned.1.call-done = bf16[576,1152]{1,0:T(8,128)(2,1)} async-done(((bf16[144,1152]{1,0:T(8,128)(2,1)}), bf16[576,1152]{1,0:T(8,128)(2,1)}) %all-gather.22.cloned.1.call-update) | async-done | bytes 1327120 | tf_op jit(solution)/shard_map/all_gather | solution.py:424
  222.9 12.5 %collective-permute-done.14.refs_1_ = bf16[2,4,144,1152]{3,2,1,0:T(8,128)(2,1)} collective-permute-done((bf16[2,4,144,1152]{3,2,1,0:T(8,128)(2,1)}, bf16[2,4,144,1152]{3,2,1,0:T(8,128)(2,1)}, u32[]{:S(2)}, u32[]{:S(2)}) %collective-permute-start.14) | collective-permute-done | bytes 2654240 | tf_op jit(solution)/shard_map/ppermute | solution.py:364
  242.5 8.6 %shard_map.232 = f32[256,1152]{1,0:T(8,128)S(1)} custom-call(s32[8]{0:T(128)S(1)} %stack.154.order_ref, bf16[256,4608]{1,0:T(8,128)(2,1)} %get-tuple-element.466.y_ref, bf16[2,4,144,1152]{3,2,1,0:T(8,128)(2,1)} %pad_maximum_fusion.2.refs_0_, bf16[2,4,144,1152]{3,2,1,0:T(8,128)(2,1)} %collective-permute-done.14.refs_1_, ...), custom_call_target="tpu_custom_call" | custom-call | flops 339738624 | bytes 1769476 | tf_op jit(solution)/shard_map/pallas_call | solution.py:630
  253.9 19.1 %all-gather.24.cloned.1.call-done = bf16[576,1152]{1,0:T(8,128)(2,1)} async-done(((bf16[144,1152]{1,0:T(8,128)(2,1)}), bf16[576,1152]{1,0:T(8,128)(2,1)}) %all-gather.24.cloned.1.call-update) | async-done | bytes 1327120 | tf_op jit(solution)/shard_map/all_gather | solution.py:424
  273.2 12.8 %collective-permute-done.19.refs_1_ = bf16[2,4,144,1152]{3,2,1,0:T(8,128)(2,1)} collective-permute-done((bf16[2,4,144,1152]{3,2,1,0:T(8,128)(2,1)}, bf16[2,4,144,1152]{3,2,1,0:T(8,128)(2,1)}, u32[]{:S(2)}, u32[]{:S(2)}) %collective-permute-start.19) | collective-permute-done | bytes 2654240 | tf_op jit(solution)/shard_map/ppermute | solution.py:364
  296.6 12.7 %all-to-all-done.2 = bf16[16,16,1152]{2,1,0:T(8,128)(2,1)} async-done(((bf16[16,16,1152]{2,1,0:T(8,128)(2,1)}), bf16[16,16,1152]{2,1,0:T(8,128)(2,1)}, u32[]{:S(2)}, u32[]{:S(2)}) %all-to-all-start.2) | async-done | bytes 589856 | tf_op jit(solution)/shard_map/all_to_all | solution.py:943
  350.5 8.9 %shard_map.236 = (f32[256,4608]{1,0:T(8,128)}, bf16[256,4608]{1,0:T(8,128)(2,1)S(1)}) custom-call(s32[8]{0:T(128)S(1)} %stack.154.order_ref, bf16[256,1152]{1,0:T(8,128)(2,1)S(1)} %get-tuple-element.408.x_ref, bf16[2,4,144,1152]{3,2,1,0:T(8,128)(2,1)S(1)} %copy-done, bf16[2,4,144,1152]{3,2,1,0:T(8,128)(2,1)} %collective-permute-done.22.refs_1_, ...), custom_call_target="tpu_custom_call" | custom-call | flops 339738624 | bytes 2285572 | tf_op jit(solution)/shard_map/pallas_call | solution.py:630
  384.9 8.8 %shard_map.238.y_ref = bf16[256,4608]{1,0:T(8,128)(2,1)S(1)} custom-call(s32[8]{0:T(128)S(1)} %stack.154.order_ref, bf16[256,1152]{1,0:T(8,128)(2,1)S(1)} %copy-done.29, f32[256,4608]{1,0:T(8,128)} %get-tuple-element.392.pre_ref, bf16[2,4,144,1152]{3,2,1,0:T(8,128)(2,1)S(1)} %pad_maximum_fusion.5.refs_0_, ...), custom_call_target="tpu_custom_call" | custom-call | flops 339738624 | bytes 2285572 | tf_op jit(solution)/shard_map/pallas_call | solution.py:630
  423.6 9.3 %shard_map.242.y_ref.refs_4_ = bf16[4,864,256]{2,1,0:T(8,128)(2,1)} custom-call(bf16[4,864,256]{2,1,0:T(8,128)(2,1)S(1)} %copy-done.6, bf16[4,288,256]{2,1,0:T(8,128)(2,1)S(1)} %shard_map.241.upstream_ref), custom_call_target="tpu_custom_call" | custom-call | flops 94371840 | bytes 516096 | tf_op jit(solution)/shard_map/pallas_call | solution.py:630
  452.3 9.9 %shard_map.244 = (bf16[2,4,144,1152]{3,2,1,0:T(8,128)(2,1)}, bf16[2,4,144,1152]{3,2,1,0:T(8,128)(2,1)}) custom-call(s32[8]{0:T(128)S(1)} %stack.154.order_ref, bf16[256,1152]{1,0:T(8,128)(2,1)S(1)} %copy-done.19, bf16[256,1152]{1,0:T(8,128)(2,1)S(1)} %copy-done.35, bf16[256,1152]{1,0:T(8,128)(2,1)} %multiply_convert_fusion.2.x_ref.refs_2_, ...), custom_call_target="tpu_custom_call" | custom-call | flops 339738624 | bytes 1548292 | tf_op jit(solution)/shard_map/pallas_call | solution.py:630
  480.2 10.5 %shard_map.245.y_ref = bf16[256,4608]{1,0:T(8,128)(2,1)} custom-call(s32[8]{0:T(128)S(1)} %stack.154.order_ref, bf16[256,1152]{1,0:T(8,128)(2,1)S(1)} %multiply_convert_fusion.1.x_ref, f32[256,4608]{1,0:T(8,128)} %get-tuple-element.455.pre_ref, bf16[2,4,144,1152]{3,2,1,0:T(8,128)(2,1)} %pad_maximum_fusion.2.refs_0_, ...), custom_call_target="tpu_custom_call" | custom-call | flops 339738624 | bytes 2285572 | tf_op jit(solution)/shard_map/pallas_call | solution.py:630
  505.5 11.4 %collective-permute-done.41 = bf16[2,4,144,1152]{3,2,1,0:T(8,128)(2,1)} collective-permute-done((bf16[2,4,144,1152]{3,2,1,0:T(8,128)(2,1)}, bf16[2,4,144,1152]{3,2,1,0:T(8,128)(2,1)}, u32[]{:S(2)}, u32[]{:S(2)}) %collective-permute-start.41) | collective-permute-done | bytes 2654240 | tf_op jit(solution)/shard_map/ppermute | solution.py:364
  526.4 8.5 %shard_map.247 = f32[256,1152]{1,0:T(8,128)S(1)} custom-call(s32[8]{0:T(128)S(1)} %stack.154.order_ref, bf16[256,4608]{1,0:T(8,128)(2,1)} %shard_map.245.y_ref, bf16[2,4,144,1152]{3,2,1,0:T(8,128)(2,1)} %pad_maximum_fusion.1.refs_0_, bf16[2,4,144,1152]{3,2,1,0:T(8,128)(2,1)} %collective-permute-done.10.refs_1_, ...), custom_call_target="tpu_custom_call" | custom-call | flops 339738624 | bytes 1769476 | tf_op jit(solution)/shard_map/pallas_call | solution.py:630
  553.0 8.4 %shard_map.250.y_ref.refs_4_ = bf16[4,864,256]{2,1,0:T(8,128)(2,1)S(1)} custom-call(bf16[4,864,256]{2,1,0:T(8,128)(2,1)S(1)} %copy-done.4, bf16[4,288,256]{2,1,0:T(8,128)(2,1)S(1)} %shard_map.249.upstream_ref), custom_call_target="tpu_custom_call" | custom-call | flops 94371840 | bytes 516096 | tf_op jit(solution)/shard_map/pallas_call | solution.py:630
  601.8 9.0 %shard_map.253 = (bf16[2,4,144,1152]{3,2,1,0:T(8,128)(2,1)}, bf16[2,4,144,1152]{3,2,1,0:T(8,128)(2,1)}) custom-call(s32[8]{0:T(128)S(1)} %stack.154.order_ref, bf16[256,1152]{1,0:T(8,128)(2,1)S(1)} %get-tuple-element.526.x_ref.refs_0_, bf16[256,1152]{1,0:T(8,128)(2,1)S(1)} %copy-done.33, bf16[256,1152]{1,0:T(8,128)(2,1)S(1)} %copy-done.22, ...), custom_call_target="tpu_custom_call" | custom-call | flops 339738624 | bytes 1548292 | tf_op jit(solution)/shard_map/pallas_call | solution.py:630
  630.5 31.0 %collective-permute-done.58 = f32[2,6,1152]{2,1,0:T(8,128)S(1)} collective-permute-done((f32[2,6,1152]{2,1,0:T(8,128)S(1)}, f32[2,6,1152]{2,1,0:T(8,128)S(1)}, u32[]{:S(2)}, u32[]{:S(2)}) %collective-permute-start.58) | collective-permute-done | bytes 55328 | tf_op jit(solution)/shard_map/ppermute | solution.py:350
  685.2 10.5 %collective-permute-done.62 = bf16[4,144,1152]{2,1,0:T(8,128)(2,1)S(1)} collective-permute-done((bf16[4,144,1152]{2,1,0:T(8,128)(2,1)}, bf16[4,144,1152]{2,1,0:T(8,128)(2,1)S(1)}, u32[]{:S(2)}, u32[]{:S(2)}) %collective-permute-start.62) | collective-permute-done | bytes 1327136 | tf_op jit(solution)/shard_map/ppermute | solution.py:364
  715.2 20.0 %reduce-scatter.7.cloned.1.call-done = bf16[1,144,1152]{2,1,0:T(8,128)(2,1)} async-done(((bf16[4,144,1152]{2,1,0:T(8,128)(2,1)}), bf16[1,144,1152]{2,1,0:T(8,128)(2,1)}) %reduce-scatter.7.cloned.1.call-update) | async-done | bytes 331792 | tf_op jit(solution)/shard_map/reduce_scatter | solution.py:470
  (509 shorter events, 405.7 us)
Async XLA Ops:
  7.2 44.8 %all-gather.14.cloned.1.call-start = ((), (), s32[]{:S(2)}) async-start(), calls=%async_computation.18 | async-start | bytes 1658880 | tf_op jit(solution)/shard_map/all_gather | solution.py:424
  24.2 60.8 %all-gather.16.cloned.1.call-start = ((), (), s32[]{:S(2)}) async-start(), calls=%async_computation.19 | async-start | bytes 1658880 | tf_op jit(solution)/shard_map/all_gather | solution.py:424
  54.2 72.7 %all-gather.18.cloned.1.call-start = ((), (), s32[]{:S(2)}) async-start(), calls=%async_computation.20 | async-start | bytes 1658880 | tf_op jit(solution)/shard_map/all_gather | solution.py:424
  73.1 53.8 %collective-permute-start.8 = (bf16[2,4,144,1152]{3,2,1,0:T(8,128)(2,1)S(1)}, bf16[2,4,144,1152]{3,2,1,0:T(8,128)(2,1)}, u32[]{:S(2)}, u32[]{:S(2)}) collective-permute-start(bf16[2,4,144,1152]{3,2,1,0:T(8,128)(2,1)S(1)} %pad_maximum_fusion.refs_0_), channel_id=1, source_target_pairs={{0,4},{4,0},{8,12},{12,8},{16,20},{20,16},{24,28},{28,24},{1,5},{5... | collective-permute-start | bytes 7962632 | tf_op jit(solution)/shard_map/ppermute | solution.py:364
  73.2 53.8 %collective-permute-start.7 = (bf16[2,4,144,1152]{3,2,1,0:T(8,128)(2,1)S(1)}, bf16[2,4,144,1152]{3,2,1,0:T(8,128)(2,1)}, u32[]{:S(2)}, u32[]{:S(2)}) collective-permute-start(bf16[2,4,144,1152]{3,2,1,0:T(8,128)(2,1)S(1)} %pad_maximum_fusion.refs_0_), channel_id=1, source_target_pairs={{0,16},{4,12},{8,24},{12,4},{16,0},{20,28},{24,8},{28,20},{1,17},{... | collective-permute-start | bytes 7962632 | tf_op jit(solution)/shard_map/ppermute | solution.py:364
  90.0 78.0 %all-gather.20.cloned.1.call-start = ((), (), s32[]{:S(2)}) async-start(), calls=%async_computation.21 | async-start | bytes 1658880 | tf_op jit(solution)/shard_map/all_gather | solution.py:424
  132.4 90.0 %all-gather.22.cloned.1.call-start = ((), (), s32[]{:S(2)}) async-start(), calls=%async_computation.22 | async-start | bytes 1658880 | tf_op jit(solution)/shard_map/all_gather | solution.py:424
  138.2 46.5 %collective-permute-start.10 = (bf16[2,4,144,1152]{3,2,1,0:T(8,128)(2,1)}, bf16[2,4,144,1152]{3,2,1,0:T(8,128)(2,1)}, u32[]{:S(2)}, u32[]{:S(2)}) collective-permute-start(bf16[2,4,144,1152]{3,2,1,0:T(8,128)(2,1)} %pad_maximum_fusion.1.refs_0_), channel_id=1, source_target_pairs={{0,16},{4,12},{8,24},{12,4},{16,0},{20,28},{24,8},{28,20},{1,17},{... | collective-permute-start | bytes 7962632 | tf_op jit(solution)/shard_map/ppermute | solution.py:364
  188.8 46.5 %collective-permute-start.14 = (bf16[2,4,144,1152]{3,2,1,0:T(8,128)(2,1)}, bf16[2,4,144,1152]{3,2,1,0:T(8,128)(2,1)}, u32[]{:S(2)}, u32[]{:S(2)}) collective-permute-start(bf16[2,4,144,1152]{3,2,1,0:T(8,128)(2,1)} %pad_maximum_fusion.2.refs_0_), channel_id=1, source_target_pairs={{0,16},{4,12},{8,24},{12,4},{16,0},{20,28},{24,8},{28,20},{1,17},{... | collective-permute-start | bytes 7962632 | tf_op jit(solution)/shard_map/ppermute | solution.py:364
  190.2 82.8 %all-gather.24.cloned.1.call-start = ((), (), s32[]{:S(2)}) async-start(), calls=%async_computation.23 | async-start | bytes 1658880 | tf_op jit(solution)/shard_map/all_gather | solution.py:424
  239.4 46.5 %collective-permute-start.19 = (bf16[2,4,144,1152]{3,2,1,0:T(8,128)(2,1)}, bf16[2,4,144,1152]{3,2,1,0:T(8,128)(2,1)}, u32[]{:S(2)}, u32[]{:S(2)}) collective-permute-start(bf16[2,4,144,1152]{3,2,1,0:T(8,128)(2,1)} %pad_maximum_fusion.3.refs_0_), channel_id=1, source_target_pairs={{0,16},{4,12},{8,24},{12,4},{16,0},{20,28},{24,8},{28,20},{1,17},{... | collective-permute-start | bytes 7962632 | tf_op jit(solution)/shard_map/ppermute | solution.py:364
  294.1 43.8 %collective-permute-start.23 = (bf16[2,4,144,1152]{3,2,1,0:T(8,128)(2,1)}, bf16[2,4,144,1152]{3,2,1,0:T(8,128)(2,1)}, u32[]{:S(2)}, u32[]{:S(2)}) collective-permute-start(bf16[2,4,144,1152]{3,2,1,0:T(8,128)(2,1)} %pad_maximum_fusion.4.refs_0_), channel_id=1, source_target_pairs={{0,4},{4,0},{8,12},{12,8},{16,20},{20,16},{24,28},{28,24},{1,5},{5... | collective-permute-start | bytes 7962632 | tf_op jit(solution)/shard_map/ppermute | solution.py:364
  294.5 46.5 %collective-permute-start.22 = (bf16[2,4,144,1152]{3,2,1,0:T(8,128)(2,1)}, bf16[2,4,144,1152]{3,2,1,0:T(8,128)(2,1)}, u32[]{:S(2)}, u32[]{:S(2)}) collective-permute-start(bf16[2,4,144,1152]{3,2,1,0:T(8,128)(2,1)} %pad_maximum_fusion.4.refs_0_), channel_id=1, source_target_pairs={{0,16},{4,12},{8,24},{12,4},{16,0},{20,28},{24,8},{28,20},{1,17},{... | collective-permute-start | bytes 7962632 | tf_op jit(solution)/shard_map/ppermute | solution.py:364
  416.2 51.5 %collective-permute-start.35 = (bf16[2,4,144,1152]{3,2,1,0:T(8,128)(2,1)}, bf16[2,4,144,1152]{3,2,1,0:T(8,128)(2,1)}, u32[]{:S(2)}, u32[]{:S(2)}) collective-permute-start(bf16[2,4,144,1152]{3,2,1,0:T(8,128)(2,1)} %get-tuple-element.432), channel_id=1, source_target_pairs={{0,16},{4,12},{8,24},{12,4},{16,0},{20,28},{24,8},{28,20},{1,17},{... | collective-permute-start | bytes 7962632 | tf_op jit(solution)/shard_map/ppermute | solution.py:364
  450.1 225.8 %reduce-scatter.17.cloned.1.call-start = ((), (), s32[]{:S(2)}) async-start(), calls=%async_computation.17 | async-start | bytes 1658880 | tf_op jit(solution)/shard_map/reduce_scatter | solution.py:470
  470.4 46.5 %collective-permute-start.41 = (bf16[2,4,144,1152]{3,2,1,0:T(8,128)(2,1)}, bf16[2,4,144,1152]{3,2,1,0:T(8,128)(2,1)}, u32[]{:S(2)}, u32[]{:S(2)}) collective-permute-start(bf16[2,4,144,1152]{3,2,1,0:T(8,128)(2,1)} %get-tuple-element.461), channel_id=1, source_target_pairs={{0,16},{4,12},{8,24},{12,4},{16,0},{20,28},{24,8},{28,20},{1,17},{... | collective-permute-start | bytes 7962632 | tf_op jit(solution)/shard_map/ppermute | solution.py:364
  477.4 222.1 %reduce-scatter.15.cloned.1.call-start = ((), (), s32[]{:S(2)}) async-start(), calls=%async_computation.16 | async-start | bytes 1658880 | tf_op jit(solution)/shard_map/reduce_scatter | solution.py:470
  519.8 46.5 %collective-permute-start.48 = (bf16[2,4,144,1152]{3,2,1,0:T(8,128)(2,1)}, bf16[2,4,144,1152]{3,2,1,0:T(8,128)(2,1)}, u32[]{:S(2)}, u32[]{:S(2)}) collective-permute-start(bf16[2,4,144,1152]{3,2,1,0:T(8,128)(2,1)} %get-tuple-element.500), channel_id=1, source_target_pairs={{0,16},{4,12},{8,24},{12,4},{16,0},{20,28},{24,8},{28,20},{1,17},{... | collective-permute-start | bytes 7962632 | tf_op jit(solution)/shard_map/ppermute | solution.py:364
  525.1 178.1 %reduce-scatter.13.cloned.1.call-start = ((), (), s32[]{:S(2)}) async-start(), calls=%async_computation.15 | async-start | bytes 1658880 | tf_op jit(solution)/shard_map/reduce_scatter | solution.py:470
  569.1 46.4 %collective-permute-start.50 = (bf16[2,4,144,1152]{3,2,1,0:T(8,128)(2,1)}, bf16[2,4,144,1152]{3,2,1,0:T(8,128)(2,1)}, u32[]{:S(2)}, u32[]{:S(2)}) collective-permute-start(bf16[2,4,144,1152]{3,2,1,0:T(8,128)(2,1)} %get-tuple-element.521), channel_id=1, source_target_pairs={{0,16},{4,12},{8,24},{12,4},{16,0},{20,28},{24,8},{28,20},{1,17},{... | collective-permute-start | bytes 7962632 | tf_op jit(solution)/shard_map/ppermute | solution.py:364
  573.0 136.7 %reduce-scatter.11.cloned.1.call-start = ((), (), s32[]{:S(2)}) async-start(), calls=%async_computation.14 | async-start | bytes 1658880 | tf_op jit(solution)/shard_map/reduce_scatter | solution.py:470
  618.2 47.8 %collective-permute-start.57 = (bf16[2,4,144,1152]{3,2,1,0:T(8,128)(2,1)}, bf16[2,4,144,1152]{3,2,1,0:T(8,128)(2,1)}, u32[]{:S(2)}, u32[]{:S(2)}) collective-permute-start(bf16[2,4,144,1152]{3,2,1,0:T(8,128)(2,1)} %get-tuple-element.542), channel_id=1, source_target_pairs={{0,16},{4,12},{8,24},{12,4},{16,0},{20,28},{24,8},{28,20},{1,17},{... | collective-permute-start | bytes 7962632 | tf_op jit(solution)/shard_map/ppermute | solution.py:364
  627.6 85.8 %reduce-scatter.9.cloned.1.call-start = ((), (), s32[]{:S(2)}) async-start(), calls=%async_computation.13 | async-start | bytes 1658880 | tf_op jit(solution)/shard_map/reduce_scatter | solution.py:470
  682.1 53.1 %reduce-scatter.7.cloned.1.call-start = ((), (), s32[]{:S(2)}) async-start(), calls=%async_computation.12 | async-start | bytes 1658880 | tf_op jit(solution)/shard_map/reduce_scatter | solution.py:470
  (141 other events, 1871.1 us)
Sparse Core Ops, SparseCore 0:
  10.8 40.1 all-gather.13
  54.3 30.6 all-gather.15
  87.2 39.6 all-gather.17
  132.5 31.2 all-gather.19
  190.3 32.0 all-gather.21
  240.9 32.0 all-gather.23
  477.5 32.5 reduce-scatter.16
  525.3 31.7 reduce-scatter.14
  573.1 33.2 reduce-scatter.12
  622.3 41.7 reduce-scatter.10
  672.3 30.1 reduce-scatter.8
  704.7 30.4 reduce-scatter.6

commit v3 on v2

--- a/solution.py
+++ b/solution.py
@@ -369,6 +369,7 @@
         self.last = ()
         self.awaited = []
         self.under_way = []
+        self.under_way_next = []
 
     def held(self, value):
         return lax.optimization_barrier((value, self.last, self.awaited))[0]
@@ -401,9 +402,14 @@
         own = (jnp.arange(count) == lax.axis_index(axis)).reshape((count,) + (1,) * array.ndim)
         return self.exchange_sum(jnp.where(own, array[None], 0.0), axis)
 
+    def send_ahead(self, array, move):
+        self.under_way_next.append(move(self.held(array)))
+        return self.under_way_next[-1]
+
     def tick(self):
         self.awaited += self.under_way
-        self.under_way = []
+        self.under_way = self.under_way_next
+        self.under_way_next = []
 
 
 def shard_index():
@@ -455,10 +461,8 @@
 class Scatter:
     def __init__(self, line, grad):
         self.line = line
-        self.keep, self.away = grad
-
-    def send(self):
-        self.far = self.line.hop(self.away, 2)
+        self.keep, away = grad
+        self.far = line.send_ahead(away, lambda held: hop(held, 2))
 
     def relay(self):
         work = lambda keep, far: total(keep[1], far[1])
@@ -1025,13 +1029,14 @@
     up_two.send()
     down_two.soon()
     between = one.mlp_down(down_one.pieces, low)
+    between = line.send_ahead(between, lambda held: deal_rows(held, (TENSOR, FRAME)))
     two.turn_back(cotangent)
     line.tick()
     attn_two.end()
     up_two.relay()
     down_two.send()
     two.share(two.d_branch_mlp)
-    between = line(wide, line.send(between, lambda held: deal_rows(held, (TENSOR, FRAME))))
+    between = line(wide, between)
     two.project(between, attn_two.pieces)
     two.attend()
     two.attention_out()
@@ -1043,7 +1048,6 @@
     down_grad = two.grad_down()
     line.tick()
     down_two.end()
-    down_grad.send()
     two.share(two.modulated_mlp, two.modulated)
     two.slope(down_two.pieces)
     two.share(two.d_pre)
@@ -1051,18 +1055,17 @@
     up_grad = two.grad_up()
     line.tick()
     down_grad.relay()
-    up_grad.send()
     two.share(two.d_branch_attn, two.attended)
     two.back_out()
     two.back_attend()
     two.share(two.d_projected)
     d_second = two.back_project(low)
+    d_second = line.send_ahead(d_second, lambda held: deal_rows(held, (TENSOR, FRAME)))
     attn_grad = two.grad_attn()
     line.tick()
     up_grad.relay()
-    attn_grad.send()
     one.share(one.hidden_act, one.attended)
-    d_second = line(wide, deal_rows(d_second, (TENSOR, FRAME)))
+    d_second = line(wide, d_second)
     down_grad.finish()
     one.turn_back(d_second)
     one.share(one.d_branch_mlp)
@@ -1070,7 +1073,6 @@
     down_last = one.grad_down()
     line.tick()
     attn_grad.relay()
-    down_last.send()
     one.share(one.d_pre, one.modulated_mlp, one.modulated)
     up_grad.finish()
     one.back_up()
@@ -1079,7 +1081,6 @@
     one.back_attend()
     line.tick()
     down_last.relay()
-    up_last.send()
     one.share(one.d_branch_attn, one.d_projected)
     attn_grad.finish()
     d_first = one.back_project(low)
@@ -1093,7 +1094,6 @@
     near_mods = flip(d_mods, TENSOR, 2)
     line.tick()
     up_last.relay()
-    attn_last.send()
     down_last.finish()
     input_grad = deal_rows(d_first, TENSOR)
     line.under_way.append(input_grad)
@@ -1103,12 +1103,12 @@
     attn_last.relay()
     up_last.finish()
     input_grad = line(wide, input_grad).reshape(x_in.shape)
+    line.tick()
+    attn_last.finish()
     layer_out = swap_blocks(deal_rows(result, FRAME), devices, own_frames).reshape(x_in.shape)
     d_mods = line(jnp.add, d_mods, near_mods)
     d_mods = lax.dynamic_slice_in_dim(d_mods, lax.axis_index(TENSOR) * part, part, axis=2)
     d_every = line.place_along(d_mods, CLIP)
-    line.tick()
-    attn_last.finish()
     silu_float = silu_rows.astype(jnp.float32)
     grad_mods = [
         sum(

time: 756 us -> 747 us (0.988)
  waiting for transfers between devices: 302 us -> 277 us
  Pallas kernels: 203 us -> 218 us
    pallas_call x26, Pallas kernels: 203 us -> 218 us  [call(): pl.pallas_call(kernel, out_shape=out_shape, grid_spec=pltpu.PrefetchScala...]
    ppermute x52, waiting for transfers between devices: 125 us -> 111 us  [hop(): return lax.ppermute(array, SHARDS, pairs)]
    unnamed x162 -> x126, local copies, waits for them, and re-layouts: 21.6 us -> 17.1 us
  transfers between devices with their start and end apart: 85 -> 85, of which waited for: 35 -> 36; matrix products, arithmetic and copies ran while one was open for 16% -> 17% of each run, Pallas kernels for 27% -> 30%
where the time goes in v3:
time: 747 us; the launch traced here: 737 us
  waiting for transfers between devices  277 us (37%)
  Pallas kernels  218 us (29%)
  other arithmetic  118 us (16%)
  starting transfers between devices  77.8 us (10%)
  local copies, waits for them, and re-layouts  25.6 us (3%)
  between operations  15.9 us (2%)
    pallas_call x26, Pallas kernels, call(): pl.pallas_call(kernel, out_shape=out_shape, grid_spec=pltpu.PrefetchScala...  218 us
    ppermute x52, waiting for transfers between devices, hop(): return lax.ppermute(array, SHARDS, pairs)  111 us
    all_gather x6, waiting for transfers between devices, __init__(): self.whole = lax.all_gather(piece, TENSOR, axis=0, tiled=False)  84.4 us
    ppermute x15, waiting for transfers between devices, flip(): return lax.ppermute(array, axis, [(i, i ^ bit) for i in range(count)])  50.8 us
    convert_element_type x21, other arithmetic, low(): return array.astype(jnp.bfloat16)  48.5 us
    ppermute x52, starting transfers between devices, hop(): return lax.ppermute(array, SHARDS, pairs)  35.4 us
    all_to_all x6, starting transfers between devices, deal_rows(): return lax.all_to_all(rows, axes, split_axis=0, concat_axis=0, tiled=True)  23.1 us
    ppermute x15, starting transfers between devices, flip(): return lax.ppermute(array, axis, [(i, i ^ bit) for i in range(count)])  18.6 us
  transfers between devices with their start and end apart: 85, of which 36 were waited for; matrix products, arithmetic and copies ran while one was open for 17% of the time, Pallas kernels for 30%

profile of v3, /device:TPU:0, one launch (start us, length us, event | category | flops | bytes accessed | tf_op | source)
XLA Modules:
  0.0 737.1 jit_solution(14961567246341570118)
XLA Ops:
  40.7 10.0 %collective-permute-done.4 = f32[4,2,6,288]{3,2,1,0:T(8,128)S(1)} collective-permute-done((f32[4,2,6,288]{3,2,1,0:T(8,128)S(1)}, f32[4,2,6,288]{3,2,1,0:T(8,128)S(1)}, u32[]{:S(2)}, u32[]{:S(2)}) %collective-permute-start.4) | collective-permute-done | bytes 55328 | tf_op jit(solution)/shard_map/ppermute | solution.py:350
  53.7 15.7 %collective-permute-done.5 = bf16[4,144,1152]{2,1,0:T(8,128)(2,1)S(1)} collective-permute-done((bf16[4,144,1152]{2,1,0:T(8,128)(2,1)}, bf16[4,144,1152]{2,1,0:T(8,128)(2,1)S(1)}, u32[]{:S(2)}, u32[]{:S(2)}) %collective-permute-start.5) | collective-permute-done | bytes 1327136 | tf_op jit(solution)/shard_map/ppermute | solution.py:364
  74.8 9.6 %all-gather.16.cloned.1.call-done = bf16[576,1152]{1,0:T(8,128)(2,1)} async-done(((bf16[144,1152]{1,0:T(8,128)(2,1)}), bf16[576,1152]{1,0:T(8,128)(2,1)}) %all-gather.16.cloned.1.call-update) | async-done | bytes 1327120 | tf_op jit(solution)/shard_map/all_gather | solution.py:430
  89.5 36.9 %all-gather.18.cloned.1.call-done = bf16[576,1152]{1,0:T(8,128)(2,1)} async-done(((bf16[144,1152]{1,0:T(8,128)(2,1)}), bf16[576,1152]{1,0:T(8,128)(2,1)}) %all-gather.18.cloned.1.call-update) | async-done | bytes 1327120 | tf_op jit(solution)/shard_map/all_gather | solution.py:430
  172.3 11.4 %collective-permute-done.10.refs_1_ = bf16[2,4,144,1152]{3,2,1,0:T(8,128)(2,1)} collective-permute-done((bf16[2,4,144,1152]{3,2,1,0:T(8,128)(2,1)}, bf16[2,4,144,1152]{3,2,1,0:T(8,128)(2,1)}, u32[]{:S(2)}, u32[]{:S(2)}) %collective-permute-start.10) | collective-permute-done | bytes 2654240 | tf_op jit(solution)/shard_map/ppermute | solution.py:364
  190.7 10.3 %shard_map.231 = (f32[256,4608]{1,0:T(8,128)}, bf16[256,4608]{1,0:T(8,128)(2,1)}) custom-call(s32[8]{0:T(128)S(1)} %stack.154.order_ref, bf16[256,1152]{1,0:T(8,128)(2,1)} %get-tuple-element.488.x_ref, bf16[2,4,144,1152]{3,2,1,0:T(8,128)(2,1)} %pad_maximum_fusion.1.refs_0_, bf16[2,4,144,1152]{3,2,1,0:T(8,128)(2,1)} %collective-permute-done.10.refs_1_, ...), custom_call_target="tpu_custom_call" | custom-call | flops 339738624 | bytes 2285572 | tf_op jit(solution)/shard_map/pallas_call | solution.py:634
  202.2 18.8 %all-gather.22.cloned.1.call-done = bf16[576,1152]{1,0:T(8,128)(2,1)} async-done(((bf16[144,1152]{1,0:T(8,128)(2,1)}), bf16[576,1152]{1,0:T(8,128)(2,1)}) %all-gather.22.cloned.1.call-update) | async-done | bytes 1327120 | tf_op jit(solution)/shard_map/all_gather | solution.py:430
  222.6 11.3 %collective-permute-done.14.refs_1_ = bf16[2,4,144,1152]{3,2,1,0:T(8,128)(2,1)} collective-permute-done((bf16[2,4,144,1152]{3,2,1,0:T(8,128)(2,1)}, bf16[2,4,144,1152]{3,2,1,0:T(8,128)(2,1)}, u32[]{:S(2)}, u32[]{:S(2)}) %collective-permute-start.14) | collective-permute-done | bytes 2654240 | tf_op jit(solution)/shard_map/ppermute | solution.py:364
  252.1 19.0 %all-gather.24.cloned.1.call-done = bf16[576,1152]{1,0:T(8,128)(2,1)} async-done(((bf16[144,1152]{1,0:T(8,128)(2,1)}), bf16[576,1152]{1,0:T(8,128)(2,1)}) %all-gather.24.cloned.1.call-update) | async-done | bytes 1327120 | tf_op jit(solution)/shard_map/all_gather | solution.py:430
  272.3 11.6 %collective-permute-done.19.refs_1_ = bf16[2,4,144,1152]{3,2,1,0:T(8,128)(2,1)} collective-permute-done((bf16[2,4,144,1152]{3,2,1,0:T(8,128)(2,1)}, bf16[2,4,144,1152]{3,2,1,0:T(8,128)(2,1)}, u32[]{:S(2)}, u32[]{:S(2)}) %collective-permute-start.19) | collective-permute-done | bytes 2654240 | tf_op jit(solution)/shard_map/ppermute | solution.py:364
  295.0 8.8 %all-to-all-done.2 = bf16[16,16,1152]{2,1,0:T(8,128)(2,1)} async-done(((bf16[16,16,1152]{2,1,0:T(8,128)(2,1)}), bf16[16,16,1152]{2,1,0:T(8,128)(2,1)}, u32[]{:S(2)}, u32[]{:S(2)}) %all-to-all-start.2) | async-done | bytes 589856 | tf_op jit(solution)/shard_map/all_to_all | solution.py:947
  346.0 9.5 %shard_map.236 = (f32[256,4608]{1,0:T(8,128)}, bf16[256,4608]{1,0:T(8,128)(2,1)S(1)}) custom-call(s32[8]{0:T(128)S(1)} %stack.154.order_ref, bf16[256,1152]{1,0:T(8,128)(2,1)} %get-tuple-element.409.x_ref, bf16[2,4,144,1152]{3,2,1,0:T(8,128)(2,1)} %pad_maximum_fusion.4.refs_0_, bf16[2,4,144,1152]{3,2,1,0:T(8,128)(2,1)} %collective-permute-done.22.refs_1_, ...), custom_call_target="tpu_custom_call" | custom-call | flops 339738624 | bytes 2285572 | tf_op jit(solution)/shard_map/pallas_call | solution.py:634
  381.9 9.0 %shard_map.238.y_ref = bf16[256,4608]{1,0:T(8,128)(2,1)S(1)} custom-call(s32[8]{0:T(128)S(1)} %stack.154.order_ref, bf16[256,1152]{1,0:T(8,128)(2,1)} %multiply_convert_fusion.3.x_ref, f32[256,4608]{1,0:T(8,128)} %get-tuple-element.393.pre_ref, bf16[2,4,144,1152]{3,2,1,0:T(8,128)(2,1)S(1)} %pad_maximum_fusion.5.refs_0_, ...), custom_call_target="tpu_custom_call" | custom-call | flops 339738624 | bytes 2285572 | tf_op jit(solution)/shard_map/pallas_call | solution.py:634
  403.8 17.2 %shard_map.240 = (bf16[2,4,144,1152]{3,2,1,0:T(8,128)(2,1)}, bf16[2,4,144,1152]{3,2,1,0:T(8,128)(2,1)}) custom-call(s32[8]{0:T(128)S(1)} %stack.154.order_ref, bf16[256,1152]{1,0:T(8,128)(2,1)} %get-tuple-element.409.x_ref, bf16[256,1152]{1,0:T(8,128)(2,1)S(1)} %collective-permute-done.32.x_other, bf16[256,4608]{1,0:T(8,128)(2,1)S(1)} %shard_map.238.y_ref, ...), custom_call_target="tpu_custom_call" | custom-call | flops 339738624 | bytes 1400836 | tf_op jit(solution)/shard_map/pallas_call | solution.py:634
  431.9 9.2 %shard_map.242.y_ref.refs_4_ = bf16[4,864,256]{2,1,0:T(8,128)(2,1)} custom-call(bf16[4,864,256]{2,1,0:T(8,128)(2,1)S(1)} %shard_map.233.projected_ref, bf16[4,288,256]{2,1,0:T(8,128)(2,1)S(1)} %shard_map.241.upstream_ref), custom_call_target="tpu_custom_call" | custom-call | flops 94371840 | bytes 516096 | tf_op jit(solution)/shard_map/pallas_call | solution.py:634
  459.6 10.0 %shard_map.244 = (bf16[2,4,144,1152]{3,2,1,0:T(8,128)(2,1)}, bf16[2,4,144,1152]{3,2,1,0:T(8,128)(2,1)}) custom-call(s32[8]{0:T(128)S(1)} %stack.154.order_ref, bf16[256,1152]{1,0:T(8,128)(2,1)} %get-tuple-element.438.x_ref.refs_0_, bf16[256,1152]{1,0:T(8,128)(2,1)S(1)} %copy-done.18, bf16[256,1152]{1,0:T(8,128)(2,1)} %multiply_convert_fusion.2.x_ref.refs_2_, ...), custom_call_target="tpu_custom_call" | custom-call | flops 339738624 | bytes 1548292 | tf_op jit(solution)/shard_map/pallas_call | solution.py:634
  483.8 10.2 %shard_map.245.y_ref = bf16[256,4608]{1,0:T(8,128)(2,1)} custom-call(s32[8]{0:T(128)S(1)} %stack.154.order_ref, bf16[256,1152]{1,0:T(8,128)(2,1)S(1)} %multiply_convert_fusion.1.x_ref, f32[256,4608]{1,0:T(8,128)} %get-tuple-element.457.pre_ref, bf16[2,4,144,1152]{3,2,1,0:T(8,128)(2,1)} %pad_maximum_fusion.2.refs_0_, ...), custom_call_target="tpu_custom_call" | custom-call | flops 339738624 | bytes 2285572 | tf_op jit(solution)/shard_map/pallas_call | solution.py:634
  526.9 8.8 %shard_map.247 = f32[256,1152]{1,0:T(8,128)S(1)} custom-call(s32[8]{0:T(128)S(1)} %stack.154.order_ref, bf16[256,4608]{1,0:T(8,128)(2,1)} %shard_map.245.y_ref, bf16[2,4,144,1152]{3,2,1,0:T(8,128)(2,1)} %pad_maximum_fusion.1.refs_0_, bf16[2,4,144,1152]{3,2,1,0:T(8,128)(2,1)} %collective-permute-done.10.refs_1_, ...), custom_call_target="tpu_custom_call" | custom-call | flops 339738624 | bytes 1769476 | tf_op jit(solution)/shard_map/pallas_call | solution.py:634
  556.1 9.2 %shard_map.250.y_ref.refs_4_ = bf16[4,864,256]{2,1,0:T(8,128)(2,1)} custom-call(bf16[4,864,256]{2,1,0:T(8,128)(2,1)S(1)} %copy-done.3, bf16[4,288,256]{2,1,0:T(8,128)(2,1)S(1)} %shard_map.249.upstream_ref), custom_call_target="tpu_custom_call" | custom-call | flops 94371840 | bytes 516096 | tf_op jit(solution)/shard_map/pallas_call | solution.py:634
  593.0 9.8 %shard_map.253 = (bf16[2,4,144,1152]{3,2,1,0:T(8,128)(2,1)}, bf16[2,4,144,1152]{3,2,1,0:T(8,128)(2,1)}) custom-call(s32[8]{0:T(128)S(1)} %stack.154.order_ref, bf16[256,1152]{1,0:T(8,128)(2,1)S(1)} %get-tuple-element.528.x_ref.refs_0_, bf16[256,1152]{1,0:T(8,128)(2,1)} %collective-permute-done.49.refs_1_, ...), custom_call_target="tpu_custom_call" | custom-call | flops 339738624 | bytes 1548292 | tf_op jit(solution)/shard_map/pallas_call | solution.py:634
  620.4 15.9 %collective-permute-done.58 = f32[2,6,1152]{2,1,0:T(8,128)S(1)} collective-permute-done((f32[2,6,1152]{2,1,0:T(8,128)S(1)}, f32[2,6,1152]{2,1,0:T(8,128)S(1)}, u32[]{:S(2)}, u32[]{:S(2)}) %collective-permute-start.58) | collective-permute-done | bytes 55328 | tf_op jit(solution)/shard_map/ppermute | solution.py:350
  636.4 10.4 %collective-permute-done.59 = f32[2,6,1152]{2,1,0:T(8,128)S(1)} collective-permute-done((f32[2,6,1152]{2,1,0:T(8,128)S(1)}, f32[2,6,1152]{2,1,0:T(8,128)S(1)}, u32[]{:S(2)}, u32[]{:S(2)}) %collective-permute-start.59) | collective-permute-done | bytes 55328 | tf_op jit(solution)/shard_map/ppermute | solution.py:350
  660.5 11.7 %collective-permute-done.60 = bf16[4,144,1152]{2,1,0:T(8,128)(2,1)} collective-permute-done((bf16[4,144,1152]{2,1,0:T(8,128)(2,1)}, bf16[4,144,1152]{2,1,0:T(8,128)(2,1)}, u32[]{:S(2)}, u32[]{:S(2)}) %collective-permute-start.60) | collective-permute-done | bytes 1327136 | tf_op jit(solution)/shard_map/ppermute | solution.py:364
  713.0 12.9 %reduce-scatter.7.cloned.1.call-done = bf16[1,144,1152]{2,1,0:T(8,128)(2,1)} async-done(((bf16[4,144,1152]{2,1,0:T(8,128)(2,1)}), bf16[1,144,1152]{2,1,0:T(8,128)(2,1)}) %reduce-scatter.7.cloned.1.call-update) | async-done | bytes 331792 | tf_op jit(solution)/shard_map/reduce_scatter | solution.py:474
  (473 shorter events, 413.9 us)
Async XLA Ops:
  23.4 61.1 %all-gather.16.cloned.1.call-start = ((), (), s32[]{:S(2)}) async-start(), calls=%async_computation.19 | async-start | bytes 1658880 | tf_op jit(solution)/shard_map/all_gather | solution.py:430
  53.6 72.7 %all-gather.18.cloned.1.call-start = ((), (), s32[]{:S(2)}) async-start(), calls=%async_computation.20 | async-start | bytes 1658880 | tf_op jit(solution)/shard_map/all_gather | solution.py:430
  72.5 53.8 %collective-permute-start.7 = (bf16[2,4,144,1152]{3,2,1,0:T(8,128)(2,1)S(1)}, bf16[2,4,144,1152]{3,2,1,0:T(8,128)(2,1)}, u32[]{:S(2)}, u32[]{:S(2)}) collective-permute-start(bf16[2,4,144,1152]{3,2,1,0:T(8,128)(2,1)S(1)} %pad_maximum_fusion.refs_0_), channel_id=1, source_target_pairs={{0,16},{4,12},{8,24},{12,4},{16,0},{20,28},{24,8},{28,20},{1,17},{... | collective-permute-start | bytes 7962632 | tf_op jit(solution)/shard_map/ppermute | solution.py:364
  74.0 52.3 %collective-permute-start.8 = (bf16[2,4,144,1152]{3,2,1,0:T(8,128)(2,1)S(1)}, bf16[2,4,144,1152]{3,2,1,0:T(8,128)(2,1)}, u32[]{:S(2)}, u32[]{:S(2)}) collective-permute-start(bf16[2,4,144,1152]{3,2,1,0:T(8,128)(2,1)S(1)} %pad_maximum_fusion.refs_0_), channel_id=1, source_target_pairs={{0,4},{4,0},{8,12},{12,8},{16,20},{20,16},{24,28},{28,24},{1,5},{5... | collective-permute-start | bytes 7962632 | tf_op jit(solution)/shard_map/ppermute | solution.py:364
  89.4 77.9 %all-gather.20.cloned.1.call-start = ((), (), s32[]{:S(2)}) async-start(), calls=%async_computation.21 | async-start | bytes 1658880 | tf_op jit(solution)/shard_map/all_gather | solution.py:430
  131.8 89.3 %all-gather.22.cloned.1.call-start = ((), (), s32[]{:S(2)}) async-start(), calls=%async_computation.22 | async-start | bytes 1658880 | tf_op jit(solution)/shard_map/all_gather | solution.py:430
  137.2 46.5 %collective-permute-start.10 = (bf16[2,4,144,1152]{3,2,1,0:T(8,128)(2,1)}, bf16[2,4,144,1152]{3,2,1,0:T(8,128)(2,1)}, u32[]{:S(2)}, u32[]{:S(2)}) collective-permute-start(bf16[2,4,144,1152]{3,2,1,0:T(8,128)(2,1)} %pad_maximum_fusion.1.refs_0_), channel_id=1, source_target_pairs={{0,16},{4,12},{8,24},{12,4},{16,0},{20,28},{24,8},{28,20},{1,17},{... | collective-permute-start | bytes 7962632 | tf_op jit(solution)/shard_map/ppermute | solution.py:364
  137.8 46.0 %collective-permute-start.11 = (bf16[2,4,144,1152]{3,2,1,0:T(8,128)(2,1)}, bf16[2,4,144,1152]{3,2,1,0:T(8,128)(2,1)}, u32[]{:S(2)}, u32[]{:S(2)}) collective-permute-start(bf16[2,4,144,1152]{3,2,1,0:T(8,128)(2,1)} %pad_maximum_fusion.1.refs_0_), channel_id=1, source_target_pairs={{0,4},{4,0},{8,12},{12,8},{16,20},{20,16},{24,28},{28,24},{1,5},{5... | collective-permute-start | bytes 7962632 | tf_op jit(solution)/shard_map/ppermute | solution.py:364
  187.3 46.5 %collective-permute-start.14 = (bf16[2,4,144,1152]{3,2,1,0:T(8,128)(2,1)}, bf16[2,4,144,1152]{3,2,1,0:T(8,128)(2,1)}, u32[]{:S(2)}, u32[]{:S(2)}) collective-permute-start(bf16[2,4,144,1152]{3,2,1,0:T(8,128)(2,1)} %pad_maximum_fusion.2.refs_0_), channel_id=1, source_target_pairs={{0,16},{4,12},{8,24},{12,4},{16,0},{20,28},{24,8},{28,20},{1,17},{... | collective-permute-start | bytes 7962632 | tf_op jit(solution)/shard_map/ppermute | solution.py:364
  187.9 46.0 %collective-permute-start.15 = (bf16[2,4,144,1152]{3,2,1,0:T(8,128)(2,1)}, bf16[2,4,144,1152]{3,2,1,0:T(8,128)(2,1)}, u32[]{:S(2)}, u32[]{:S(2)}) collective-permute-start(bf16[2,4,144,1152]{3,2,1,0:T(8,128)(2,1)} %pad_maximum_fusion.2.refs_0_), channel_id=1, source_target_pairs={{0,4},{4,0},{8,12},{12,8},{16,20},{20,16},{24,28},{28,24},{1,5},{5... | collective-permute-start | bytes 7962632 | tf_op jit(solution)/shard_map/ppermute | solution.py:364
  189.8 81.3 %all-gather.24.cloned.1.call-start = ((), (), s32[]{:S(2)}) async-start(), calls=%async_computation.23 | async-start | bytes 1658880 | tf_op jit(solution)/shard_map/all_gather | solution.py:430
  237.4 46.5 %collective-permute-start.19 = (bf16[2,4,144,1152]{3,2,1,0:T(8,128)(2,1)}, bf16[2,4,144,1152]{3,2,1,0:T(8,128)(2,1)}, u32[]{:S(2)}, u32[]{:S(2)}) collective-permute-start(bf16[2,4,144,1152]{3,2,1,0:T(8,128)(2,1)} %pad_maximum_fusion.3.refs_0_), channel_id=1, source_target_pairs={{0,16},{4,12},{8,24},{12,4},{16,0},{20,28},{24,8},{28,20},{1,17},{... | collective-permute-start | bytes 7962632 | tf_op jit(solution)/shard_map/ppermute | solution.py:364
  292.2 46.5 %collective-permute-start.22 = (bf16[2,4,144,1152]{3,2,1,0:T(8,128)(2,1)}, bf16[2,4,144,1152]{3,2,1,0:T(8,128)(2,1)}, u32[]{:S(2)}, u32[]{:S(2)}) collective-permute-start(bf16[2,4,144,1152]{3,2,1,0:T(8,128)(2,1)} %pad_maximum_fusion.4.refs_0_), channel_id=1, source_target_pairs={{0,16},{4,12},{8,24},{12,4},{16,0},{20,28},{24,8},{28,20},{1,17},{... | collective-permute-start | bytes 7962632 | tf_op jit(solution)/shard_map/ppermute | solution.py:364
  375.2 47.1 %collective-permute-start.31 = (bf16[2,4,144,1152]{3,2,1,0:T(8,128)(2,1)}, bf16[2,4,144,1152]{3,2,1,0:T(8,128)(2,1)}, u32[]{:S(2)}, u32[]{:S(2)}) collective-permute-start(bf16[2,4,144,1152]{3,2,1,0:T(8,128)(2,1)} %get-tuple-element.406), channel_id=1, source_target_pairs={{0,16},{4,12},{8,24},{12,4},{16,0},{20,28},{24,8},{28,20},{1,17},{... | collective-permute-start | bytes 7962632 | tf_op jit(solution)/shard_map/ppermute | solution.py:364
  421.0 49.9 %collective-permute-start.35 = (bf16[2,4,144,1152]{3,2,1,0:T(8,128)(2,1)}, bf16[2,4,144,1152]{3,2,1,0:T(8,128)(2,1)}, u32[]{:S(2)}, u32[]{:S(2)}) collective-permute-start(bf16[2,4,144,1152]{3,2,1,0:T(8,128)(2,1)} %get-tuple-element.434), channel_id=1, source_target_pairs={{0,16},{4,12},{8,24},{12,4},{16,0},{20,28},{24,8},{28,20},{1,17},{... | collective-permute-start | bytes 7962632 | tf_op jit(solution)/shard_map/ppermute | solution.py:364
  458.5 226.6 %reduce-scatter.17.cloned.1.call-start = ((), (), s32[]{:S(2)}) async-start(), calls=%async_computation.17 | async-start | bytes 1658880 | tf_op jit(solution)/shard_map/reduce_scatter | solution.py:474
  469.7 46.5 %collective-permute-start.41 = (bf16[2,4,144,1152]{3,2,1,0:T(8,128)(2,1)}, bf16[2,4,144,1152]{3,2,1,0:T(8,128)(2,1)}, u32[]{:S(2)}, u32[]{:S(2)}) collective-permute-start(bf16[2,4,144,1152]{3,2,1,0:T(8,128)(2,1)} %get-tuple-element.463), channel_id=1, source_target_pairs={{0,16},{4,12},{8,24},{12,4},{16,0},{20,28},{24,8},{28,20},{1,17},{... | collective-permute-start | bytes 7962632 | tf_op jit(solution)/shard_map/ppermute | solution.py:364
  481.7 212.6 %reduce-scatter.15.cloned.1.call-start = ((), (), s32[]{:S(2)}) async-start(), calls=%async_computation.16 | async-start | bytes 1658880 | tf_op jit(solution)/shard_map/reduce_scatter | solution.py:474
  516.2 49.1 %collective-permute-start.48 = (bf16[2,4,144,1152]{3,2,1,0:T(8,128)(2,1)}, bf16[2,4,144,1152]{3,2,1,0:T(8,128)(2,1)}, u32[]{:S(2)}, u32[]{:S(2)}) collective-permute-start(bf16[2,4,144,1152]{3,2,1,0:T(8,128)(2,1)} %get-tuple-element.502), channel_id=1, source_target_pairs={{0,16},{4,12},{8,24},{12,4},{16,0},{20,28},{24,8},{28,20},{1,17},{... | collective-permute-start | bytes 7962632 | tf_op jit(solution)/shard_map/ppermute | solution.py:364
  526.8 175.0 %reduce-scatter.13.cloned.1.call-start = ((), (), s32[]{:S(2)}) async-start(), calls=%async_computation.15 | async-start | bytes 1658880 | tf_op jit(solution)/shard_map/reduce_scatter | solution.py:474
  554.6 55.0 %collective-permute-start.50 = (bf16[2,4,144,1152]{3,2,1,0:T(8,128)(2,1)}, bf16[2,4,144,1152]{3,2,1,0:T(8,128)(2,1)}, u32[]{:S(2)}, u32[]{:S(2)}) collective-permute-start(bf16[2,4,144,1152]{3,2,1,0:T(8,128)(2,1)} %get-tuple-element.523), channel_id=1, source_target_pairs={{0,16},{4,12},{8,24},{12,4},{16,0},{20,28},{24,8},{28,20},{1,17},{... | collective-permute-start | bytes 7962632 | tf_op jit(solution)/shard_map/ppermute | solution.py:364
  602.8 46.4 %collective-permute-start.57 = (bf16[2,4,144,1152]{3,2,1,0:T(8,128)(2,1)}, bf16[2,4,144,1152]{3,2,1,0:T(8,128)(2,1)S(1)}, u32[]{:S(2)}, u32[]{:S(2)}) collective-permute-start(bf16[2,4,144,1152]{3,2,1,0:T(8,128)(2,1)} %get-tuple-element.544), channel_id=1, source_target_pairs={{0,16},{4,12},{8,24},{12,4},{16,0},{20,28},{24,8},{28,20},{1,17},{... | collective-permute-start | bytes 7962632 | tf_op jit(solution)/shard_map/ppermute | solution.py:364
  609.5 98.5 %reduce-scatter.11.cloned.1.call-start = ((), (), s32[]{:S(2)}) async-start(), calls=%async_computation.14 | async-start | bytes 1658880 | tf_op jit(solution)/shard_map/reduce_scatter | solution.py:474
  617.3 93.8 %reduce-scatter.9.cloned.1.call-start = ((), (), s32[]{:S(2)}) async-start(), calls=%async_computation.13 | async-start | bytes 1658880 | tf_op jit(solution)/shard_map/reduce_scatter | solution.py:474
  (123 other events, 1700.5 us)
Sparse Core Ops, SparseCore 0:
  10.2 40.2 all-gather.13
  53.7 30.6 all-gather.15
  86.6 39.6 all-gather.17
  131.9 31.2 all-gather.19
  189.9 31.0 all-gather.21
  240.0 31.0 all-gather.23
  481.8 31.1 reduce-scatter.16
  526.9 31.3 reduce-scatter.14
  572.1 32.2 reduce-scatter.12
  617.4 33.8 reduce-scatter.10
  659.5 31.5 reduce-scatter.8
  694.1 31.6 reduce-scatter.6

commit v4 on v3

--- a/solution.py
+++ b/solution.py
@@ -1002,16 +1002,17 @@
     one = Layer(line, order, modulations[0], 0)
     two = Layer(line, order, modulations[1], own_places)
 
+    line.wait(packed)
     attn_one.send()
     line.tick()
     attn_one.relay()
-    frames_in = line.send(x_in.reshape(-1, width), lambda held: deal_rows(held, TENSOR))
     up_one.send()
     down_one.soon()
     line.tick()
     attn_one.end()
     up_one.relay()
     down_one.send()
+    frames_in = line.send(x_in.reshape(-1, width), lambda held: deal_rows(held, TENSOR))
     one.project(line(wide, frames_in), attn_one.pieces)
     one.attend()
     one.attention_out()
@@ -1029,7 +1030,7 @@
     up_two.send()
     down_two.soon()
     between = one.mlp_down(down_one.pieces, low)
-    between = line.send_ahead(between, lambda held: deal_rows(held, (TENSOR, FRAME)))
+    between = line.send(between, lambda held: deal_rows(held, (TENSOR, FRAME)))
     two.turn_back(cotangent)
     line.tick()
     attn_two.end()

time: 747 us -> 731 us (0.979)
  Pallas kernels: 218 us -> 207 us
    ppermute x52, waiting for transfers between devices: 111 us -> 89.7 us  [hop(): return lax.ppermute(array, SHARDS, pairs)]
    pallas_call x26, Pallas kernels: 218 us -> 207 us  [call(): pl.pallas_call(kernel, out_shape=out_shape, grid_spec=pltpu.PrefetchScala...]
    all_to_all x6, waiting for transfers between devices: 17.1 us -> 27.5 us  [deal_rows(): return lax.all_to_all(rows, axes, split_axis=0, concat_axis=0, tiled=True)]
    unnamed x126 -> x142, local copies, waits for them, and re-layouts: 17.1 us -> 21.3 us
  transfers between devices with their start and end apart: 85 -> 85, of which waited for: 36 -> 33; matrix products, arithmetic and copies ran while one was open for 17% -> 16% of each run, Pallas kernels for 30% -> 29%
where the time goes in v4:
time: 731 us; the launch traced here: 721 us
  waiting for transfers between devices  272 us (37%)
  Pallas kernels  207 us (28%)
  other arithmetic  114 us (16%)
  starting transfers between devices  78.7 us (11%)
  local copies, waits for them, and re-layouts  27.9 us (4%)
  between operations  15.8 us (2%)
    pallas_call x26, Pallas kernels, call(): pl.pallas_call(kernel, out_shape=out_shape, grid_spec=pltpu.PrefetchScala...  207 us
    ppermute x52, waiting for transfers between devices, hop(): return lax.ppermute(array, SHARDS, pairs)  89.7 us
    all_gather x6, waiting for transfers between devices, __init__(): self.whole = lax.all_gather(piece, TENSOR, axis=0, tiled=False)  89.2 us
    ppermute x15, waiting for transfers between devices, flip(): return lax.ppermute(array, axis, [(i, i ^ bit) for i in range(count)])  51.8 us
    convert_element_type x21, other arithmetic, low(): return array.astype(jnp.bfloat16)  50 us
    ppermute x52, starting transfers between devices, hop(): return lax.ppermute(array, SHARDS, pairs)  37.1 us
    all_to_all x6, waiting for transfers between devices, deal_rows(): return lax.all_to_all(rows, axes, split_axis=0, concat_axis=0, tiled=True)  27.5 us
    all_to_all x6, starting transfers between devices, deal_rows(): return lax.all_to_all(rows, axes, split_axis=0, concat_axis=0, tiled=True)  22.7 us
  transfers between devices with their start and end apart: 85, of which 33 were waited for; matrix products, arithmetic and copies ran while one was open for 16% of the time, Pallas kernels for 29%

profile of v4, /device:TPU:0, one launch (start us, length us, event | category | flops | bytes accessed | tf_op | source)
XLA Modules:
  0.0 721.3 jit_solution(10803324688136531393)
XLA Ops:
  54.4 16.9 %collective-permute-done.5 = bf16[4,144,1152]{2,1,0:T(8,128)(2,1)S(1)} collective-permute-done((bf16[4,144,1152]{2,1,0:T(8,128)(2,1)}, bf16[4,144,1152]{2,1,0:T(8,128)(2,1)S(1)}, u32[]{:S(2)}, u32[]{:S(2)}) %collective-permute-start.5) | collective-permute-done | bytes 1327136 | tf_op jit(solution)/shard_map/ppermute | solution.py:364
  75.9 10.7 %all-gather.14.cloned.1.call-done = bf16[576,1152]{1,0:T(8,128)(2,1)} async-done(((bf16[144,1152]{1,0:T(8,128)(2,1)}), bf16[576,1152]{1,0:T(8,128)(2,1)}) %all-gather.14.cloned.1.call-update) | async-done | bytes 1327120 | tf_op jit(solution)/shard_map/all_gather | solution.py:430
  88.0 32.7 %all-gather.18.cloned.1.call-done = bf16[576,1152]{1,0:T(8,128)(2,1)} async-done(((bf16[144,1152]{1,0:T(8,128)(2,1)}), bf16[576,1152]{1,0:T(8,128)(2,1)}) %all-gather.18.cloned.1.call-update) | async-done | bytes 1327120 | tf_op jit(solution)/shard_map/all_gather | solution.py:430
  132.0 17.0 %all-to-all-done.1 = bf16[4,64,1152]{2,1,0:T(8,128)(2,1)S(1)} async-done(((bf16[4,64,1152]{2,1,0:T(8,128)(2,1)}), bf16[4,64,1152]{2,1,0:T(8,128)(2,1)S(1)}, u32[]{:S(2)}, u32[]{:S(2)}) %all-to-all-start.1) | async-done | bytes 589856 | tf_op jit(solution)/shard_map/all_to_all | solution.py:947
  185.4 9.6 %shard_map.231 = (f32[256,4608]{1,0:T(8,128)}, bf16[256,4608]{1,0:T(8,128)(2,1)}) custom-call(s32[8]{0:T(128)S(1)} %stack.154.order_ref, bf16[256,1152]{1,0:T(8,128)(2,1)} %get-tuple-element.488.x_ref, bf16[2,4,144,1152]{3,2,1,0:T(8,128)(2,1)S(1)} %copy-done, bf16[2,4,144,1152]{3,2,1,0:T(8,128)(2,1)} %collective-permute-done.10.refs_1_, ...), custom_call_target="tpu_custom_call" | custom-call | flops 339738624 | bytes 2285572 | tf_op jit(solution)/shard_map/pallas_call | solution.py:634
  196.1 18.4 %all-gather.22.cloned.1.call-done = bf16[576,1152]{1,0:T(8,128)(2,1)} async-done(((bf16[144,1152]{1,0:T(8,128)(2,1)}), bf16[576,1152]{1,0:T(8,128)(2,1)}) %all-gather.22.cloned.1.call-update) | async-done | bytes 1327120 | tf_op jit(solution)/shard_map/all_gather | solution.py:430
  214.8 12.2 %collective-permute-done.14.refs_1_ = bf16[2,4,144,1152]{3,2,1,0:T(8,128)(2,1)} collective-permute-done((bf16[2,4,144,1152]{3,2,1,0:T(8,128)(2,1)}, bf16[2,4,144,1152]{3,2,1,0:T(8,128)(2,1)}, u32[]{:S(2)}, u32[]{:S(2)}) %collective-permute-start.14) | collective-permute-done | bytes 2654240 | tf_op jit(solution)/shard_map/ppermute | solution.py:364
  233.5 8.6 %shard_map.232 = f32[256,1152]{1,0:T(8,128)S(1)} custom-call(s32[8]{0:T(128)S(1)} %stack.154.order_ref, bf16[256,4608]{1,0:T(8,128)(2,1)} %get-tuple-element.468.y_ref, bf16[2,4,144,1152]{3,2,1,0:T(8,128)(2,1)} %pad_maximum_fusion.2.refs_0_, bf16[2,4,144,1152]{3,2,1,0:T(8,128)(2,1)} %collective-permute-done.14.refs_1_, ...), custom_call_target="tpu_custom_call" | custom-call | flops 339738624 | bytes 1769476 | tf_op jit(solution)/shard_map/pallas_call | solution.py:634
  249.9 27.4 %all-gather.24.cloned.1.call-done = bf16[576,1152]{1,0:T(8,128)(2,1)} async-done(((bf16[144,1152]{1,0:T(8,128)(2,1)}), bf16[576,1152]{1,0:T(8,128)(2,1)}) %all-gather.24.cloned.1.call-update) | async-done | bytes 1327120 | tf_op jit(solution)/shard_map/all_gather | solution.py:430
  323.2 10.0 %collective-permute-done.22.refs_1_ = bf16[2,4,144,1152]{3,2,1,0:T(8,128)(2,1)} collective-permute-done((bf16[2,4,144,1152]{3,2,1,0:T(8,128)(2,1)}, bf16[2,4,144,1152]{3,2,1,0:T(8,128)(2,1)}, u32[]{:S(2)}, u32[]{:S(2)}) %collective-permute-start.22) | collective-permute-done | bytes 2654240 | tf_op jit(solution)/shard_map/ppermute | solution.py:364
  339.9 9.3 %shard_map.236 = (f32[256,4608]{1,0:T(8,128)}, bf16[256,4608]{1,0:T(8,128)(2,1)S(1)}) custom-call(s32[8]{0:T(128)S(1)} %stack.154.order_ref, bf16[256,1152]{1,0:T(8,128)(2,1)S(1)} %get-tuple-element.409.x_ref, bf16[2,4,144,1152]{3,2,1,0:T(8,128)(2,1)} %pad_maximum_fusion.4.refs_0_, bf16[2,4,144,1152]{3,2,1,0:T(8,128)(2,1)} %collective-permute-done.22.refs_1_, ...), custom_call_target="tpu_custom_call" | custom-call | flops 339738624 | bytes 2285572 | tf_op jit(solution)/shard_map/pallas_call | solution.py:634
  374.1 9.0 %shard_map.238.y_ref = bf16[256,4608]{1,0:T(8,128)(2,1)S(1)} custom-call(s32[8]{0:T(128)S(1)} %stack.154.order_ref, bf16[256,1152]{1,0:T(8,128)(2,1)} %multiply_convert_fusion.3.x_ref, f32[256,4608]{1,0:T(8,128)} %get-tuple-element.393.pre_ref, bf16[2,4,144,1152]{3,2,1,0:T(8,128)(2,1)S(1)} %pad_maximum_fusion.5.refs_0_, ...), custom_call_target="tpu_custom_call" | custom-call | flops 339738624 | bytes 2285572 | tf_op jit(solution)/shard_map/pallas_call | solution.py:634
  383.8 8.6 %shard_map.239 = f32[256,1152]{1,0:T(8,128)S(1)} custom-call(s32[8]{0:T(128)S(1)} %stack.154.order_ref, bf16[256,4608]{1,0:T(8,128)(2,1)S(1)} %shard_map.238.y_ref, bf16[2,4,144,1152]{3,2,1,0:T(8,128)(2,1)} %pad_maximum_fusion.4.refs_0_, bf16[2,4,144,1152]{3,2,1,0:T(8,128)(2,1)} %collective-permute-done.22.refs_1_, ...), custom_call_target="tpu_custom_call" | custom-call | flops 339738624 | bytes 1769476 | tf_op jit(solution)/shard_map/pallas_call | solution.py:634
  415.6 9.3 %shard_map.242.y_ref.refs_4_ = bf16[4,864,256]{2,1,0:T(8,128)(2,1)} custom-call(bf16[4,864,256]{2,1,0:T(8,128)(2,1)S(1)} %shard_map.233.projected_ref, bf16[4,288,256]{2,1,0:T(8,128)(2,1)S(1)} %shard_map.241.upstream_ref), custom_call_target="tpu_custom_call" | custom-call | flops 94371840 | bytes 516096 | tf_op jit(solution)/shard_map/pallas_call | solution.py:634
  442.5 10.1 %shard_map.244 = (bf16[2,4,144,1152]{3,2,1,0:T(8,128)(2,1)}, bf16[2,4,144,1152]{3,2,1,0:T(8,128)(2,1)}) custom-call(s32[8]{0:T(128)S(1)} %stack.154.order_ref, bf16[256,1152]{1,0:T(8,128)(2,1)} %get-tuple-element.438.x_ref.refs_0_, bf16[256,1152]{1,0:T(8,128)(2,1)S(1)} %copy-done.23, bf16[256,1152]{1,0:T(8,128)(2,1)} %multiply_convert_fusion.2.x_ref.refs_2_, ...), custom_call_target="tpu_custom_call" | custom-call | flops 339738624 | bytes 1548292 | tf_op jit(solution)/shard_map/pallas_call | solution.py:634
  466.9 10.4 %shard_map.245.y_ref = bf16[256,4608]{1,0:T(8,128)(2,1)} custom-call(s32[8]{0:T(128)S(1)} %stack.154.order_ref, bf16[256,1152]{1,0:T(8,128)(2,1)S(1)} %multiply_convert_fusion.1.x_ref, f32[256,4608]{1,0:T(8,128)} %get-tuple-element.457.pre_ref, bf16[2,4,144,1152]{3,2,1,0:T(8,128)(2,1)} %pad_maximum_fusion.2.refs_0_, ...), custom_call_target="tpu_custom_call" | custom-call | flops 339738624 | bytes 2285572 | tf_op jit(solution)/shard_map/pallas_call | solution.py:634
  477.4 8.2 %shard_map.246 = (bf16[2,4,144,1152]{3,2,1,0:T(8,128)(2,1)}, bf16[2,4,144,1152]{3,2,1,0:T(8,128)(2,1)}) custom-call(s32[8]{0:T(128)S(1)} %stack.154.order_ref, bf16[256,1152]{1,0:T(8,128)(2,1)S(1)} %multiply_convert_fusion.1.x_ref, bf16[256,1152]{1,0:T(8,128)(2,1)S(1)} %collective-permute-done.42.x_other, bf16[256,4608]{1,0:T(8,128)(2,1)} %get-tuple-element.468.y_ref, ...), custom_call_target="tpu_custom_call" | custom-call | flops 339738624 | bytes 1400836 | tf_op jit(solution)/shard_map/pallas_call | solution.py:634
  524.3 8.3 %shard_map.248 = (bf16[2,4,144,1152]{3,2,1,0:T(8,128)(2,1)}, bf16[2,4,144,1152]{3,2,1,0:T(8,128)(2,1)}) custom-call(s32[8]{0:T(128)S(1)} %stack.154.order_ref, bf16[256,1152]{1,0:T(8,128)(2,1)} %get-tuple-element.488.x_ref, bf16[256,1152]{1,0:T(8,128)(2,1)} %collective-permute-done.45.x_other, bf16[256,4608]{1,0:T(8,128)(2,1)} %shard_map.245.y_ref, ...), custom_call_target="tpu_custom_call" | custom-call | flops 339738624 | bytes 1400836 | tf_op jit(solution)/shard_map/pallas_call | solution.py:634
  540.0 9.2 %shard_map.250.y_ref.refs_4_ = bf16[4,864,256]{2,1,0:T(8,128)(2,1)} custom-call(bf16[4,864,256]{2,1,0:T(8,128)(2,1)S(1)} %copy-done.5, bf16[4,288,256]{2,1,0:T(8,128)(2,1)S(1)} %shard_map.249.upstream_ref), custom_call_target="tpu_custom_call" | custom-call | flops 94371840 | bytes 516096 | tf_op jit(solution)/shard_map/pallas_call | solution.py:634
  577.9 9.7 %shard_map.253 = (bf16[2,4,144,1152]{3,2,1,0:T(8,128)(2,1)}, bf16[2,4,144,1152]{3,2,1,0:T(8,128)(2,1)}) custom-call(s32[8]{0:T(128)S(1)} %stack.154.order_ref, bf16[256,1152]{1,0:T(8,128)(2,1)S(1)} %get-tuple-element.528.x_ref.refs_0_, bf16[256,1152]{1,0:T(8,128)(2,1)} %collective-permute-done.49.refs_1_, ...), custom_call_target="tpu_custom_call" | custom-call | flops 339738624 | bytes 1548292 | tf_op jit(solution)/shard_map/pallas_call | solution.py:634
  604.9 14.3 %collective-permute-done.58 = f32[2,6,1152]{2,1,0:T(8,128)S(1)} collective-permute-done((f32[2,6,1152]{2,1,0:T(8,128)S(1)}, f32[2,6,1152]{2,1,0:T(8,128)S(1)}, u32[]{:S(2)}, u32[]{:S(2)}) %collective-permute-start.58) | collective-permute-done | bytes 55328 | tf_op jit(solution)/shard_map/ppermute | solution.py:350
  619.8 11.1 %collective-permute-done.59 = f32[2,6,1152]{2,1,0:T(8,128)S(1)} collective-permute-done((f32[2,6,1152]{2,1,0:T(8,128)S(1)}, f32[2,6,1152]{2,1,0:T(8,128)S(1)}, u32[]{:S(2)}, u32[]{:S(2)}) %collective-permute-start.59) | collective-permute-done | bytes 55328 | tf_op jit(solution)/shard_map/ppermute | solution.py:350
  644.3 12.6 %collective-permute-done.60 = bf16[4,144,1152]{2,1,0:T(8,128)(2,1)} collective-permute-done((bf16[4,144,1152]{2,1,0:T(8,128)(2,1)}, bf16[4,144,1152]{2,1,0:T(8,128)(2,1)}, u32[]{:S(2)}, u32[]{:S(2)}) %collective-permute-start.60) | collective-permute-done | bytes 1327136 | tf_op jit(solution)/shard_map/ppermute | solution.py:364
  697.6 12.6 %reduce-scatter.7.cloned.1.call-done = bf16[1,144,1152]{2,1,0:T(8,128)(2,1)} async-done(((bf16[4,144,1152]{2,1,0:T(8,128)(2,1)}), bf16[1,144,1152]{2,1,0:T(8,128)(2,1)}) %reduce-scatter.7.cloned.1.call-update) | async-done | bytes 331792 | tf_op jit(solution)/shard_map/reduce_scatter | solution.py:474
  (489 shorter events, 399.4 us)
Async XLA Ops:
  7.2 46.0 %all-gather.16.cloned.1.call-start = ((), (), s32[]{:S(2)}) async-start(), calls=%async_computation.19 | async-start | bytes 1658880 | tf_op jit(solution)/shard_map/all_gather | solution.py:430
  20.6 65.9 %all-gather.14.cloned.1.call-start = ((), (), s32[]{:S(2)}) async-start(), calls=%async_computation.18 | async-start | bytes 1658880 | tf_op jit(solution)/shard_map/all_gather | solution.py:430
  54.3 66.4 %all-gather.18.cloned.1.call-start = ((), (), s32[]{:S(2)}) async-start(), calls=%async_computation.20 | async-start | bytes 1658880 | tf_op jit(solution)/shard_map/all_gather | solution.py:430
  74.3 46.4 %collective-permute-start.7 = (bf16[2,4,144,1152]{3,2,1,0:T(8,128)(2,1)S(1)}, bf16[2,4,144,1152]{3,2,1,0:T(8,128)(2,1)}, u32[]{:S(2)}, u32[]{:S(2)}) collective-permute-start(bf16[2,4,144,1152]{3,2,1,0:T(8,128)(2,1)S(1)} %pad_maximum_fusion.refs_0_), channel_id=1, source_target_pairs={{0,16},{4,12},{8,24},{12,4},{16,0},{20,28},{24,8},{28,20},{1,17},{... | collective-permute-start | bytes 7962632 | tf_op jit(solution)/shard_map/ppermute | solution.py:364
  127.7 49.1 %all-gather.20.cloned.1.call-start = ((), (), s32[]{:S(2)}) async-start(), calls=%async_computation.21 | async-start | bytes 1658880 | tf_op jit(solution)/shard_map/all_gather | solution.py:430
  128.3 86.2 %all-gather.22.cloned.1.call-start = ((), (), s32[]{:S(2)}) async-start(), calls=%async_computation.22 | async-start | bytes 1658880 | tf_op jit(solution)/shard_map/all_gather | solution.py:430
  129.1 47.7 %collective-permute-start.10 = (bf16[2,4,144,1152]{3,2,1,0:T(8,128)(2,1)}, bf16[2,4,144,1152]{3,2,1,0:T(8,128)(2,1)}, u32[]{:S(2)}, u32[]{:S(2)}) collective-permute-start(bf16[2,4,144,1152]{3,2,1,0:T(8,128)(2,1)} %pad_maximum_fusion.1.refs_0_), channel_id=1, source_target_pairs={{0,16},{4,12},{8,24},{12,4},{16,0},{20,28},{24,8},{28,20},{1,17},{... | collective-permute-start | bytes 7962632 | tf_op jit(solution)/shard_map/ppermute | solution.py:364
  130.6 46.2 %collective-permute-start.11 = (bf16[2,4,144,1152]{3,2,1,0:T(8,128)(2,1)}, bf16[2,4,144,1152]{3,2,1,0:T(8,128)(2,1)}, u32[]{:S(2)}, u32[]{:S(2)}) collective-permute-start(bf16[2,4,144,1152]{3,2,1,0:T(8,128)(2,1)} %pad_maximum_fusion.1.refs_0_), channel_id=1, source_target_pairs={{0,4},{4,0},{8,12},{12,8},{16,20},{20,16},{24,28},{28,24},{1,5},{5... | collective-permute-start | bytes 7962632 | tf_op jit(solution)/shard_map/ppermute | solution.py:364
  130.8 46.0 %collective-permute-start.12 = (bf16[4,144,1152]{2,1,0:T(8,128)(2,1)}, bf16[4,144,1152]{2,1,0:T(8,128)(2,1)}, u32[]{:S(2)}, u32[]{:S(2)}) collective-permute-start(bf16[4,144,1152]{2,1,0:T(8,128)(2,1)} %bitcast.171), channel_id=1, source_target_pairs={{0,8},{4,20},{8,0},{12,28},{16,24},{20,4},{24,16},{28,12},{1,9},{5... | collective-permute-start | bytes 3981320 | tf_op jit(solution)/shard_map/ppermute | solution.py:364
  180.4 46.5 %collective-permute-start.14 = (bf16[2,4,144,1152]{3,2,1,0:T(8,128)(2,1)}, bf16[2,4,144,1152]{3,2,1,0:T(8,128)(2,1)}, u32[]{:S(2)}, u32[]{:S(2)}) collective-permute-start(bf16[2,4,144,1152]{3,2,1,0:T(8,128)(2,1)} %pad_maximum_fusion.2.refs_0_), channel_id=1, source_target_pairs={{0,16},{4,12},{8,24},{12,4},{16,0},{20,28},{24,8},{28,20},{1,17},{... | collective-permute-start | bytes 7962632 | tf_op jit(solution)/shard_map/ppermute | solution.py:364
  182.1 95.1 %all-gather.24.cloned.1.call-start = ((), (), s32[]{:S(2)}) async-start(), calls=%async_computation.23 | async-start | bytes 1658880 | tf_op jit(solution)/shard_map/all_gather | solution.py:430
  230.4 46.8 %collective-permute-start.19 = (bf16[2,4,144,1152]{3,2,1,0:T(8,128)(2,1)}, bf16[2,4,144,1152]{3,2,1,0:T(8,128)(2,1)}, u32[]{:S(2)}, u32[]{:S(2)}) collective-permute-start(bf16[2,4,144,1152]{3,2,1,0:T(8,128)(2,1)} %pad_maximum_fusion.3.refs_0_), channel_id=1, source_target_pairs={{0,16},{4,12},{8,24},{12,4},{16,0},{20,28},{24,8},{28,20},{1,17},{... | collective-permute-start | bytes 7962632 | tf_op jit(solution)/shard_map/ppermute | solution.py:364
  231.9 45.4 %collective-permute-start.20 = (bf16[2,4,144,1152]{3,2,1,0:T(8,128)(2,1)}, bf16[2,4,144,1152]{3,2,1,0:T(8,128)(2,1)}, u32[]{:S(2)}, u32[]{:S(2)}) collective-permute-start(bf16[2,4,144,1152]{3,2,1,0:T(8,128)(2,1)} %pad_maximum_fusion.3.refs_0_), channel_id=1, source_target_pairs={{0,4},{4,0},{8,12},{12,8},{16,20},{20,16},{24,28},{28,24},{1,5},{5... | collective-permute-start | bytes 7962632 | tf_op jit(solution)/shard_map/ppermute | solution.py:364
  286.7 46.5 %collective-permute-start.22 = (bf16[2,4,144,1152]{3,2,1,0:T(8,128)(2,1)}, bf16[2,4,144,1152]{3,2,1,0:T(8,128)(2,1)}, u32[]{:S(2)}, u32[]{:S(2)}) collective-permute-start(bf16[2,4,144,1152]{3,2,1,0:T(8,128)(2,1)} %pad_maximum_fusion.4.refs_0_), channel_id=1, source_target_pairs={{0,16},{4,12},{8,24},{12,4},{16,0},{20,28},{24,8},{28,20},{1,17},{... | collective-permute-start | bytes 7962632 | tf_op jit(solution)/shard_map/ppermute | solution.py:364
  404.3 49.9 %collective-permute-start.35 = (bf16[2,4,144,1152]{3,2,1,0:T(8,128)(2,1)}, bf16[2,4,144,1152]{3,2,1,0:T(8,128)(2,1)}, u32[]{:S(2)}, u32[]{:S(2)}) collective-permute-start(bf16[2,4,144,1152]{3,2,1,0:T(8,128)(2,1)} %get-tuple-element.434), channel_id=1, source_target_pairs={{0,16},{4,12},{8,24},{12,4},{16,0},{20,28},{24,8},{28,20},{1,17},{... | collective-permute-start | bytes 7962632 | tf_op jit(solution)/shard_map/ppermute | solution.py:364
  441.3 228.4 %reduce-scatter.17.cloned.1.call-start = ((), (), s32[]{:S(2)}) async-start(), calls=%async_computation.17 | async-start | bytes 1658880 | tf_op jit(solution)/shard_map/reduce_scatter | solution.py:474
  452.6 46.5 %collective-permute-start.41 = (bf16[2,4,144,1152]{3,2,1,0:T(8,128)(2,1)}, bf16[2,4,144,1152]{3,2,1,0:T(8,128)(2,1)}, u32[]{:S(2)}, u32[]{:S(2)}) collective-permute-start(bf16[2,4,144,1152]{3,2,1,0:T(8,128)(2,1)} %get-tuple-element.463), channel_id=1, source_target_pairs={{0,16},{4,12},{8,24},{12,4},{16,0},{20,28},{24,8},{28,20},{1,17},{... | collective-permute-start | bytes 7962632 | tf_op jit(solution)/shard_map/ppermute | solution.py:364
  464.8 213.8 %reduce-scatter.15.cloned.1.call-start = ((), (), s32[]{:S(2)}) async-start(), calls=%async_computation.16 | async-start | bytes 1658880 | tf_op jit(solution)/shard_map/reduce_scatter | solution.py:474
  499.1 50.1 %collective-permute-start.48 = (bf16[2,4,144,1152]{3,2,1,0:T(8,128)(2,1)}, bf16[2,4,144,1152]{3,2,1,0:T(8,128)(2,1)}, u32[]{:S(2)}, u32[]{:S(2)}) collective-permute-start(bf16[2,4,144,1152]{3,2,1,0:T(8,128)(2,1)} %get-tuple-element.502), channel_id=1, source_target_pairs={{0,16},{4,12},{8,24},{12,4},{16,0},{20,28},{24,8},{28,20},{1,17},{... | collective-permute-start | bytes 7962632 | tf_op jit(solution)/shard_map/ppermute | solution.py:364
  510.4 176.0 %reduce-scatter.13.cloned.1.call-start = ((), (), s32[]{:S(2)}) async-start(), calls=%async_computation.15 | async-start | bytes 1658880 | tf_op jit(solution)/shard_map/reduce_scatter | solution.py:474
  539.2 54.6 %collective-permute-start.50 = (bf16[2,4,144,1152]{3,2,1,0:T(8,128)(2,1)}, bf16[2,4,144,1152]{3,2,1,0:T(8,128)(2,1)}, u32[]{:S(2)}, u32[]{:S(2)}) collective-permute-start(bf16[2,4,144,1152]{3,2,1,0:T(8,128)(2,1)} %get-tuple-element.523), channel_id=1, source_target_pairs={{0,16},{4,12},{8,24},{12,4},{16,0},{20,28},{24,8},{28,20},{1,17},{... | collective-permute-start | bytes 7962632 | tf_op jit(solution)/shard_map/ppermute | solution.py:364
  587.6 46.4 %collective-permute-start.57 = (bf16[2,4,144,1152]{3,2,1,0:T(8,128)(2,1)}, bf16[2,4,144,1152]{3,2,1,0:T(8,128)(2,1)S(1)}, u32[]{:S(2)}, u32[]{:S(2)}) collective-permute-start(bf16[2,4,144,1152]{3,2,1,0:T(8,128)(2,1)} %get-tuple-element.544), channel_id=1, source_target_pairs={{0,16},{4,12},{8,24},{12,4},{16,0},{20,28},{24,8},{28,20},{1,17},{... | collective-permute-start | bytes 7962632 | tf_op jit(solution)/shard_map/ppermute | solution.py:364
  593.7 98.4 %reduce-scatter.11.cloned.1.call-start = ((), (), s32[]{:S(2)}) async-start(), calls=%async_computation.14 | async-start | bytes 1658880 | tf_op jit(solution)/shard_map/reduce_scatter | solution.py:474
  601.9 93.9 %reduce-scatter.9.cloned.1.call-start = ((), (), s32[]{:S(2)}) async-start(), calls=%async_computation.13 | async-start | bytes 1658880 | tf_op jit(solution)/shard_map/reduce_scatter | solution.py:474
  (131 other events, 1699.6 us)
Sparse Core Ops, SparseCore 0:
  10.2 36.7 all-gather.15
  54.4 32.0 all-gather.13
  88.7 31.9 all-gather.17
  130.4 35.8 all-gather.19
  182.2 32.2 all-gather.21
  232.3 44.9 all-gather.23
  465.0 31.8 reduce-scatter.16
  510.5 31.3 reduce-scatter.14
  557.0 32.0 reduce-scatter.12
  602.0 33.1 reduce-scatter.10
  643.3 31.5 reduce-scatter.8
  678.7 31.4 reduce-scatter.6

commit v5 on v4

--- a/solution.py
+++ b/solution.py
@@ -429,15 +429,33 @@
         self.line = line
         self.whole = lax.all_gather(piece, TENSOR, axis=0, tiled=False)
 
-    def soon(self):
-        self.line.under_way.append(self.whole)
-
     def send(self):
         self.line.wait(self.whole)
         self.near = self.line.hop(self.whole, 1)
 
     def relay(self):
         self.pair = self.line(lambda *pair: jnp.stack(pair), self.whole, self.near)
+        self.far = self.line.hop(self.pair, 2)
+        self.other_pair = self.line.hop(self.pair, 0)
+
+    def end(self):
+        other_far = self.line.hop(self.far, 0)
+        self.pieces = (self.pair, self.far, self.other_pair, other_far)
+
+
+class MidGather:
+    def __init__(self, line, piece):
+        self.line = line
+        self.piece = piece
+
+    def send(self):
+        self.near = self.line.hop(self.piece, 1)
+
+    def join(self):
+        pair = self.line(lambda *pair: jnp.stack(pair), self.piece, self.near)
+        self.pair = lax.all_gather(pair, TENSOR, axis=0, tiled=False)
+
+    def relay(self):
         self.far = self.line.hop(self.pair, 2)
         self.other_pair = self.line.hop(self.pair, 0)
 
@@ -494,10 +512,11 @@
 
 
 def assemble(order_ref, piece_refs, whole_ref):
-    rows = piece_refs[0].shape[2]
     for j in range(PIECES):
+        ref = piece_refs[j // 2]
+        rows = ref.shape[2]
         start = pl.multiple_of(order_ref[j] * rows, 16)
-        whole_ref[pl.ds(start, rows), :] = piece_refs[j // 2][j % 2, 0]
+        whole_ref[pl.ds(start, rows), :] = ref[(0, j % 2) if ref.shape[0] == 1 else (j % 2, 0)]
 
 
 def up_kernel(order_ref, x_ref, *refs):
@@ -660,23 +679,31 @@
     return pl.BlockSpec((tokens, width), lambda z, *_: (0, z))
 
 
-def sizes(pieces):
-    _, groups, rows, width = pieces[0].shape
+def sizes(pieces, groups_first):
+    groups = pieces[0].shape[0 if groups_first else 1]
+    rows, width = pieces[0].shape[2:]
     return groups, rows, width, rows * PIECES
+
+
+def piece_specs(pieces, groups_first):
+    rows, width = pieces[0].shape[2:]
+    if groups_first:
+        return [lead((2, rows, width))] * PAIRS
+    return pair_specs(rows, width, PAIRS)
 
 
 def pair_specs(rows, width, count):
     return [pl.BlockSpec((2, 1, rows, width), lambda z, *_: (0, z, 0, 0))] * count
 
 
-def times_up(order, x, pieces):
-    groups, rows, width, depth = sizes(pieces)
+def times_up(order, x, pieces, groups_first):
+    groups, rows, width, depth = sizes(pieces, groups_first)
     tokens = x.shape[0]
     shape = (tokens, groups * width)
     return call(
         up_kernel,
         (groups,),
-        [still(x.shape)] + pair_specs(rows, width, PAIRS),
+        [still(x.shape)] + piece_specs(pieces, groups_first),
         [column(tokens, width)] * 2,
         [jax.ShapeDtypeStruct(shape, jnp.float32), jax.ShapeDtypeStruct(shape, jnp.bfloat16)],
         [pltpu.VMEM((depth, width), jnp.bfloat16)],
@@ -685,13 +712,13 @@
     )
 
 
-def times_slope(order, x, pre, pieces):
-    groups, rows, width, depth = sizes(pieces)
+def times_slope(order, x, pre, pieces, groups_first=False):
+    groups, rows, width, depth = sizes(pieces, groups_first)
     tokens = x.shape[0]
     return call(
         slope_kernel,
         (groups,),
-        [still(x.shape), column(tokens, width)] + pair_specs(rows, width, PAIRS),
+        [still(x.shape), column(tokens, width)] + piece_specs(pieces, groups_first),
         column(tokens, width),
         jax.ShapeDtypeStruct(pre.shape, jnp.bfloat16),
         [pltpu.VMEM((depth, width), jnp.bfloat16)],
@@ -700,13 +727,13 @@
     )
 
 
-def times_turned(order, x, pieces, low, high):
-    groups, rows, width, depth = sizes(pieces)
+def times_turned(order, x, pieces, low, high, groups_first=False):
+    groups, rows, width, depth = sizes(pieces, groups_first)
     tokens = x.shape[0]
     return call(
         functools.partial(turned_kernel, low, high),
         (groups,),
-        [still(x.shape)] + pair_specs(rows, width, PAIRS),
+        [still(x.shape)] + piece_specs(pieces, groups_first),
         lead((high - low, tokens)),
         jax.ShapeDtypeStruct((groups, high - low, tokens), jnp.bfloat16),
         [pltpu.VMEM((depth, width), jnp.bfloat16)],
@@ -715,14 +742,14 @@
     )
 
 
-def collect(order, y, pieces, low, high, turned):
-    groups, rows, width, depth = sizes(pieces)
+def collect(order, y, pieces, low, high, turned, groups_first=False):
+    groups, rows, width, depth = sizes(pieces, groups_first)
     tokens = y.shape[2] if turned else y.shape[0]
     return call(
         functools.partial(collect_kernel, low, high, turned),
         (groups,),
         [lead(y.shape[1:]) if turned else column(tokens, width)]
-        + pair_specs(rows, width, PAIRS),
+        + piece_specs(pieces, groups_first),
         still((tokens, depth)),
         jax.ShapeDtypeStruct((tokens, depth), jnp.float32),
         [pltpu.VMEM((depth, width), jnp.bfloat16)],
@@ -846,9 +873,10 @@
         made = self.line(work, self.attended, self.stream, self.attn)
         self.branch_attn, self.middle, self.normed_mlp, self.inv_mlp, self.modulated_mlp = made
 
-    def mlp_up(self, up):
+    def mlp_up(self, up, groups_first):
         self.up = up
-        work = lambda rows, up: times_up(self.order, rows, up)
+        self.up_first = groups_first
+        work = lambda rows, up: times_up(self.order, rows, up, self.up_first)
         self.hidden_pre, self.hidden_act = self.line(work, self.modulated_mlp, up)
 
     def mlp_down(self, down, last):
@@ -885,7 +913,9 @@
         rows = self.modulation
 
         def work(d_pre, upstream, normed, inv_mlp, up):
-            d_mod_mlp = collect(self.order, d_pre, up, 0, self.width, False)
+            d_mod_mlp = collect(
+                self.order, d_pre, up, 0, self.width, False, self.up_first
+            )
             d_middle = upstream + norm_back(normed, inv_mlp, d_mod_mlp * (1.0 + rows[4]))
             return d_mod_mlp, d_middle, low(d_middle * rows[2])
 
@@ -990,6 +1020,9 @@
     cotangent = deal_rows(swap_blocks(out_cotangent.reshape(-1, width), own_frames, devices), FRAME)
     cotangent = swap_blocks(cotangent, devices, own_frames)
     line = Line()
+    up_one = MidGather(line, packed[0][1])
+    up_one.send()
+    line.tick()
     summed = line.exchange_sum(line.exchange_sum(partial_value, FRAME), CLIP)
     line.wait(cotangent)
     summed = lax.dynamic_index_in_dim(summed, lax.axis_index(CLIP), 0, keepdims=False)
@@ -997,54 +1030,52 @@
     modulations = placed.transpose(1, 2, 0, 3).reshape(summed.shape[:2] + (-1,))
 
     order = piece_order()
-    attn_one, up_one, down_one = (Gather(line, piece) for piece in packed[0])
+    attn_one, down_one = (Gather(line, piece) for piece in packed[0][::2])
     attn_two, up_two, down_two = (Gather(line, piece) for piece in packed[1])
     one = Layer(line, order, modulations[0], 0)
     two = Layer(line, order, modulations[1], own_places)
 
     line.wait(packed)
+    up_one.join()
+    line.wait(attn_one.whole)
     attn_one.send()
     line.tick()
     attn_one.relay()
-    up_one.send()
-    down_one.soon()
+    line.under_way.append(up_one.pair)
     line.tick()
     attn_one.end()
     up_one.relay()
-    down_one.send()
     frames_in = line.send(x_in.reshape(-1, width), lambda held: deal_rows(held, TENSOR))
     one.project(line(wide, frames_in), attn_one.pieces)
+    down_one.send()
     one.attend()
     one.attention_out()
-    attn_two.soon()
     line.tick()
     up_one.end()
     down_one.relay()
+    one.mlp_up(up_one.pieces, True)
+    cotangent = line(wide, cotangent)
     attn_two.send()
-    one.mlp_up(up_one.pieces)
-    cotangent = line(wide, cotangent)
-    up_two.soon()
     line.tick()
     down_one.end()
     attn_two.relay()
-    up_two.send()
-    down_two.soon()
     between = one.mlp_down(down_one.pieces, low)
     between = line.send(between, lambda held: deal_rows(held, (TENSOR, FRAME)))
     two.turn_back(cotangent)
+    up_two.send()
     line.tick()
     attn_two.end()
     up_two.relay()
-    down_two.send()
     two.share(two.d_branch_mlp)
     between = line(wide, between)
     two.project(between, attn_two.pieces)
+    down_two.send()
     two.attend()
     two.attention_out()
     line.tick()
     up_two.end()
     down_two.relay()
-    two.mlp_up(up_two.pieces)
+    two.mlp_up(up_two.pieces, False)
     two.share(two.hidden_act)
     down_grad = two.grad_down()
     line.tick()

time: 731 us -> 721 us (0.986)
    all_gather x6 -> x5, waiting for transfers between devices: 89.2 us -> 45.5 us  [__init__(): self.whole = lax.all_gather(piece, TENSOR, axis=0, tiled=False)]
    all_gather x0 -> x1, waiting for transfers between devices: none -> 32.1 us  [join(): self.pair = lax.all_gather(pair, TENSOR, axis=0, tiled=False)]
    all_to_all x6, waiting for transfers between devices: 27.5 us -> 43.4 us  [deal_rows(): return lax.all_to_all(rows, axes, split_axis=0, concat_axis=0, tiled=True)]
    ppermute x52, waiting for transfers between devices: 89.7 us -> 82.2 us  [hop(): return lax.ppermute(array, SHARDS, pairs)]
    another operation x6 -> x5, other arithmetic: 17.9 us -> 13 us  [relay(): self.pair = self.line(lambda *pair: jnp.stack(pair), self.whole, self.near)]
    unnamed x142 -> x152, local copies, waits for them, and re-layouts: 21.3 us -> 24.2 us
  transfers between devices with their start and end apart: 85 -> 85, of which waited for: 33 -> 34; matrix products, arithmetic and copies ran while one was open for 16% -> 16% of each run, Pallas kernels for 29% -> 29%
where the time goes in v5:
time: 721 us; the launch traced here: 712 us
  waiting for transfers between devices  267 us (37%)
  Pallas kernels  206 us (29%)
  other arithmetic  109 us (15%)
  starting transfers between devices  78.5 us (11%)
  local copies, waits for them, and re-layouts  30.8 us (4%)
  between operations  16 us (2%)
    pallas_call x26, Pallas kernels, call(): pl.pallas_call(kernel, out_shape=out_shape, grid_spec=pltpu.PrefetchScala...  206 us
    ppermute x52, waiting for transfers between devices, hop(): return lax.ppermute(array, SHARDS, pairs)  82.2 us
    ppermute x15, waiting for transfers between devices, flip(): return lax.ppermute(array, axis, [(i, i ^ bit) for i in range(count)])  49.8 us
    convert_element_type x21, other arithmetic, low(): return array.astype(jnp.bfloat16)  48.5 us
    all_gather x5, waiting for transfers between devices, __init__(): self.whole = lax.all_gather(piece, TENSOR, axis=0, tiled=False)  45.5 us
    all_to_all x6, waiting for transfers between devices, deal_rows(): return lax.all_to_all(rows, axes, split_axis=0, concat_axis=0, tiled=True)  43.4 us
    ppermute x52, starting transfers between devices, hop(): return lax.ppermute(array, SHARDS, pairs)  39.5 us
    all_gather x1, waiting for transfers between devices, join(): self.pair = lax.all_gather(pair, TENSOR, axis=0, tiled=False)  32.1 us
  transfers between devices with their start and end apart: 85, of which 34 were waited for; matrix products, arithmetic and copies ran while one was open for 16% of the time, Pallas kernels for 29%

profile of v5, /device:TPU:0, one launch (start us, length us, event | category | flops | bytes accessed | tf_op | source)
XLA Modules:
  0.0 712.0 jit_solution(1973959460137226949)
XLA Ops:
  44.0 8.3 %collective-permute-done.5 = f32[4,2,6,288]{3,2,1,0:T(8,128)S(1)} collective-permute-done((f32[4,2,6,288]{3,2,1,0:T(8,128)S(1)}, f32[4,2,6,288]{3,2,1,0:T(8,128)S(1)}, u32[]{:S(2)}, u32[]{:S(2)}) %collective-permute-start.5) | collective-permute-done | bytes 55328 | tf_op jit(solution)/shard_map/ppermute | solution.py:350
  55.7 16.5 %collective-permute-done.6 = bf16[4,144,1152]{2,1,0:T(8,128)(2,1)S(1)} collective-permute-done((bf16[4,144,1152]{2,1,0:T(8,128)(2,1)}, bf16[4,144,1152]{2,1,0:T(8,128)(2,1)S(1)}, u32[]{:S(2)}, u32[]{:S(2)}) %collective-permute-start.6) | collective-permute-done | bytes 1327136 | tf_op jit(solution)/shard_map/ppermute | solution.py:364
  76.8 32.1 %all-gather.16.cloned.1.call-done = bf16[8,144,1152]{2,1,0:T(8,128)(2,1)} async-done(((bf16[2,144,1152]{2,1,0:T(8,128)(2,1)}), bf16[8,144,1152]{2,1,0:T(8,128)(2,1)}) %all-gather.16.cloned.1.call-update) | async-done | bytes 2654224 | tf_op jit(solution)/shard_map/all_gather | solution.py:456
  115.6 17.0 %all-to-all-done.1 = bf16[4,64,1152]{2,1,0:T(8,128)(2,1)S(1)} async-done(((bf16[4,64,1152]{2,1,0:T(8,128)(2,1)}), bf16[4,64,1152]{2,1,0:T(8,128)(2,1)S(1)}, u32[]{:S(2)}, u32[]{:S(2)}) %all-to-all-start.1) | async-done | bytes 589856 | tf_op jit(solution)/shard_map/all_to_all | solution.py:977
  174.8 10.0 %shard_map.231 = (f32[256,4608]{1,0:T(8,128)}, bf16[256,4608]{1,0:T(8,128)(2,1)}) custom-call(s32[8]{0:T(128)S(1)} %stack.154.order_ref, bf16[256,1152]{1,0:T(8,128)(2,1)} %get-tuple-element.486.x_ref, bf16[4,2,144,1152]{3,2,1,0:T(8,128)(2,1)S(1)} %bitcast.161, bf16[4,2,144,1152]{3,2,1,0:T(8,128)(2,1)} %collective-permute-done.10.refs_1_, ...), custom_call_target="tpu_custom_call" | custom-call | flops 339738624 | bytes 2285572 | tf_op jit(solution)/shard_map/pallas_call | solution.py:653
  186.0 15.4 %all-gather.20.cloned.1.call-done = bf16[576,1152]{1,0:T(8,128)(2,1)} async-done(((bf16[144,1152]{1,0:T(8,128)(2,1)}), bf16[576,1152]{1,0:T(8,128)(2,1)}) %all-gather.20.cloned.1.call-update) | async-done | bytes 1327120 | tf_op jit(solution)/shard_map/all_gather | solution.py:430
  207.2 12.3 %collective-permute-done.16 = bf16[4,144,1152]{2,1,0:T(8,128)(2,1)} collective-permute-done((bf16[4,144,1152]{2,1,0:T(8,128)(2,1)}, bf16[4,144,1152]{2,1,0:T(8,128)(2,1)}, u32[]{:S(2)}, u32[]{:S(2)}) %collective-permute-start.16) | collective-permute-done | bytes 1327136 | tf_op jit(solution)/shard_map/ppermute | solution.py:364
  224.9 8.6 %shard_map.232 = f32[256,1152]{1,0:T(8,128)S(1)} custom-call(s32[8]{0:T(128)S(1)} %stack.154.order_ref, bf16[256,4608]{1,0:T(8,128)(2,1)} %get-tuple-element.466.y_ref, bf16[2,4,144,1152]{3,2,1,0:T(8,128)(2,1)} %pad_maximum_fusion.1.refs_0_, bf16[2,4,144,1152]{3,2,1,0:T(8,128)(2,1)} %collective-permute-done.14.refs_1_, ...), custom_call_target="tpu_custom_call" | custom-call | flops 339738624 | bytes 1769476 | tf_op jit(solution)/shard_map/pallas_call | solution.py:653
  236.3 15.6 %all-gather.22.cloned.1.call-done = bf16[576,1152]{1,0:T(8,128)(2,1)} async-done(((bf16[144,1152]{1,0:T(8,128)(2,1)}), bf16[576,1152]{1,0:T(8,128)(2,1)}) %all-gather.22.cloned.1.call-update) | async-done | bytes 1327120 | tf_op jit(solution)/shard_map/all_gather | solution.py:430
  257.6 18.2 %all-to-all-done.2 = bf16[16,16,1152]{2,1,0:T(8,128)(2,1)} async-done(((bf16[16,16,1152]{2,1,0:T(8,128)(2,1)}), bf16[16,16,1152]{2,1,0:T(8,128)(2,1)}, u32[]{:S(2)}, u32[]{:S(2)}) %all-to-all-start.2) | async-done | bytes 589856 | tf_op jit(solution)/shard_map/all_to_all | solution.py:977
  298.5 10.0 %all-gather.24.cloned.1.call-done = bf16[576,1152]{1,0:T(8,128)(2,1)} async-done(((bf16[144,1152]{1,0:T(8,128)(2,1)}), bf16[576,1152]{1,0:T(8,128)(2,1)}) %all-gather.24.cloned.1.call-update) | async-done | bytes 1327120 | tf_op jit(solution)/shard_map/all_gather | solution.py:430
  333.2 9.3 %shard_map.236 = (f32[256,4608]{1,0:T(8,128)}, bf16[256,4608]{1,0:T(8,128)(2,1)S(1)}) custom-call(s32[8]{0:T(128)S(1)} %stack.154.order_ref, bf16[256,1152]{1,0:T(8,128)(2,1)S(1)} %get-tuple-element.407.x_ref, bf16[2,4,144,1152]{3,2,1,0:T(8,128)(2,1)} %pad_maximum_fusion.3.refs_0_, bf16[2,4,144,1152]{3,2,1,0:T(8,128)(2,1)} %collective-permute-done.22.refs_1_, ...), custom_call_target="tpu_custom_call" | custom-call | flops 339738624 | bytes 2285572 | tf_op jit(solution)/shard_map/pallas_call | solution.py:653
  365.7 9.1 %shard_map.238.y_ref = bf16[256,4608]{1,0:T(8,128)(2,1)S(1)} custom-call(s32[8]{0:T(128)S(1)} %stack.154.order_ref, bf16[256,1152]{1,0:T(8,128)(2,1)} %multiply_convert_fusion.3.x_ref, f32[256,4608]{1,0:T(8,128)} %get-tuple-element.391.pre_ref, bf16[2,4,144,1152]{3,2,1,0:T(8,128)(2,1)S(1)} %pad_maximum_fusion.4.refs_0_, ...), custom_call_target="tpu_custom_call" | custom-call | flops 339738624 | bytes 2285572 | tf_op jit(solution)/shard_map/pallas_call | solution.py:653
  405.4 9.3 %shard_map.242.y_ref.refs_4_ = bf16[4,864,256]{2,1,0:T(8,128)(2,1)} custom-call(bf16[4,864,256]{2,1,0:T(8,128)(2,1)S(1)} %copy-done.7, bf16[4,288,256]{2,1,0:T(8,128)(2,1)S(1)} %shard_map.241.upstream_ref), custom_call_target="tpu_custom_call" | custom-call | flops 94371840 | bytes 516096 | tf_op jit(solution)/shard_map/pallas_call | solution.py:653
  433.5 9.9 %shard_map.244 = (bf16[2,4,144,1152]{3,2,1,0:T(8,128)(2,1)}, bf16[2,4,144,1152]{3,2,1,0:T(8,128)(2,1)}) custom-call(s32[8]{0:T(128)S(1)} %stack.154.order_ref, bf16[256,1152]{1,0:T(8,128)(2,1)S(1)} %copy-done.18, bf16[256,1152]{1,0:T(8,128)(2,1)S(1)} %copy-done.25, bf16[256,1152]{1,0:T(8,128)(2,1)} %multiply_convert_fusion.2.x_ref.refs_2_, ...), custom_call_target="tpu_custom_call" | custom-call | flops 339738624 | bytes 1548292 | tf_op jit(solution)/shard_map/pallas_call | solution.py:653
  457.0 10.2 %shard_map.245.y_ref = bf16[256,4608]{1,0:T(8,128)(2,1)} custom-call(s32[8]{0:T(128)S(1)} %stack.154.order_ref, bf16[256,1152]{1,0:T(8,128)(2,1)S(1)} %multiply_convert_fusion.1.x_ref, f32[256,4608]{1,0:T(8,128)} %get-tuple-element.455.pre_ref, bf16[2,4,144,1152]{3,2,1,0:T(8,128)(2,1)} %pad_maximum_fusion.1.refs_0_, ...), custom_call_target="tpu_custom_call" | custom-call | flops 339738624 | bytes 2285572 | tf_op jit(solution)/shard_map/pallas_call | solution.py:653
  502.2 8.2 %shard_map.247 = f32[256,1152]{1,0:T(8,128)S(1)} custom-call(s32[8]{0:T(128)S(1)} %stack.154.order_ref, bf16[256,4608]{1,0:T(8,128)(2,1)} %shard_map.245.y_ref, bf16[4,2,144,1152]{3,2,1,0:T(8,128)(2,1)S(1)} %bitcast.162, bf16[4,2,144,1152]{3,2,1,0:T(8,128)(2,1)} %collective-permute-done.10.refs_1_, ...), custom_call_target="tpu_custom_call" | custom-call | flops 339738624 | bytes 1769476 | tf_op jit(solution)/shard_map/pallas_call | solution.py:653
  514.4 8.4 %shard_map.248 = (bf16[2,4,144,1152]{3,2,1,0:T(8,128)(2,1)}, bf16[2,4,144,1152]{3,2,1,0:T(8,128)(2,1)}) custom-call(s32[8]{0:T(128)S(1)} %stack.154.order_ref, bf16[256,1152]{1,0:T(8,128)(2,1)} %get-tuple-element.486.x_ref, bf16[256,1152]{1,0:T(8,128)(2,1)} %collective-permute-done.45.x_other, bf16[256,4608]{1,0:T(8,128)(2,1)} %shard_map.245.y_ref, ...), custom_call_target="tpu_custom_call" | custom-call | flops 339738624 | bytes 1400836 | tf_op jit(solution)/shard_map/pallas_call | solution.py:653
  530.9 9.2 %shard_map.250.y_ref.refs_4_ = bf16[4,864,256]{2,1,0:T(8,128)(2,1)} custom-call(bf16[4,864,256]{2,1,0:T(8,128)(2,1)S(1)} %copy-done.4, bf16[4,288,256]{2,1,0:T(8,128)(2,1)S(1)} %shard_map.249.upstream_ref), custom_call_target="tpu_custom_call" | custom-call | flops 94371840 | bytes 516096 | tf_op jit(solution)/shard_map/pallas_call | solution.py:653
  568.2 9.8 %shard_map.253 = (bf16[2,4,144,1152]{3,2,1,0:T(8,128)(2,1)}, bf16[2,4,144,1152]{3,2,1,0:T(8,128)(2,1)}) custom-call(s32[8]{0:T(128)S(1)} %stack.154.order_ref, bf16[256,1152]{1,0:T(8,128)(2,1)S(1)} %get-tuple-element.526.x_ref.refs_0_, bf16[256,1152]{1,0:T(8,128)(2,1)} %collective-permute-done.49.refs_1_, ...), custom_call_target="tpu_custom_call" | custom-call | flops 339738624 | bytes 1548292 | tf_op jit(solution)/shard_map/pallas_call | solution.py:653
  595.1 16.0 %collective-permute-done.58 = f32[2,6,1152]{2,1,0:T(8,128)S(1)} collective-permute-done((f32[2,6,1152]{2,1,0:T(8,128)S(1)}, f32[2,6,1152]{2,1,0:T(8,128)S(1)}, u32[]{:S(2)}, u32[]{:S(2)}) %collective-permute-start.58) | collective-permute-done | bytes 55328 | tf_op jit(solution)/shard_map/ppermute | solution.py:350
  611.2 10.1 %collective-permute-done.59 = f32[2,6,1152]{2,1,0:T(8,128)S(1)} collective-permute-done((f32[2,6,1152]{2,1,0:T(8,128)S(1)}, f32[2,6,1152]{2,1,0:T(8,128)S(1)}, u32[]{:S(2)}, u32[]{:S(2)}) %collective-permute-start.59) | collective-permute-done | bytes 55328 | tf_op jit(solution)/shard_map/ppermute | solution.py:350
  635.2 12.0 %collective-permute-done.60 = bf16[4,144,1152]{2,1,0:T(8,128)(2,1)} collective-permute-done((bf16[4,144,1152]{2,1,0:T(8,128)(2,1)}, bf16[4,144,1152]{2,1,0:T(8,128)(2,1)}, u32[]{:S(2)}, u32[]{:S(2)}) %collective-permute-start.60) | collective-permute-done | bytes 1327136 | tf_op jit(solution)/shard_map/ppermute | solution.py:364
  687.9 12.8 %reduce-scatter.7.cloned.1.call-done = bf16[1,144,1152]{2,1,0:T(8,128)(2,1)} async-done(((bf16[4,144,1152]{2,1,0:T(8,128)(2,1)}), bf16[1,144,1152]{2,1,0:T(8,128)(2,1)}) %reduce-scatter.7.cloned.1.call-update) | async-done | bytes 331792 | tf_op jit(solution)/shard_map/reduce_scatter | solution.py:492
  (498 shorter events, 397.6 us)
Async XLA Ops:
  7.2 47.0 %all-gather.14.cloned.1.call-start = ((), (), s32[]{:S(2)}) async-start(), calls=%async_computation.18 | async-start | bytes 1658880 | tf_op jit(solution)/shard_map/all_gather | solution.py:430
  25.3 83.6 %all-gather.16.cloned.1.call-start = ((), (), s32[]{:S(2)}) async-start(), calls=%async_computation.19 | async-start | bytes 3317760 | tf_op jit(solution)/shard_map/all_gather | solution.py:456
  112.4 38.6 %all-gather.18.cloned.1.call-start = ((), (), s32[]{:S(2)}) async-start(), calls=%async_computation.20 | async-start | bytes 1658880 | tf_op jit(solution)/shard_map/all_gather | solution.py:430
  113.2 88.2 %all-gather.20.cloned.1.call-start = ((), (), s32[]{:S(2)}) async-start(), calls=%async_computation.21 | async-start | bytes 1658880 | tf_op jit(solution)/shard_map/all_gather | solution.py:430
  113.9 53.3 %collective-permute-start.10 = (bf16[4,2,144,1152]{3,2,1,0:T(8,128)(2,1)}, bf16[4,2,144,1152]{3,2,1,0:T(8,128)(2,1)}, u32[]{:S(2)}, u32[]{:S(2)}) collective-permute-start(bf16[4,2,144,1152]{3,2,1,0:T(8,128)(2,1)} %bitcast.159), channel_id=1, source_target_pairs={{0,16},{4,12},{8,24},{12,4},{16,0},{20,28},{24,8},{28,20},{1,17},{... | collective-permute-start | bytes 7962632 | tf_op jit(solution)/shard_map/ppermute | solution.py:364
  115.4 51.8 %collective-permute-start.11 = (bf16[4,2,144,1152]{3,2,1,0:T(8,128)(2,1)}, bf16[4,2,144,1152]{3,2,1,0:T(8,128)(2,1)}, u32[]{:S(2)}, u32[]{:S(2)}) collective-permute-start(bf16[4,2,144,1152]{3,2,1,0:T(8,128)(2,1)} %bitcast.160), channel_id=1, source_target_pairs={{0,4},{4,0},{8,12},{12,8},{16,20},{20,16},{24,28},{28,24},{1,5},{5... | collective-permute-start | bytes 7962632 | tf_op jit(solution)/shard_map/ppermute | solution.py:364
  169.1 82.7 %all-gather.22.cloned.1.call-start = ((), (), s32[]{:S(2)}) async-start(), calls=%async_computation.22 | async-start | bytes 1658880 | tf_op jit(solution)/shard_map/all_gather | solution.py:430
  257.6 51.0 %all-gather.24.cloned.1.call-start = ((), (), s32[]{:S(2)}) async-start(), calls=%async_computation.23 | async-start | bytes 1658880 | tf_op jit(solution)/shard_map/all_gather | solution.py:430
  280.0 44.7 %collective-permute-start.22 = (bf16[2,4,144,1152]{3,2,1,0:T(8,128)(2,1)}, bf16[2,4,144,1152]{3,2,1,0:T(8,128)(2,1)}, u32[]{:S(2)}, u32[]{:S(2)}) collective-permute-start(bf16[2,4,144,1152]{3,2,1,0:T(8,128)(2,1)} %pad_maximum_fusion.3.refs_0_), channel_id=1, source_target_pairs={{0,16},{4,12},{8,24},{12,4},{16,0},{20,28},{24,8},{28,20},{1,17},{... | collective-permute-start | bytes 7962632 | tf_op jit(solution)/shard_map/ppermute | solution.py:364
  281.5 43.3 %collective-permute-start.23 = (bf16[2,4,144,1152]{3,2,1,0:T(8,128)(2,1)}, bf16[2,4,144,1152]{3,2,1,0:T(8,128)(2,1)}, u32[]{:S(2)}, u32[]{:S(2)}) collective-permute-start(bf16[2,4,144,1152]{3,2,1,0:T(8,128)(2,1)} %pad_maximum_fusion.3.refs_0_), channel_id=1, source_target_pairs={{0,4},{4,0},{8,12},{12,8},{16,20},{20,16},{24,28},{28,24},{1,5},{5... | collective-permute-start | bytes 7962632 | tf_op jit(solution)/shard_map/ppermute | solution.py:364
  284.1 40.7 %collective-permute-start.24 = (bf16[256,1152]{1,0:T(8,128)(2,1)}, bf16[256,1152]{1,0:T(8,128)(2,1)}, u32[]{:S(2)}, u32[]{:S(2)}) collective-permute-start(bf16[256,1152]{1,0:T(8,128)(2,1)} %multiply_convert_fusion.3.x_ref), channel_id=1, source_target_pairs={{0,4},{4,0},{8,12},{12,8},{16,20},{20,16},{24,28},{28,24},{1,5},{5... | collective-permute-start | bytes 1769480 | tf_op jit(solution)/shard_map/ppermute | solution.py:364
  394.1 50.0 %collective-permute-start.35 = (bf16[2,4,144,1152]{3,2,1,0:T(8,128)(2,1)}, bf16[2,4,144,1152]{3,2,1,0:T(8,128)(2,1)}, u32[]{:S(2)}, u32[]{:S(2)}) collective-permute-start(bf16[2,4,144,1152]{3,2,1,0:T(8,128)(2,1)} %get-tuple-element.432), channel_id=1, source_target_pairs={{0,16},{4,12},{8,24},{12,4},{16,0},{20,28},{24,8},{28,20},{1,17},{... | collective-permute-start | bytes 7962632 | tf_op jit(solution)/shard_map/ppermute | solution.py:364
  431.3 228.7 %reduce-scatter.17.cloned.1.call-start = ((), (), s32[]{:S(2)}) async-start(), calls=%async_computation.17 | async-start | bytes 1658880 | tf_op jit(solution)/shard_map/reduce_scatter | solution.py:492
  443.4 46.5 %collective-permute-start.41 = (bf16[2,4,144,1152]{3,2,1,0:T(8,128)(2,1)}, bf16[2,4,144,1152]{3,2,1,0:T(8,128)(2,1)}, u32[]{:S(2)}, u32[]{:S(2)}) collective-permute-start(bf16[2,4,144,1152]{3,2,1,0:T(8,128)(2,1)} %get-tuple-element.461), channel_id=1, source_target_pairs={{0,16},{4,12},{8,24},{12,4},{16,0},{20,28},{24,8},{28,20},{1,17},{... | collective-permute-start | bytes 7962632 | tf_op jit(solution)/shard_map/ppermute | solution.py:364
  454.9 214.4 %reduce-scatter.15.cloned.1.call-start = ((), (), s32[]{:S(2)}) async-start(), calls=%async_computation.16 | async-start | bytes 1658880 | tf_op jit(solution)/shard_map/reduce_scatter | solution.py:492
  490.0 50.2 %collective-permute-start.48 = (bf16[2,4,144,1152]{3,2,1,0:T(8,128)(2,1)}, bf16[2,4,144,1152]{3,2,1,0:T(8,128)(2,1)}, u32[]{:S(2)}, u32[]{:S(2)}) collective-permute-start(bf16[2,4,144,1152]{3,2,1,0:T(8,128)(2,1)} %get-tuple-element.500), channel_id=1, source_target_pairs={{0,16},{4,12},{8,24},{12,4},{16,0},{20,28},{24,8},{28,20},{1,17},{... | collective-permute-start | bytes 7962632 | tf_op jit(solution)/shard_map/ppermute | solution.py:364
  494.9 45.3 %collective-permute-start.49 = (bf16[256,1152]{1,0:T(8,128)(2,1)S(1)}, bf16[256,1152]{1,0:T(8,128)(2,1)}, u32[]{:S(2)}, u32[]{:S(2)}) collective-permute-start(bf16[256,1152]{1,0:T(8,128)(2,1)S(1)} %get-tuple-element.526.x_ref.refs_0_), channel_id=1, source_target_pairs={{0,4},{4,0},{8,12},{12,8},{16,20},{20,16},{24,28},{28,24},{1,5},{5... | collective-permute-start | bytes 1769480 | tf_op jit(solution)/shard_map/ppermute | solution.py:364
  498.7 41.4 %collective-permute-start.47 = (bf16[4,144,1152]{2,1,0:T(8,128)(2,1)}, bf16[4,144,1152]{2,1,0:T(8,128)(2,1)}, u32[]{:S(2)}, u32[]{:S(2)}) collective-permute-start(bf16[4,144,1152]{2,1,0:T(8,128)(2,1)} %fusion.12), channel_id=1, source_target_pairs={{0,8},{4,20},{8,0},{12,28},{16,24},{20,4},{24,16},{28,12},{1,9},{5... | collective-permute-start | bytes 3981320 | tf_op jit(solution)/shard_map/ppermute | solution.py:364
  500.3 176.4 %reduce-scatter.13.cloned.1.call-start = ((), (), s32[]{:S(2)}) async-start(), calls=%async_computation.15 | async-start | bytes 1658880 | tf_op jit(solution)/shard_map/reduce_scatter | solution.py:492
  529.3 55.0 %collective-permute-start.50 = (bf16[2,4,144,1152]{3,2,1,0:T(8,128)(2,1)}, bf16[2,4,144,1152]{3,2,1,0:T(8,128)(2,1)}, u32[]{:S(2)}, u32[]{:S(2)}) collective-permute-start(bf16[2,4,144,1152]{3,2,1,0:T(8,128)(2,1)} %get-tuple-element.521), channel_id=1, source_target_pairs={{0,16},{4,12},{8,24},{12,4},{16,0},{20,28},{24,8},{28,20},{1,17},{... | collective-permute-start | bytes 7962632 | tf_op jit(solution)/shard_map/ppermute | solution.py:364
  546.8 37.4 %collective-permute-start.55 = (bf16[4,144,1152]{2,1,0:T(8,128)(2,1)}, bf16[4,144,1152]{2,1,0:T(8,128)(2,1)}, u32[]{:S(2)}, u32[]{:S(2)}) collective-permute-start(bf16[4,144,1152]{2,1,0:T(8,128)(2,1)} %fusion.13), channel_id=1, source_target_pairs={{0,8},{4,20},{8,0},{12,28},{16,24},{20,4},{24,16},{28,12},{1,9},{5... | collective-permute-start | bytes 3981320 | tf_op jit(solution)/shard_map/ppermute | solution.py:364
  578.0 46.4 %collective-permute-start.57 = (bf16[2,4,144,1152]{3,2,1,0:T(8,128)(2,1)}, bf16[2,4,144,1152]{3,2,1,0:T(8,128)(2,1)S(1)}, u32[]{:S(2)}, u32[]{:S(2)}) collective-permute-start(bf16[2,4,144,1152]{3,2,1,0:T(8,128)(2,1)} %get-tuple-element.542), channel_id=1, source_target_pairs={{0,16},{4,12},{8,24},{12,4},{16,0},{20,28},{24,8},{28,20},{1,17},{... | collective-permute-start | bytes 7962632 | tf_op jit(solution)/shard_map/ppermute | solution.py:364
  584.2 98.3 %reduce-scatter.11.cloned.1.call-start = ((), (), s32[]{:S(2)}) async-start(), calls=%async_computation.14 | async-start | bytes 1658880 | tf_op jit(solution)/shard_map/reduce_scatter | solution.py:492
  592.0 94.0 %reduce-scatter.9.cloned.1.call-start = ((), (), s32[]{:S(2)}) async-start(), calls=%async_computation.13 | async-start | bytes 1658880 | tf_op jit(solution)/shard_map/reduce_scatter | solution.py:492
  (136 other events, 1507.4 us)
Sparse Core Ops, SparseCore 0:
  14.1 37.8 all-gather.13
  55.8 53.0 all-gather.15
  115.4 35.5 all-gather.17
  169.2 32.1 all-gather.19
  219.8 32.0 all-gather.21
  276.2 32.2 all-gather.23
  455.0 31.0 reduce-scatter.16
  500.5 31.6 reduce-scatter.14
  547.3 31.8 reduce-scatter.12
  592.2 33.9 reduce-scatter.10
  634.2 31.6 reduce-scatter.8
  669.1 31.5 reduce-scatter.6

commit v6 on v5

--- a/solution.py
+++ b/solution.py
@@ -1026,25 +1026,25 @@
     summed = line.exchange_sum(line.exchange_sum(partial_value, FRAME), CLIP)
     line.wait(cotangent)
     summed = lax.dynamic_index_in_dim(summed, lax.axis_index(CLIP), 0, keepdims=False)
-    placed = line.place_along(summed, TENSOR)
-    modulations = placed.transpose(1, 2, 0, 3).reshape(summed.shape[:2] + (-1,))
-
     order = piece_order()
     attn_one, down_one = (Gather(line, piece) for piece in packed[0][::2])
     attn_two, up_two, down_two = (Gather(line, piece) for piece in packed[1])
-    one = Layer(line, order, modulations[0], 0)
-    two = Layer(line, order, modulations[1], own_places)
-
     line.wait(packed)
     up_one.join()
     line.wait(attn_one.whole)
     attn_one.send()
+    placed = line.place_along(summed, TENSOR)
+    modulations = placed.transpose(1, 2, 0, 3).reshape(summed.shape[:2] + (-1,))
+
     line.tick()
     attn_one.relay()
     line.under_way.append(up_one.pair)
     line.tick()
     attn_one.end()
     up_one.relay()
+    one = Layer(line, order, modulations[0], 0)
+    two = Layer(line, order, modulations[1], own_places)
+
     frames_in = line.send(x_in.reshape(-1, width), lambda held: deal_rows(held, TENSOR))
     one.project(line(wide, frames_in), attn_one.pieces)
     down_one.send()

time: 721 us -> 715 us (level)
    ppermute x52, waiting for transfers between devices: 82.2 us -> 70.6 us  [hop(): return lax.ppermute(array, SHARDS, pairs)]
    all_gather x5, waiting for transfers between devices: 45.5 us -> 53.7 us  [__init__(): self.whole = lax.all_gather(piece, TENSOR, axis=0, tiled=False)]
    unnamed x152 -> x150, local copies, waits for them, and re-layouts: 24.2 us -> 24.1 us
  transfers between devices with their start and end apart: 85 -> 85, of which waited for: 34 -> 35; matrix products, arithmetic and copies ran while one was open for 16% -> 16% of each run, Pallas kernels for 29% -> 29%
where the time goes in v6:
time: 715 us; the launch traced here: 706 us
  waiting for transfers between devices  261 us (37%)
  Pallas kernels  206 us (29%)
  other arithmetic  109 us (15%)
  starting transfers between devices  79.2 us (11%)
  local copies, waits for them, and re-layouts  30.7 us (4%)
  between operations  16 us (2%)
    pallas_call x26, Pallas kernels, call(): pl.pallas_call(kernel, out_shape=out_shape, grid_spec=pltpu.PrefetchScala...  206 us
    ppermute x52, waiting for transfers between devices, hop(): return lax.ppermute(array, SHARDS, pairs)  70.6 us
    all_gather x5, waiting for transfers between devices, __init__(): self.whole = lax.all_gather(piece, TENSOR, axis=0, tiled=False)  53.7 us
    convert_element_type x21, other arithmetic, low(): return array.astype(jnp.bfloat16)  48.5 us
    all_to_all x6, waiting for transfers between devices, deal_rows(): return lax.all_to_all(rows, axes, split_axis=0, concat_axis=0, tiled=True)  45.1 us
    ppermute x15, waiting for transfers between devices, flip(): return lax.ppermute(array, axis, [(i, i ^ bit) for i in range(count)])  43.1 us
    ppermute x52, starting transfers between devices, hop(): return lax.ppermute(array, SHARDS, pairs)  39.6 us
    all_gather x1, waiting for transfers between devices, join(): self.pair = lax.all_gather(pair, TENSOR, axis=0, tiled=False)  33.9 us
  transfers between devices with their start and end apart: 85, of which 35 were waited for; matrix products, arithmetic and copies ran while one was open for 16% of the time, Pallas kernels for 29%

profile of v6, /device:TPU:0, one launch (start us, length us, event | category | flops | bytes accessed | tf_op | source)
XLA Modules:
  0.0 706.3 jit_solution(8034613492747165609)
XLA Ops:
  38.6 8.2 %all-gather.14.cloned.1.call-done = bf16[576,1152]{1,0:T(8,128)(2,1)} async-done(((bf16[144,1152]{1,0:T(8,128)(2,1)}), bf16[576,1152]{1,0:T(8,128)(2,1)}) %all-gather.14.cloned.1.call-update) | async-done | bytes 1327120 | tf_op jit(solution)/shard_map/all_gather | solution.py:430
  69.4 33.9 %all-gather.16.cloned.1.call-done = bf16[8,144,1152]{2,1,0:T(8,128)(2,1)} async-done(((bf16[2,144,1152]{2,1,0:T(8,128)(2,1)}), bf16[8,144,1152]{2,1,0:T(8,128)(2,1)}) %all-gather.16.cloned.1.call-update) | async-done | bytes 2654224 | tf_op jit(solution)/shard_map/all_gather | solution.py:456
  110.1 17.0 %all-to-all-done.1 = bf16[4,64,1152]{2,1,0:T(8,128)(2,1)S(1)} async-done(((bf16[4,64,1152]{2,1,0:T(8,128)(2,1)}), bf16[4,64,1152]{2,1,0:T(8,128)(2,1)S(1)}, u32[]{:S(2)}, u32[]{:S(2)}) %all-to-all-start.1) | async-done | bytes 589856 | tf_op jit(solution)/shard_map/all_to_all | solution.py:977
  169.2 10.0 %shard_map.231 = (f32[256,4608]{1,0:T(8,128)}, bf16[256,4608]{1,0:T(8,128)(2,1)}) custom-call(s32[8]{0:T(128)S(1)} %stack.154.order_ref, bf16[256,1152]{1,0:T(8,128)(2,1)} %get-tuple-element.486.x_ref, bf16[4,2,144,1152]{3,2,1,0:T(8,128)(2,1)S(1)} %bitcast.161, bf16[4,2,144,1152]{3,2,1,0:T(8,128)(2,1)} %collective-permute-done.10.refs_1_, ...), custom_call_target="tpu_custom_call" | custom-call | flops 339738624 | bytes 2285572 | tf_op jit(solution)/shard_map/pallas_call | solution.py:653
  180.3 15.5 %all-gather.20.cloned.1.call-done = bf16[576,1152]{1,0:T(8,128)(2,1)} async-done(((bf16[144,1152]{1,0:T(8,128)(2,1)}), bf16[576,1152]{1,0:T(8,128)(2,1)}) %all-gather.20.cloned.1.call-update) | async-done | bytes 1327120 | tf_op jit(solution)/shard_map/all_gather | solution.py:430
  201.7 12.3 %collective-permute-done.16 = bf16[4,144,1152]{2,1,0:T(8,128)(2,1)} collective-permute-done((bf16[4,144,1152]{2,1,0:T(8,128)(2,1)}, bf16[4,144,1152]{2,1,0:T(8,128)(2,1)}, u32[]{:S(2)}, u32[]{:S(2)}) %collective-permute-start.16) | collective-permute-done | bytes 1327136 | tf_op jit(solution)/shard_map/ppermute | solution.py:364
  219.3 8.6 %shard_map.232 = f32[256,1152]{1,0:T(8,128)S(1)} custom-call(s32[8]{0:T(128)S(1)} %stack.154.order_ref, bf16[256,4608]{1,0:T(8,128)(2,1)} %get-tuple-element.466.y_ref, bf16[2,4,144,1152]{3,2,1,0:T(8,128)(2,1)} %pad_maximum_fusion.1.refs_0_, bf16[2,4,144,1152]{3,2,1,0:T(8,128)(2,1)} %collective-permute-done.14.refs_1_, ...), custom_call_target="tpu_custom_call" | custom-call | flops 339738624 | bytes 1769476 | tf_op jit(solution)/shard_map/pallas_call | solution.py:653
  230.7 15.5 %all-gather.22.cloned.1.call-done = bf16[576,1152]{1,0:T(8,128)(2,1)} async-done(((bf16[144,1152]{1,0:T(8,128)(2,1)}), bf16[576,1152]{1,0:T(8,128)(2,1)}) %all-gather.22.cloned.1.call-update) | async-done | bytes 1327120 | tf_op jit(solution)/shard_map/all_gather | solution.py:430
  252.0 18.2 %all-to-all-done.2 = bf16[16,16,1152]{2,1,0:T(8,128)(2,1)} async-done(((bf16[16,16,1152]{2,1,0:T(8,128)(2,1)}), bf16[16,16,1152]{2,1,0:T(8,128)(2,1)}, u32[]{:S(2)}, u32[]{:S(2)}) %all-to-all-start.2) | async-done | bytes 589856 | tf_op jit(solution)/shard_map/all_to_all | solution.py:977
  292.9 10.0 %all-gather.24.cloned.1.call-done = bf16[576,1152]{1,0:T(8,128)(2,1)} async-done(((bf16[144,1152]{1,0:T(8,128)(2,1)}), bf16[576,1152]{1,0:T(8,128)(2,1)}) %all-gather.24.cloned.1.call-update) | async-done | bytes 1327120 | tf_op jit(solution)/shard_map/all_gather | solution.py:430
  327.6 9.3 %shard_map.236 = (f32[256,4608]{1,0:T(8,128)}, bf16[256,4608]{1,0:T(8,128)(2,1)S(1)}) custom-call(s32[8]{0:T(128)S(1)} %stack.154.order_ref, bf16[256,1152]{1,0:T(8,128)(2,1)S(1)} %get-tuple-element.407.x_ref, bf16[2,4,144,1152]{3,2,1,0:T(8,128)(2,1)} %pad_maximum_fusion.3.refs_0_, bf16[2,4,144,1152]{3,2,1,0:T(8,128)(2,1)} %collective-permute-done.22.refs_1_, ...), custom_call_target="tpu_custom_call" | custom-call | flops 339738624 | bytes 2285572 | tf_op jit(solution)/shard_map/pallas_call | solution.py:653
  360.1 9.0 %shard_map.238.y_ref = bf16[256,4608]{1,0:T(8,128)(2,1)S(1)} custom-call(s32[8]{0:T(128)S(1)} %stack.154.order_ref, bf16[256,1152]{1,0:T(8,128)(2,1)} %multiply_convert_fusion.3.x_ref, f32[256,4608]{1,0:T(8,128)} %get-tuple-element.391.pre_ref, bf16[2,4,144,1152]{3,2,1,0:T(8,128)(2,1)S(1)} %pad_maximum_fusion.4.refs_0_, ...), custom_call_target="tpu_custom_call" | custom-call | flops 339738624 | bytes 2285572 | tf_op jit(solution)/shard_map/pallas_call | solution.py:653
  399.8 9.3 %shard_map.242.y_ref.refs_4_ = bf16[4,864,256]{2,1,0:T(8,128)(2,1)} custom-call(bf16[4,864,256]{2,1,0:T(8,128)(2,1)S(1)} %copy-done.7, bf16[4,288,256]{2,1,0:T(8,128)(2,1)S(1)} %shard_map.241.upstream_ref), custom_call_target="tpu_custom_call" | custom-call | flops 94371840 | bytes 516096 | tf_op jit(solution)/shard_map/pallas_call | solution.py:653
  427.9 9.9 %shard_map.244 = (bf16[2,4,144,1152]{3,2,1,0:T(8,128)(2,1)}, bf16[2,4,144,1152]{3,2,1,0:T(8,128)(2,1)}) custom-call(s32[8]{0:T(128)S(1)} %stack.154.order_ref, bf16[256,1152]{1,0:T(8,128)(2,1)S(1)} %copy-done.18, bf16[256,1152]{1,0:T(8,128)(2,1)S(1)} %copy-done.25, bf16[256,1152]{1,0:T(8,128)(2,1)} %multiply_convert_fusion.2.x_ref.refs_2_, ...), custom_call_target="tpu_custom_call" | custom-call | flops 339738624 | bytes 1548292 | tf_op jit(solution)/shard_map/pallas_call | solution.py:653
  451.4 10.2 %shard_map.245.y_ref = bf16[256,4608]{1,0:T(8,128)(2,1)} custom-call(s32[8]{0:T(128)S(1)} %stack.154.order_ref, bf16[256,1152]{1,0:T(8,128)(2,1)S(1)} %multiply_convert_fusion.1.x_ref, f32[256,4608]{1,0:T(8,128)} %get-tuple-element.455.pre_ref, bf16[2,4,144,1152]{3,2,1,0:T(8,128)(2,1)} %pad_maximum_fusion.1.refs_0_, ...), custom_call_target="tpu_custom_call" | custom-call | flops 339738624 | bytes 2285572 | tf_op jit(solution)/shard_map/pallas_call | solution.py:653
  461.7 8.2 %shard_map.246 = (bf16[2,4,144,1152]{3,2,1,0:T(8,128)(2,1)}, bf16[2,4,144,1152]{3,2,1,0:T(8,128)(2,1)}) custom-call(s32[8]{0:T(128)S(1)} %stack.154.order_ref, bf16[256,1152]{1,0:T(8,128)(2,1)S(1)} %multiply_convert_fusion.1.x_ref, bf16[256,1152]{1,0:T(8,128)(2,1)S(1)} %collective-permute-done.42.x_other, bf16[256,4608]{1,0:T(8,128)(2,1)} %get-tuple-element.466.y_ref, ...), custom_call_target="tpu_custom_call" | custom-call | flops 339738624 | bytes 1400836 | tf_op jit(solution)/shard_map/pallas_call | solution.py:653
  496.5 8.3 %shard_map.247 = f32[256,1152]{1,0:T(8,128)S(1)} custom-call(s32[8]{0:T(128)S(1)} %stack.154.order_ref, bf16[256,4608]{1,0:T(8,128)(2,1)} %shard_map.245.y_ref, bf16[4,2,144,1152]{3,2,1,0:T(8,128)(2,1)S(1)} %bitcast.162, bf16[4,2,144,1152]{3,2,1,0:T(8,128)(2,1)} %collective-permute-done.10.refs_1_, ...), custom_call_target="tpu_custom_call" | custom-call | flops 339738624 | bytes 1769476 | tf_op jit(solution)/shard_map/pallas_call | solution.py:653
  508.7 8.3 %shard_map.248 = (bf16[2,4,144,1152]{3,2,1,0:T(8,128)(2,1)}, bf16[2,4,144,1152]{3,2,1,0:T(8,128)(2,1)}) custom-call(s32[8]{0:T(128)S(1)} %stack.154.order_ref, bf16[256,1152]{1,0:T(8,128)(2,1)} %get-tuple-element.486.x_ref, bf16[256,1152]{1,0:T(8,128)(2,1)} %collective-permute-done.45.x_other, bf16[256,4608]{1,0:T(8,128)(2,1)} %shard_map.245.y_ref, ...), custom_call_target="tpu_custom_call" | custom-call | flops 339738624 | bytes 1400836 | tf_op jit(solution)/shard_map/pallas_call | solution.py:653
  525.2 9.2 %shard_map.250.y_ref.refs_4_ = bf16[4,864,256]{2,1,0:T(8,128)(2,1)} custom-call(bf16[4,864,256]{2,1,0:T(8,128)(2,1)S(1)} %copy-done.4, bf16[4,288,256]{2,1,0:T(8,128)(2,1)S(1)} %shard_map.249.upstream_ref), custom_call_target="tpu_custom_call" | custom-call | flops 94371840 | bytes 516096 | tf_op jit(solution)/shard_map/pallas_call | solution.py:653
  562.6 9.8 %shard_map.253 = (bf16[2,4,144,1152]{3,2,1,0:T(8,128)(2,1)}, bf16[2,4,144,1152]{3,2,1,0:T(8,128)(2,1)}) custom-call(s32[8]{0:T(128)S(1)} %stack.154.order_ref, bf16[256,1152]{1,0:T(8,128)(2,1)S(1)} %get-tuple-element.526.x_ref.refs_0_, bf16[256,1152]{1,0:T(8,128)(2,1)} %collective-permute-done.49.refs_1_, ...), custom_call_target="tpu_custom_call" | custom-call | flops 339738624 | bytes 1548292 | tf_op jit(solution)/shard_map/pallas_call | solution.py:653
  589.4 16.1 %collective-permute-done.58 = f32[2,6,1152]{2,1,0:T(8,128)S(1)} collective-permute-done((f32[2,6,1152]{2,1,0:T(8,128)S(1)}, f32[2,6,1152]{2,1,0:T(8,128)S(1)}, u32[]{:S(2)}, u32[]{:S(2)}) %collective-permute-start.58) | collective-permute-done | bytes 55328 | tf_op jit(solution)/shard_map/ppermute | solution.py:350
  605.6 10.1 %collective-permute-done.59 = f32[2,6,1152]{2,1,0:T(8,128)S(1)} collective-permute-done((f32[2,6,1152]{2,1,0:T(8,128)S(1)}, f32[2,6,1152]{2,1,0:T(8,128)S(1)}, u32[]{:S(2)}, u32[]{:S(2)}) %collective-permute-start.59) | collective-permute-done | bytes 55328 | tf_op jit(solution)/shard_map/ppermute | solution.py:350
  629.6 12.1 %collective-permute-done.60 = bf16[4,144,1152]{2,1,0:T(8,128)(2,1)} collective-permute-done((bf16[4,144,1152]{2,1,0:T(8,128)(2,1)}, bf16[4,144,1152]{2,1,0:T(8,128)(2,1)}, u32[]{:S(2)}, u32[]{:S(2)}) %collective-permute-start.60) | collective-permute-done | bytes 1327136 | tf_op jit(solution)/shard_map/ppermute | solution.py:364
  682.3 12.8 %reduce-scatter.7.cloned.1.call-done = bf16[1,144,1152]{2,1,0:T(8,128)(2,1)} async-done(((bf16[4,144,1152]{2,1,0:T(8,128)(2,1)}), bf16[1,144,1152]{2,1,0:T(8,128)(2,1)}) %reduce-scatter.7.cloned.1.call-update) | async-done | bytes 331792 | tf_op jit(solution)/shard_map/reduce_scatter | solution.py:492
  (496 shorter events, 398.4 us)
Async XLA Ops:
  7.2 39.6 %all-gather.14.cloned.1.call-start = ((), (), s32[]{:S(2)}) async-start(), calls=%async_computation.18 | async-start | bytes 1658880 | tf_op jit(solution)/shard_map/all_gather | solution.py:430
  27.3 76.0 %all-gather.16.cloned.1.call-start = ((), (), s32[]{:S(2)}) async-start(), calls=%async_computation.19 | async-start | bytes 3317760 | tf_op jit(solution)/shard_map/all_gather | solution.py:456
  106.9 38.6 %all-gather.18.cloned.1.call-start = ((), (), s32[]{:S(2)}) async-start(), calls=%async_computation.20 | async-start | bytes 1658880 | tf_op jit(solution)/shard_map/all_gather | solution.py:430
  107.6 88.2 %all-gather.20.cloned.1.call-start = ((), (), s32[]{:S(2)}) async-start(), calls=%async_computation.21 | async-start | bytes 1658880 | tf_op jit(solution)/shard_map/all_gather | solution.py:430
  108.4 53.3 %collective-permute-start.10 = (bf16[4,2,144,1152]{3,2,1,0:T(8,128)(2,1)}, bf16[4,2,144,1152]{3,2,1,0:T(8,128)(2,1)}, u32[]{:S(2)}, u32[]{:S(2)}) collective-permute-start(bf16[4,2,144,1152]{3,2,1,0:T(8,128)(2,1)} %bitcast.159), channel_id=1, source_target_pairs={{0,16},{4,12},{8,24},{12,4},{16,0},{20,28},{24,8},{28,20},{1,17},{... | collective-permute-start | bytes 7962632 | tf_op jit(solution)/shard_map/ppermute | solution.py:364
  109.9 51.8 %collective-permute-start.11 = (bf16[4,2,144,1152]{3,2,1,0:T(8,128)(2,1)}, bf16[4,2,144,1152]{3,2,1,0:T(8,128)(2,1)}, u32[]{:S(2)}, u32[]{:S(2)}) collective-permute-start(bf16[4,2,144,1152]{3,2,1,0:T(8,128)(2,1)} %bitcast.160), channel_id=1, source_target_pairs={{0,4},{4,0},{8,12},{12,8},{16,20},{20,16},{24,28},{28,24},{1,5},{5... | collective-permute-start | bytes 7962632 | tf_op jit(solution)/shard_map/ppermute | solution.py:364
  163.5 82.7 %all-gather.22.cloned.1.call-start = ((), (), s32[]{:S(2)}) async-start(), calls=%async_computation.22 | async-start | bytes 1658880 | tf_op jit(solution)/shard_map/all_gather | solution.py:430
  251.9 51.0 %all-gather.24.cloned.1.call-start = ((), (), s32[]{:S(2)}) async-start(), calls=%async_computation.23 | async-start | bytes 1658880 | tf_op jit(solution)/shard_map/all_gather | solution.py:430
  274.4 44.8 %collective-permute-start.22 = (bf16[2,4,144,1152]{3,2,1,0:T(8,128)(2,1)}, bf16[2,4,144,1152]{3,2,1,0:T(8,128)(2,1)}, u32[]{:S(2)}, u32[]{:S(2)}) collective-permute-start(bf16[2,4,144,1152]{3,2,1,0:T(8,128)(2,1)} %pad_maximum_fusion.3.refs_0_), channel_id=1, source_target_pairs={{0,16},{4,12},{8,24},{12,4},{16,0},{20,28},{24,8},{28,20},{1,17},{... | collective-permute-start | bytes 7962632 | tf_op jit(solution)/shard_map/ppermute | solution.py:364
  275.9 43.3 %collective-permute-start.23 = (bf16[2,4,144,1152]{3,2,1,0:T(8,128)(2,1)}, bf16[2,4,144,1152]{3,2,1,0:T(8,128)(2,1)}, u32[]{:S(2)}, u32[]{:S(2)}) collective-permute-start(bf16[2,4,144,1152]{3,2,1,0:T(8,128)(2,1)} %pad_maximum_fusion.3.refs_0_), channel_id=1, source_target_pairs={{0,4},{4,0},{8,12},{12,8},{16,20},{20,16},{24,28},{28,24},{1,5},{5... | collective-permute-start | bytes 7962632 | tf_op jit(solution)/shard_map/ppermute | solution.py:364
  278.5 40.7 %collective-permute-start.24 = (bf16[256,1152]{1,0:T(8,128)(2,1)}, bf16[256,1152]{1,0:T(8,128)(2,1)}, u32[]{:S(2)}, u32[]{:S(2)}) collective-permute-start(bf16[256,1152]{1,0:T(8,128)(2,1)} %multiply_convert_fusion.3.x_ref), channel_id=1, source_target_pairs={{0,4},{4,0},{8,12},{12,8},{16,20},{20,16},{24,28},{28,24},{1,5},{5... | collective-permute-start | bytes 1769480 | tf_op jit(solution)/shard_map/ppermute | solution.py:364
  388.4 50.0 %collective-permute-start.35 = (bf16[2,4,144,1152]{3,2,1,0:T(8,128)(2,1)}, bf16[2,4,144,1152]{3,2,1,0:T(8,128)(2,1)}, u32[]{:S(2)}, u32[]{:S(2)}) collective-permute-start(bf16[2,4,144,1152]{3,2,1,0:T(8,128)(2,1)} %get-tuple-element.432), channel_id=1, source_target_pairs={{0,16},{4,12},{8,24},{12,4},{16,0},{20,28},{24,8},{28,20},{1,17},{... | collective-permute-start | bytes 7962632 | tf_op jit(solution)/shard_map/ppermute | solution.py:364
  425.7 228.6 %reduce-scatter.17.cloned.1.call-start = ((), (), s32[]{:S(2)}) async-start(), calls=%async_computation.17 | async-start | bytes 1658880 | tf_op jit(solution)/shard_map/reduce_scatter | solution.py:492
  437.8 46.5 %collective-permute-start.41 = (bf16[2,4,144,1152]{3,2,1,0:T(8,128)(2,1)}, bf16[2,4,144,1152]{3,2,1,0:T(8,128)(2,1)}, u32[]{:S(2)}, u32[]{:S(2)}) collective-permute-start(bf16[2,4,144,1152]{3,2,1,0:T(8,128)(2,1)} %get-tuple-element.461), channel_id=1, source_target_pairs={{0,16},{4,12},{8,24},{12,4},{16,0},{20,28},{24,8},{28,20},{1,17},{... | collective-permute-start | bytes 7962632 | tf_op jit(solution)/shard_map/ppermute | solution.py:364
  449.3 214.4 %reduce-scatter.15.cloned.1.call-start = ((), (), s32[]{:S(2)}) async-start(), calls=%async_computation.16 | async-start | bytes 1658880 | tf_op jit(solution)/shard_map/reduce_scatter | solution.py:492
  484.3 50.1 %collective-permute-start.48 = (bf16[2,4,144,1152]{3,2,1,0:T(8,128)(2,1)}, bf16[2,4,144,1152]{3,2,1,0:T(8,128)(2,1)}, u32[]{:S(2)}, u32[]{:S(2)}) collective-permute-start(bf16[2,4,144,1152]{3,2,1,0:T(8,128)(2,1)} %get-tuple-element.500), channel_id=1, source_target_pairs={{0,16},{4,12},{8,24},{12,4},{16,0},{20,28},{24,8},{28,20},{1,17},{... | collective-permute-start | bytes 7962632 | tf_op jit(solution)/shard_map/ppermute | solution.py:364
  489.2 45.2 %collective-permute-start.49 = (bf16[256,1152]{1,0:T(8,128)(2,1)S(1)}, bf16[256,1152]{1,0:T(8,128)(2,1)}, u32[]{:S(2)}, u32[]{:S(2)}) collective-permute-start(bf16[256,1152]{1,0:T(8,128)(2,1)S(1)} %get-tuple-element.526.x_ref.refs_0_), channel_id=1, source_target_pairs={{0,4},{4,0},{8,12},{12,8},{16,20},{20,16},{24,28},{28,24},{1,5},{5... | collective-permute-start | bytes 1769480 | tf_op jit(solution)/shard_map/ppermute | solution.py:364
  493.1 41.3 %collective-permute-start.47 = (bf16[4,144,1152]{2,1,0:T(8,128)(2,1)}, bf16[4,144,1152]{2,1,0:T(8,128)(2,1)}, u32[]{:S(2)}, u32[]{:S(2)}) collective-permute-start(bf16[4,144,1152]{2,1,0:T(8,128)(2,1)} %fusion.12), channel_id=1, source_target_pairs={{0,8},{4,20},{8,0},{12,28},{16,24},{20,4},{24,16},{28,12},{1,9},{5... | collective-permute-start | bytes 3981320 | tf_op jit(solution)/shard_map/ppermute | solution.py:364
  494.7 176.3 %reduce-scatter.13.cloned.1.call-start = ((), (), s32[]{:S(2)}) async-start(), calls=%async_computation.15 | async-start | bytes 1658880 | tf_op jit(solution)/shard_map/reduce_scatter | solution.py:492
  523.6 54.9 %collective-permute-start.50 = (bf16[2,4,144,1152]{3,2,1,0:T(8,128)(2,1)}, bf16[2,4,144,1152]{3,2,1,0:T(8,128)(2,1)}, u32[]{:S(2)}, u32[]{:S(2)}) collective-permute-start(bf16[2,4,144,1152]{3,2,1,0:T(8,128)(2,1)} %get-tuple-element.521), channel_id=1, source_target_pairs={{0,16},{4,12},{8,24},{12,4},{16,0},{20,28},{24,8},{28,20},{1,17},{... | collective-permute-start | bytes 7962632 | tf_op jit(solution)/shard_map/ppermute | solution.py:364
  541.1 37.5 %collective-permute-start.55 = (bf16[4,144,1152]{2,1,0:T(8,128)(2,1)}, bf16[4,144,1152]{2,1,0:T(8,128)(2,1)}, u32[]{:S(2)}, u32[]{:S(2)}) collective-permute-start(bf16[4,144,1152]{2,1,0:T(8,128)(2,1)} %fusion.13), channel_id=1, source_target_pairs={{0,8},{4,20},{8,0},{12,28},{16,24},{20,4},{24,16},{28,12},{1,9},{5... | collective-permute-start | bytes 3981320 | tf_op jit(solution)/shard_map/ppermute | solution.py:364
  572.4 46.4 %collective-permute-start.57 = (bf16[2,4,144,1152]{3,2,1,0:T(8,128)(2,1)}, bf16[2,4,144,1152]{3,2,1,0:T(8,128)(2,1)S(1)}, u32[]{:S(2)}, u32[]{:S(2)}) collective-permute-start(bf16[2,4,144,1152]{3,2,1,0:T(8,128)(2,1)} %get-tuple-element.542), channel_id=1, source_target_pairs={{0,16},{4,12},{8,24},{12,4},{16,0},{20,28},{24,8},{28,20},{1,17},{... | collective-permute-start | bytes 7962632 | tf_op jit(solution)/shard_map/ppermute | solution.py:364
  578.5 98.4 %reduce-scatter.11.cloned.1.call-start = ((), (), s32[]{:S(2)}) async-start(), calls=%async_computation.14 | async-start | bytes 1658880 | tf_op jit(solution)/shard_map/reduce_scatter | solution.py:492
  586.4 94.0 %reduce-scatter.9.cloned.1.call-start = ((), (), s32[]{:S(2)}) async-start(), calls=%async_computation.13 | async-start | bytes 1658880 | tf_op jit(solution)/shard_map/reduce_scatter | solution.py:492
  (135 other events, 1475.5 us)
Sparse Core Ops, SparseCore 0:
  11.1 35.6 all-gather.13
  48.9 54.3 all-gather.15
  109.8 35.5 all-gather.17
  163.7 32.1 all-gather.19
  214.2 31.9 all-gather.21
  270.6 32.2 all-gather.23
  449.4 31.0 reduce-scatter.16
  494.8 31.6 reduce-scatter.14
  541.7 31.8 reduce-scatter.12
  586.5 33.9 reduce-scatter.10
  628.6 31.6 reduce-scatter.8
  663.4 31.5 reduce-scatter.6
